TPU v7x, 256 devices: a whole 4x4x8 slice. The times are simulated.
256 devices in a mesh: blk: 8 (over x_hi, y), group: 32 (over z, x_lo, core).
Axes of the slice: x: 4 (x_hi: 2, x_lo: 2; x = x_hi * 2 + x_lo), y: 4, z: 8, core: 2. Of those that a mesh axis runs over, the one named last changes fastest.
Arguments:
- walk_rows: bfloat16 [4096, 131072], P('blk', 'group'), may hold values from -6 to 6
- col_values: bfloat16 [49152, 4096], P('group', 'blk'), may hold values from -0.02734375 to 0.02734375
- col_index: int32 [96, 8], P('group'), may hold values from 0 to 7
- col_count: int32 [32, 8], P('group'), may hold values from 1 to 3, as said below
Outputs:
- inflated: float32 [4096, 4096], P(('blk', 'group'))
Inputs may be any that keep to these rules, and one draw needn't show every extreme that they name: `col_count`: each list holds 1 to 3 valid slots; some list holds 3; contents of the other slots are arbitrary.
All inputs are finite; a program needn't handle non-finite values.
Results may differ from a plain program's by a relative error of at most 0.0003.
Values may be sent and summed in bfloat16 or wider, within the bound.
No kernel may reach another device: no remote copies, remote signals or barrier semaphores. Data moves between devices by JAX's collectives and lax.ppermute only.
A program may use at most 64 MiB of HBM per device.

v0:
```python
import itertools

import jax
import jax.numpy as jnp
import numpy as np
from jax import lax
from jax.experimental import pallas as pl
from jax.experimental.pallas import tpu as pltpu
from jax.sharding import Mesh
from jax.sharding import PartitionSpec as P


AXES = ("xh", "y", "z", "xl", "core")
SIZES = (2, 4, 8, 2, 2)
SLOTS = 3
WIDTH = 512
HALF = 256
F32 = jnp.float32
WIRE = jnp.float16
TOP = 60000.0
SCALE = 64.0

BATCHES = (
    ((0, 0, (0, 1)),),
    ((0, 3, (0, 1)), (0, 1, (0, 1)), (1, 0, (0, 1))),
    ((0, 2, (0, 1)), (1, 3, (0,)), (1, 1, (0,)), (1, 2, (0,))),
    ((1, 3, (1,)), (1, 1, (1,)), (1, 2, (1,))),
)
PANELS = tuple(itertools.chain(*BATCHES))
CORE = len(PANELS)


def moves(dxh=0, dy=0, dz=0, dxl=0, dc=0):
    pairs = []
    for at in itertools.product(*(range(n) for n in SIZES)):
        to = [(a + d) % n for a, d, n in zip(at, (dxh, dy, dz, dxl, dc), SIZES)]
        pairs.append((int(np.ravel_multi_index(at, SIZES)), int(np.ravel_multi_index(to, SIZES))))
    return pairs


def send(x, **by):
    return lax.ppermute(x, AXES, moves(**by))


def coordinates():
    dx = np.array([p[0] for p in PANELS] + [0], np.int32)
    dy = np.array([p[1] for p in PANELS] + [0], np.int32)
    is_core = (np.arange(len(dx)) == CORE).astype(np.int32)
    xh, y, core = (lax.axis_index(name).astype(jnp.int32) for name in ("xh", "y", "core"))
    return ((xh ^ dx) * 4 + ((y + dy) & 3)) * (1 - is_core) + core * is_core


def product(batch, scalars, walk, values):
    panels = BATCHES[batch]
    first = sum(len(b) for b in BATCHES[:batch])
    rows = walk.shape[0]
    arrays = []
    pieces = []
    for given in values:
        for array, column, width in given:
            known = [i for i, a in enumerate(arrays) if a is array]
            if not known:
                arrays.append(array)
            pieces.append((known[0] if known else len(arrays) - 1, column, width))
    per_panel = [len(given) for given in values]
    starts = np.cumsum([0] + per_panel)
    halves = sum(p[2] for p in pieces) // HALF
    widest = max(p[2] for p in pieces)
    n = len(panels)

    def body(meta, index, count, w_hbm, *refs):
        v_hbm = refs[: len(arrays)]
        keep_ref, send_ref, w_buf, v_buf, acc_ref, w_sem, v_sem = refs[len(arrays) :]

        def w_copy(k, s):
            block = index[s * 8 + meta[first + k]]
            source = w_hbm.at[:, pl.ds(pl.multiple_of(block * WIDTH, WIDTH), WIDTH)]
            return pltpu.make_async_copy(source, w_buf.at[k * SLOTS + s], w_sem.at[k * SLOTS + s])

        def v_copy(p, s):
            array, column, width = pieces[p]
            source = v_hbm[array].at[pl.ds(s * WIDTH, WIDTH), pl.ds(column, width)]
            return pltpu.make_async_copy(source, v_buf.at[p * SLOTS + s, :, pl.ds(0, width)], v_sem.at[p * SLOTS + s])

        def each(k, s, act):
            if s == 0:
                act()
            else:
                pl.when(s < count[meta[first + k]])(act)

        for k in range(n):
            for s in range(SLOTS):

                def begin(k=k, s=s):
                    w_copy(k, s).start()
                    for p in range(starts[k], starts[k + 1]):
                        v_copy(p, s).start()

                each(k, s, begin)

        core = meta[CORE]
        half = 0
        for k in range(n):
            for p in range(starts[k], starts[k + 1]):
                width = pieces[p][2]
                for s in range(SLOTS):

                    def add(k=k, s=s, p=p, width=width):
                        if p == starts[k]:
                            w_copy(k, s).wait()
                        v_copy(p, s).wait()
                        part = jnp.dot(
                            w_buf[k * SLOTS + s], v_buf[p * SLOTS + s, :, :width], preferred_element_type=F32
                        ).reshape(rows // 64, 2, 2, 16, width)
                        if s == 0:
                            acc_ref[..., :width] = part
                        else:
                            acc_ref[..., :width] += part

                    each(k, s, add)
                for column in range(0, width, HALF):
                    keep_ref[:, half] = acc_ref[:, :, core, :, column : column + HALF]
                    send_ref[:, half] = acc_ref[:, :, 1 - core, :, column : column + HALF]
                    half += 1

    out = jax.ShapeDtypeStruct((rows // 64, halves, 2, 16, HALF), F32)
    blank = pl.BlockSpec(memory_space=pl.ANY)
    whole = pl.BlockSpec(memory_space=pltpu.VMEM)
    return pl.pallas_call(
        body,
        out_shape=(out, out),
        grid_spec=pltpu.PrefetchScalarGridSpec(
            num_scalar_prefetch=3,
            in_specs=[blank] * (1 + len(arrays)),
            out_specs=(whole, whole),
            scratch_shapes=[
                pltpu.VMEM((n * SLOTS, rows, WIDTH), walk.dtype),
                pltpu.VMEM((len(pieces) * SLOTS, WIDTH, widest), walk.dtype),
                pltpu.VMEM((rows // 64, 2, 2, 16, widest), F32),
                pltpu.SemaphoreType.DMA((n * SLOTS,)),
                pltpu.SemaphoreType.DMA((len(pieces) * SLOTS,)),
            ],
        ),
    )(*scalars, walk, *arrays)


def squares(meta, keeps, gots):
    spots = [(p, half) for p, panel in enumerate(PANELS) for half in panel[2]]

    def body(meta, *refs):
        m = len(keeps)
        sq_ref, sum_ref, row_ref = refs[2 * m :]
        e = 0
        for b in range(m):
            for j in range(keeps[b].shape[0]):
                x = refs[b][j] + refs[m + b][j]
                x = x * x
                p, half = spots[e]
                at = pl.multiple_of(meta[p] * WIDTH + half * HALF, HALF)
                sq_ref[:, pl.ds(at, HALF)] = x
                total = jnp.sum(x, axis=0, keepdims=True)
                row_ref[pl.ds(at // 128, 1)] = total[:, :128]
                row_ref[pl.ds(at // 128 + 1, 1)] = total[:, 128:]
                e += 1
        sum_ref[...] = jnp.broadcast_to(row_ref[...][None], sum_ref.shape)

    whole = pl.BlockSpec(memory_space=pltpu.VMEM)
    return pl.pallas_call(
        body,
        out_shape=(jax.ShapeDtypeStruct((16, 4096), F32), jax.ShapeDtypeStruct((16, 32, 128), F32)),
        grid_spec=pltpu.PrefetchScalarGridSpec(
            num_scalar_prefetch=1,
            in_specs=[whole] * (2 * len(keeps)),
            out_specs=(whole, whole),
            scratch_shapes=[pltpu.VMEM((32, 128), F32)],
        ),
        name="squares",
    )(meta, *keeps, *gots)


def scaled(squared, sums):
    def body(sq_ref, sum_ref, out_ref):
        total = sum_ref[0]
        for t in range(1, sums.shape[0]):
            total = total + sum_ref[t]
        scale = total / 4096 + 1e-06
        for r in range(32):
            at = slice(r * 128, r * 128 + 128)
            out_ref[:, at] = sq_ref[:, at] / scale[r : r + 1]

    return pl.pallas_call(body, out_shape=jax.ShapeDtypeStruct(squared.shape, F32), name="scaled")(squared, sums)


def encode(total):
    n = total.shape[1]
    top = jnp.max(jnp.abs(total), axis=(0, 2, 3))
    scale = lax.reduce_precision(jnp.maximum(top * (SCALE * 1.002), 6.2e-05), 5, 10)
    t = total * (SCALE / scale)[None, :, None, None]
    codes = (t * jnp.abs(t) * TOP).astype(WIRE).reshape(8, n * 32, HALF)
    rows = jnp.pad(scale.astype(WIRE), ((0, 16 - n), (0, 0)))
    return jnp.concatenate([codes, jnp.broadcast_to(rows[None], (8, 16, HALF))], axis=1)


def decode(coded, n):
    codes = coded[:, : n * 32].astype(F32).reshape(8, n, 2, 16, HALF)
    scale = coded[:, n * 32 : n * 33].astype(F32) * (1 / SCALE)
    size = jnp.sqrt(jnp.abs(codes) * (1 / TOP))
    return jnp.sum(jnp.where(codes < 0, -size, size) * scale[:, :, None, None], axis=0)


def pipeline(walk, values, col_index, col_count):
    meta = coordinates()
    scalars = (meta, col_index.reshape(-1), col_count.reshape(-1))
    xl = lax.axis_index("xl")

    def move(x, **by):
        return send(x, **by)

    def whole(array):
        return [(array, 0, WIDTH)]

    def pair(left, right):
        return [(left, 0, HALF), (right, 0, HALF)]

    def one(array):
        return [(array, 0, HALF)]

    ends = []

    def work(batch, given):
        keep, give = product(batch, scalars, walk, given)
        got = move(give, dc=1)
        arrived = lax.all_to_all(encode(keep + got), "z", 0, 0, tiled=True)
        total = decode(arrived, keep.shape[1])
        mine = lax.dynamic_index_in_dim(total, xl, 1, keepdims=False)
        other = lax.dynamic_index_in_dim(total, 1 - xl, 1, keepdims=False)
        ends.append((mine, move(other, dxl=1)))

    up = move(values, dy=1)
    down = move(values, dy=3)
    over = move(values, dxh=1)
    far = [move(up[:, :HALF], dy=1), move(down[:, HALF:], dy=3)]
    over_half = (over[:, :HALF], over[:, HALF:])
    over_up = [move(over_half[t], dy=1) for t in range(2)]
    over_down = [move(over_half[t], dy=3) for t in range(2)]
    over_far = [move(far[t], dxh=1) for t in range(2)]

    work(0, [whole(values)])
    work(1, [whole(up), whole(down), whole(over)])
    work(2, [pair(*far), one(over_up[0]), one(over_down[0]), one(over_far[0])])
    work(3, [one(over_up[1]), one(over_down[1]), one(over_far[1])])

    squared, sums = squares(meta, [e[0] for e in ends], [e[1] for e in ends])
    sums = jnp.sum(lax.all_to_all(sums, ("z", "core"), 0, 0), axis=0)
    sums = lax.all_to_all(jnp.broadcast_to(sums[None], (16, 32, 128)), ("xh", "y", "xl"), 0, 0)
    return scaled(squared, sums)


def solution(mesh):
    fine = Mesh(mesh.devices.reshape(SIZES), AXES)
    blk, group = ("xh", "y"), ("z", "xl", "core")
    return jax.shard_map(
        pipeline,
        mesh=fine,
        in_specs=(P(blk, group), P(group, blk), P(group, None), P(group, None)),
        out_specs=P((*blk, *group), None),
        check_vma=False,
    )
```

profile of v0, /device:TPU:1, one launch (start us, length us, event | category | flops | bytes accessed | tf_op | source)
XLA Modules:
  0.0 229.9 jit_solution(1846663875464294320)
XLA Ops:
  0.0 3.6 %collective-permute-start.2 = (bf16[1536,512]{1,0:T(8,128)(2,1)}, bf16[1536,512]{1,0:T(8,128)(2,1)}, u32[]{:S(2)}, u32[]{:S(2)}) collective-permute-start(bf16[1536,512]{1,0:T(8,128)(2,1)} %refs_0_.1), channel_id=1, source_target_pairs={{0,96},{1,97},{2,98},{3,99},{4,100},{5,101},{6,102},{7,103},{8,104... | collective-permute-start | bytes 4718600 | tf_op jit(solution)/shard_map/ppermute | solution.py:42
  3.7 2.7 %collective-permute-start.3 = (bf16[1536,512]{1,0:T(8,128)(2,1)}, bf16[1536,512]{1,0:T(8,128)(2,1)S(1)}, u32[]{:S(2)}, u32[]{:S(2)}) collective-permute-start(bf16[1536,512]{1,0:T(8,128)(2,1)} %refs_0_.1), channel_id=1, source_target_pairs={{0,128},{1,129},{2,130},{3,131},{4,132},{5,133},{6,134},{7,135},{8... | collective-permute-start | bytes 4718600 | tf_op jit(solution)/shard_map/ppermute | solution.py:42
  6.4 30.6 %collective-permute-done.2.refs_1_ = bf16[1536,512]{1,0:T(8,128)(2,1)} collective-permute-done((bf16[1536,512]{1,0:T(8,128)(2,1)}, bf16[1536,512]{1,0:T(8,128)(2,1)}, u32[]{:S(2)}, u32[]{:S(2)}) %collective-permute-start.2) | collective-permute-done | bytes 1572896 | tf_op jit(solution)/shard_map/ppermute | solution.py:42
  37.1 2.1 slice.53
  39.1 3.4 %collective-permute-start.6 = (bf16[1536,256]{1,0:T(8,128)(2,1)}, bf16[1536,256]{1,0:T(8,128)(2,1)}, u32[]{:S(2)}, u32[]{:S(2)}) collective-permute-start(bf16[1536,256]{1,0:T(8,128)(2,1)} %slice.53), channel_id=1, source_target_pairs={{0,96},{1,97},{2,98},{3,99},{4,100},{5,101},{6,102},{7,103},{8,104... | collective-permute-start | bytes 2359304 | tf_op jit(solution)/shard_map/ppermute | solution.py:42
  45.4 7.0 %shard_map.83 = (f32[8,6,2,16,256]{4,3,2,1,0:T(8,128)}, f32[8,6,2,16,256]{4,3,2,1,0:T(8,128)}) custom-call(s32[12]{0:T(128)} %multiply_add_fusion.meta, s32[24]{0:T(128)} %reshape.63.index, s32[8]{0:T(128)} %bitcast.41, bf16[512,4096]{1,0:T(8,128)(2,1)} %w_hbm.7, bf16[1536,512]{1,0:T(8,128)(2,1)} %copy-done.2, ...), custom_call_target="tpu_custom_call" | custom-call | tf_op jit(solution)/shard_map/pallas_call | solution.py:129
  52.5 3.6 %shard_map.82 = (f32[8,2,2,16,256]{4,3,2,1,0:T(8,128)}, f32[8,2,2,16,256]{4,3,2,1,0:T(8,128)}) custom-call(s32[12]{0:T(128)} %multiply_add_fusion.meta, s32[24]{0:T(128)} %reshape.63.index, s32[8]{0:T(128)} %bitcast.42, bf16[512,4096]{1,0:T(8,128)(2,1)} %w_hbm.7, bf16[1536,512]{1,0:T(8,128)(2,1)} %refs_0_.1), custom_call_target="tpu_custom_call" | custom-call | tf_op jit(solution)/shard_map/pallas_call | solution.py:129
  56.1 1.3 collective-permute-start
  57.5 1.3 fusion.31
  58.8 2.7 %collective-permute-start.12 = (bf16[1536,256]{1,0:T(8,128)(2,1)}, bf16[1536,256]{1,0:T(8,128)(2,1)}, u32[]{:S(2)}, u32[]{:S(2)}) collective-permute-start(bf16[1536,256]{1,0:T(8,128)(2,1)} %get-tuple-element.33), channel_id=1, source_target_pairs={{0,96},{1,97},{2,98},{3,99},{4,100},{5,101},{6,102},{7,103},{8,104... | collective-permute-start | bytes 2359304 | tf_op jit(solution)/shard_map/ppermute | solution.py:42
  61.6 4.2 %collective-permute-start.13 = (bf16[1536,256]{1,0:T(8,128)(2,1)}, bf16[1536,256]{1,0:T(8,128)(2,1)}, u32[]{:S(2)}, u32[]{:S(2)}) collective-permute-start(bf16[1536,256]{1,0:T(8,128)(2,1)} %collective-permute-done.6.refs_1_), channel_id=1, source_target_pairs={{0,128},{1,129},{2,130},{3,131},{4,132},{5,133},{6,134},{7,135},{8... | collective-permute-start | bytes 2359304 | tf_op jit(solution)/shard_map/ppermute | solution.py:42
  66.8 7.0 %all-to-all-start = ((f16[8,80,256]{2,1,0:T(8,128)(2,1)}), f16[8,80,256]{2,1,0:T(8,128)(2,1)S(1)}, u32[]{:S(2)}, u32[]{:S(2)}) async-start(f16[8,80,256]{2,1,0:T(8,128)(2,1)} %pad_maximum_fusion.3), calls=%async_computation | async-start | bytes 655360 | tf_op jit(solution)/shard_map/all_to_all | solution.py:233
  73.8 22.3 %collective-permute-done.5.refs_0_ = bf16[1536,256]{1,0:T(8,128)(2,1)S(1)} collective-permute-done((bf16[1536,256]{1,0:T(8,128)(2,1)S(1)}, bf16[1536,256]{1,0:T(8,128)(2,1)S(1)}, u32[]{:S(2)}, u32[]{:S(2)}) %collective-permute-start.5) | collective-permute-done | bytes 786464 | tf_op jit(solution)/shard_map/ppermute | solution.py:42
  97.0 2.7 %collective-permute-start.8 = (bf16[1536,256]{1,0:T(8,128)(2,1)}, bf16[1536,256]{1,0:T(8,128)(2,1)}, u32[]{:S(2)}, u32[]{:S(2)}) collective-permute-start(bf16[1536,256]{1,0:T(8,128)(2,1)} %get-tuple-element.34), channel_id=1, source_target_pairs={{0,96},{1,97},{2,98},{3,99},{4,100},{5,101},{6,102},{7,103},{8,104... | collective-permute-start | bytes 2359304 | tf_op jit(solution)/shard_map/ppermute | solution.py:42
  99.7 3.6 %collective-permute-start.9 = (bf16[1536,256]{1,0:T(8,128)(2,1)}, bf16[1536,256]{1,0:T(8,128)(2,1)}, u32[]{:S(2)}, u32[]{:S(2)}) collective-permute-start(bf16[1536,256]{1,0:T(8,128)(2,1)} %copy-done.8), channel_id=1, source_target_pairs={{0,128},{1,129},{2,130},{3,131},{4,132},{5,133},{6,134},{7,135},{8... | collective-permute-start | bytes 2359304 | tf_op jit(solution)/shard_map/ppermute | solution.py:42
  103.3 4.2 %shard_map.85 = (f32[8,3,2,16,256]{4,3,2,1,0:T(8,128)}, f32[8,3,2,16,256]{4,3,2,1,0:T(8,128)}) custom-call(s32[12]{0:T(128)} %multiply_add_fusion.meta, s32[24]{0:T(128)} %reshape.63.index, s32[8]{0:T(128)} %bitcast.43, bf16[512,4096]{1,0:T(8,128)(2,1)} %w_hbm.7, bf16[1536,256]{1,0:T(8,128)(2,1)} %collective-permute-done.11.refs_0_, ...), custom_call_target="tpu_custom_call" | custom-call | tf_op jit(solution)/shard_map/pallas_call | solution.py:129
  107.5 2.9 %collective-permute-start.14 = (f32[8,3,2,16,256]{4,3,2,1,0:T(8,128)}, f32[8,3,2,16,256]{4,3,2,1,0:T(8,128)}, u32[]{:S(2)}, u32[]{:S(2)}) collective-permute-start(f32[8,3,2,16,256]{4,3,2,1,0:T(8,128)} %get-tuple-element.22), channel_id=1, source_target_pairs={{0,1},{1,0},{2,3},{3,2},{4,5},{5,4},{6,7},{7,6},{8,9},{9,8},{10,11... | collective-permute-start | bytes 2359304 | tf_op jit(solution)/shard_map/ppermute | solution.py:42
  112.3 7.5 %all-to-all-start.1 = ((f16[8,208,256]{2,1,0:T(8,128)(2,1)}), f16[8,208,256]{2,1,0:T(8,128)(2,1)S(1)}, u32[]{:S(2)}, u32[]{:S(2)}) async-start(f16[8,208,256]{2,1,0:T(8,128)(2,1)} %pad_maximum_fusion), calls=%async_computation.1 | async-start | bytes 1703936 | tf_op jit(solution)/shard_map/all_to_all | solution.py:233
  119.9 6.9 %shard_map.84 = (f32[8,5,2,16,256]{4,3,2,1,0:T(8,128)}, f32[8,5,2,16,256]{4,3,2,1,0:T(8,128)}) custom-call(s32[12]{0:T(128)} %multiply_add_fusion.meta, s32[24]{0:T(128)} %reshape.63.index, s32[8]{0:T(128)} %bitcast.44, bf16[512,4096]{1,0:T(8,128)(2,1)} %w_hbm.7, bf16[1536,256]{1,0:T(8,128)(2,1)} %copy-done.8, ...), custom_call_target="tpu_custom_call" | custom-call | tf_op jit(solution)/shard_map/pallas_call | solution.py:129
  126.8 2.7 %collective-permute-start.10 = (f32[8,5,2,16,256]{4,3,2,1,0:T(8,128)}, f32[8,5,2,16,256]{4,3,2,1,0:T(8,128)}, u32[]{:S(2)}, u32[]{:S(2)}) collective-permute-start(f32[8,5,2,16,256]{4,3,2,1,0:T(8,128)} %get-tuple-element.20), channel_id=1, source_target_pairs={{0,1},{1,0},{2,3},{3,2},{4,5},{5,4},{6,7},{7,6},{8,9},{9,8},{10,11... | collective-permute-start | bytes 3932168 | tf_op jit(solution)/shard_map/ppermute | solution.py:42
  129.5 1.3 abs_reduce_fusion.2
  131.9 13.0 %all-to-all-done.1 = f16[8,208,256]{2,1,0:T(8,128)(2,1)S(1)} async-done(((f16[8,208,256]{2,1,0:T(8,128)(2,1)}), f16[8,208,256]{2,1,0:T(8,128)(2,1)S(1)}, u32[]{:S(2)}, u32[]{:S(2)}) %all-to-all-start.1) | async-done | bytes 852000 | tf_op jit(solution)/shard_map/all_to_all | solution.py:233
  144.9 3.5 %all-to-all-start.3 = ((f16[8,112,256]{2,1,0:T(8,128)(2,1)}), f16[8,112,256]{2,1,0:T(8,128)(2,1)S(1)}, u32[]{:S(2)}, u32[]{:S(2)}) async-start(f16[8,112,256]{2,1,0:T(8,128)(2,1)} %pad_maximum_fusion.2), calls=%async_computation.3 | async-start | bytes 917504 | tf_op jit(solution)/shard_map/all_to_all | solution.py:233
  148.4 1.6 abs_reduce_fusion.1
  151.4 13.4 %all-to-all-done.3 = f16[8,112,256]{2,1,0:T(8,128)(2,1)S(1)} async-done(((f16[8,112,256]{2,1,0:T(8,128)(2,1)}), f16[8,112,256]{2,1,0:T(8,128)(2,1)S(1)}, u32[]{:S(2)}, u32[]{:S(2)}) %all-to-all-start.3) | async-done | bytes 458784 | tf_op jit(solution)/shard_map/all_to_all | solution.py:233
  164.8 3.5 %all-to-all-start.2 = ((f16[8,176,256]{2,1,0:T(8,128)(2,1)}), f16[8,176,256]{2,1,0:T(8,128)(2,1)S(1)}, u32[]{:S(2)}, u32[]{:S(2)}) async-start(f16[8,176,256]{2,1,0:T(8,128)(2,1)} %pad_maximum_fusion.1), calls=%async_computation.2 | async-start | bytes 1441792 | tf_op jit(solution)/shard_map/all_to_all | solution.py:233
  172.7 17.8 %all-to-all-done.2 = f16[8,176,256]{2,1,0:T(8,128)(2,1)S(1)} async-done(((f16[8,176,256]{2,1,0:T(8,128)(2,1)}), f16[8,176,256]{2,1,0:T(8,128)(2,1)S(1)}, u32[]{:S(2)}, u32[]{:S(2)}) %all-to-all-start.2) | async-done | bytes 720928 | tf_op jit(solution)/shard_map/all_to_all | solution.py:233
  193.9 2.1 collective-permute-done.15.refs_4_
  196.7 2.6 %squares.1 = (f32[16,4096]{1,0:T(8,128)}, f32[16,32,128]{2,1,0:T(8,128)}) custom-call(s32[12]{0:T(128)} %multiply_add_fusion.meta, f32[2,16,256]{2,1,0:T(8,128)} %get-tuple-element.42.refs_0_, f32[6,16,256]{2,1,0:T(8,128)} %get-tuple-element.36.refs_1_, f32[5,16,256]{2,1,0:T(8,128)} %get-tuple-element.38.refs_2_, f32[3,16,256]{2,1,0:T(8,128)} %get-tuple-element.40.refs_3_, ...), custom_call_target="tpu_custom_call" | custom-call | tf_op jit(solution)/shard_map/squares/pallas_call | solution.py:168
  199.3 16.4 %all_to_all.30 = f32[16,32,128]{2,1,0:T(8,128)S(1)} all-to-all(f32[16,32,128]{2,1,0:T(8,128)} %get-tuple-element.24), channel_id=1, replica_groups=mesh['xh'=2,'y'=4,'z'=8,'xl'=2,'core'=2] {'z','core'}, dimensions={0} | all-to-all | bytes 524288 | tf_op jit(solution)/shard_map/all_to_all | solution.py:254
  215.8 12.3 %all_to_all.31.sum_ref = f32[16,32,128]{2,1,0:T(8,128)} all-to-all(f32[16,32,128]{2,1,0:T(8,128)S(1)} %broadcast_in_dim.14), channel_id=1, replica_groups=mesh['xh'=2,'y'=4,'z'=8,'xl'=2,'core'=2] {'xh','y','xl'}, dimensions={0} | all-to-all | bytes 524288 | tf_op jit(solution)/shard_map/all_to_all | solution.py:255
  228.1 1.8 scaled.1
  (105 shorter events, 17.7 us)
Async XLA Ops:
  0.0 42.6 %copy-start.16 = (s32[12]{0:T(128)S(1)}, s32[12]{0:T(128)}, u32[]{:S(2)}) copy-start(s32[12]{0:T(128)} %constant.56.clone) | copy-start | bytes 148
  0.0 42.6 %copy-start.17 = (s32[12]{0:T(128)S(1)}, s32[12]{0:T(128)}, u32[]{:S(2)}) copy-start(s32[12]{0:T(128)} %constant.55.clone) | copy-start | bytes 148
  0.0 42.6 %copy-start.18 = (s32[12]{0:T(128)S(1)}, s32[12]{0:T(128)}, u32[]{:S(2)}) copy-start(s32[12]{0:T(128)} %constant.52.clone) | copy-start | bytes 148
  0.0 42.6 %copy-start.19 = (s32[12]{0:T(128)S(1)}, s32[12]{0:T(128)}, u32[]{:S(2)}) copy-start(s32[12]{0:T(128)} %constant.51.clone) | copy-start | bytes 148
  0.0 43.1 %copy-start.15 = (s32[3,8]{1,0:T(4,128)S(1)}, s32[3,8]{1,0:T(4,128)}, u32[]{:S(2)}) copy-start(s32[3,8]{1,0:T(4,128)} %param.10) | copy-start | bytes 292
  0.0 37.0 %collective-permute-start.2 = (bf16[1536,512]{1,0:T(8,128)(2,1)}, bf16[1536,512]{1,0:T(8,128)(2,1)}, u32[]{:S(2)}, u32[]{:S(2)}) collective-permute-start(bf16[1536,512]{1,0:T(8,128)(2,1)} %refs_0_.1), channel_id=1, source_target_pairs={{0,96},{1,97},{2,98},{3,99},{4,100},{5,101},{6,102},{7,103},{8,104... | collective-permute-start | bytes 4718600 | tf_op jit(solution)/shard_map/ppermute | solution.py:42
  3.7 40.0 %collective-permute-start.1 = (bf16[1536,512]{1,0:T(8,128)(2,1)}, bf16[1536,512]{1,0:T(8,128)(2,1)S(1)}, u32[]{:S(2)}, u32[]{:S(2)}) collective-permute-start(bf16[1536,512]{1,0:T(8,128)(2,1)} %refs_0_.1), channel_id=1, source_target_pairs={{0,32},{1,33},{2,34},{3,35},{4,36},{5,37},{6,38},{7,39},{8,40},{9,... | collective-permute-start | bytes 4718600 | tf_op jit(solution)/shard_map/ppermute | solution.py:42
  3.7 40.0 %collective-permute-start.3 = (bf16[1536,512]{1,0:T(8,128)(2,1)}, bf16[1536,512]{1,0:T(8,128)(2,1)S(1)}, u32[]{:S(2)}, u32[]{:S(2)}) collective-permute-start(bf16[1536,512]{1,0:T(8,128)(2,1)} %refs_0_.1), channel_id=1, source_target_pairs={{0,128},{1,129},{2,130},{3,131},{4,132},{5,133},{6,134},{7,135},{8... | collective-permute-start | bytes 4718600 | tf_op jit(solution)/shard_map/ppermute | solution.py:42
  39.1 22.5 %collective-permute-start.6 = (bf16[1536,256]{1,0:T(8,128)(2,1)}, bf16[1536,256]{1,0:T(8,128)(2,1)}, u32[]{:S(2)}, u32[]{:S(2)}) collective-permute-start(bf16[1536,256]{1,0:T(8,128)(2,1)} %slice.53), channel_id=1, source_target_pairs={{0,96},{1,97},{2,98},{3,99},{4,100},{5,101},{6,102},{7,103},{8,104... | collective-permute-start | bytes 2359304 | tf_op jit(solution)/shard_map/ppermute | solution.py:42
  52.4 58.1 %collective-permute-start.4 = (f32[8,6,2,16,256]{4,3,2,1,0:T(8,128)}, f32[8,6,2,16,256]{4,3,2,1,0:T(8,128)S(1)}, u32[]{:S(2)}, u32[]{:S(2)}) collective-permute-start(f32[8,6,2,16,256]{4,3,2,1,0:T(8,128)} %get-tuple-element.18), channel_id=1, source_target_pairs={{0,1},{1,0},{2,3},{3,2},{4,5},{5,4},{6,7},{7,6},{8,9},{9,8},{10,11... | collective-permute-start | bytes 4718600 | tf_op jit(solution)/shard_map/ppermute | solution.py:42
  56.1 5.4 %collective-permute-start = (f32[8,2,2,16,256]{4,3,2,1,0:T(8,128)}, f32[8,2,2,16,256]{4,3,2,1,0:T(8,128)S(1)}, u32[]{:S(2)}, u32[]{:S(2)}) collective-permute-start(f32[8,2,2,16,256]{4,3,2,1,0:T(8,128)} %get-tuple-element.16), channel_id=1, source_target_pairs={{0,1},{1,0},{2,3},{3,2},{4,5},{5,4},{6,7},{7,6},{8,9},{9,8},{10,11... | collective-permute-start | bytes 1572872 | tf_op jit(solution)/shard_map/ppermute | solution.py:42
  58.8 38.3 %collective-permute-start.11 = (bf16[1536,256]{1,0:T(8,128)(2,1)}, bf16[1536,256]{1,0:T(8,128)(2,1)}, u32[]{:S(2)}, u32[]{:S(2)}) collective-permute-start(bf16[1536,256]{1,0:T(8,128)(2,1)} %get-tuple-element.33), channel_id=1, source_target_pairs={{0,32},{1,33},{2,34},{3,35},{4,36},{5,37},{6,38},{7,39},{8,40},{9,... | collective-permute-start | bytes 2359304 | tf_op jit(solution)/shard_map/ppermute | solution.py:42
  58.8 40.9 %collective-permute-start.12 = (bf16[1536,256]{1,0:T(8,128)(2,1)}, bf16[1536,256]{1,0:T(8,128)(2,1)}, u32[]{:S(2)}, u32[]{:S(2)}) collective-permute-start(bf16[1536,256]{1,0:T(8,128)(2,1)} %get-tuple-element.33), channel_id=1, source_target_pairs={{0,96},{1,97},{2,98},{3,99},{4,100},{5,101},{6,102},{7,103},{8,104... | collective-permute-start | bytes 2359304 | tf_op jit(solution)/shard_map/ppermute | solution.py:42
  61.5 34.6 %collective-permute-start.5 = (bf16[1536,256]{1,0:T(8,128)(2,1)S(1)}, bf16[1536,256]{1,0:T(8,128)(2,1)S(1)}, u32[]{:S(2)}, u32[]{:S(2)}) collective-permute-start(bf16[1536,256]{1,0:T(8,128)(2,1)S(1)} %slice.52), channel_id=1, source_target_pairs={{0,32},{1,33},{2,34},{3,35},{4,36},{5,37},{6,38},{7,39},{8,40},{9,... | collective-permute-start | bytes 2359304 | tf_op jit(solution)/shard_map/ppermute | solution.py:42
  61.6 41.7 %collective-permute-start.13 = (bf16[1536,256]{1,0:T(8,128)(2,1)}, bf16[1536,256]{1,0:T(8,128)(2,1)}, u32[]{:S(2)}, u32[]{:S(2)}) collective-permute-start(bf16[1536,256]{1,0:T(8,128)(2,1)} %collective-permute-done.6.refs_1_), channel_id=1, source_target_pairs={{0,128},{1,129},{2,130},{3,131},{4,132},{5,133},{6,134},{7,135},{8... | collective-permute-start | bytes 2359304 | tf_op jit(solution)/shard_map/ppermute | solution.py:42
  66.8 45.5 %all-to-all-start = ((f16[8,80,256]{2,1,0:T(8,128)(2,1)}), f16[8,80,256]{2,1,0:T(8,128)(2,1)S(1)}, u32[]{:S(2)}, u32[]{:S(2)}) async-start(f16[8,80,256]{2,1,0:T(8,128)(2,1)} %pad_maximum_fusion.3), calls=%async_computation | async-start | bytes 655360 | tf_op jit(solution)/shard_map/all_to_all | solution.py:233
  97.0 13.4 %copy-start.4 = (f32[8,6,2,16,256]{4,3,2,1,0:T(8,128)S(1)}, f32[8,6,2,16,256]{4,3,2,1,0:T(8,128)}, u32[]{:S(2)}) copy-start(f32[8,6,2,16,256]{4,3,2,1,0:T(8,128)} %get-tuple-element.17) | copy-start | bytes 4718596
  97.0 22.8 %collective-permute-start.7 = (bf16[1536,256]{1,0:T(8,128)(2,1)}, bf16[1536,256]{1,0:T(8,128)(2,1)}, u32[]{:S(2)}, u32[]{:S(2)}) collective-permute-start(bf16[1536,256]{1,0:T(8,128)(2,1)} %get-tuple-element.34), channel_id=1, source_target_pairs={{0,32},{1,33},{2,34},{3,35},{4,36},{5,37},{6,38},{7,39},{8,40},{9,... | collective-permute-start | bytes 2359304 | tf_op jit(solution)/shard_map/ppermute | solution.py:42
  97.0 22.8 %collective-permute-start.8 = (bf16[1536,256]{1,0:T(8,128)(2,1)}, bf16[1536,256]{1,0:T(8,128)(2,1)}, u32[]{:S(2)}, u32[]{:S(2)}) collective-permute-start(bf16[1536,256]{1,0:T(8,128)(2,1)} %get-tuple-element.34), channel_id=1, source_target_pairs={{0,96},{1,97},{2,98},{3,99},{4,100},{5,101},{6,102},{7,103},{8,104... | collective-permute-start | bytes 2359304 | tf_op jit(solution)/shard_map/ppermute | solution.py:42
  99.7 20.1 %collective-permute-start.9 = (bf16[1536,256]{1,0:T(8,128)(2,1)}, bf16[1536,256]{1,0:T(8,128)(2,1)}, u32[]{:S(2)}, u32[]{:S(2)}) collective-permute-start(bf16[1536,256]{1,0:T(8,128)(2,1)} %copy-done.8), channel_id=1, source_target_pairs={{0,128},{1,129},{2,130},{3,131},{4,132},{5,133},{6,134},{7,135},{8... | collective-permute-start | bytes 2359304 | tf_op jit(solution)/shard_map/ppermute | solution.py:42
  107.5 22.0 %collective-permute-start.14 = (f32[8,3,2,16,256]{4,3,2,1,0:T(8,128)}, f32[8,3,2,16,256]{4,3,2,1,0:T(8,128)}, u32[]{:S(2)}, u32[]{:S(2)}) collective-permute-start(f32[8,3,2,16,256]{4,3,2,1,0:T(8,128)} %get-tuple-element.22), channel_id=1, source_target_pairs={{0,1},{1,0},{2,3},{3,2},{4,5},{5,4},{6,7},{7,6},{8,9},{9,8},{10,11... | collective-permute-start | bytes 2359304 | tf_op jit(solution)/shard_map/ppermute | solution.py:42
  112.3 14.5 %copy-start.6 = (f16[8,80,256]{2,1,0:T(8,128)(2,1)}, f16[8,80,256]{2,1,0:T(8,128)(2,1)S(1)}, u32[]{:S(2)}) copy-start(f16[8,80,256]{2,1,0:T(8,128)(2,1)S(1)} %all-to-all-done) | copy-start | bytes 983044
  112.3 32.6 %all-to-all-start.1 = ((f16[8,208,256]{2,1,0:T(8,128)(2,1)}), f16[8,208,256]{2,1,0:T(8,128)(2,1)S(1)}, u32[]{:S(2)}, u32[]{:S(2)}) async-start(f16[8,208,256]{2,1,0:T(8,128)(2,1)} %pad_maximum_fusion), calls=%async_computation.1 | async-start | bytes 1703936 | tf_op jit(solution)/shard_map/all_to_all | solution.py:233
  126.8 21.6 %collective-permute-start.10 = (f32[8,5,2,16,256]{4,3,2,1,0:T(8,128)}, f32[8,5,2,16,256]{4,3,2,1,0:T(8,128)}, u32[]{:S(2)}, u32[]{:S(2)}) collective-permute-start(f32[8,5,2,16,256]{4,3,2,1,0:T(8,128)} %get-tuple-element.20), channel_id=1, source_target_pairs={{0,1},{1,0},{2,3},{3,2},{4,5},{5,4},{6,7},{7,6},{8,9},{9,8},{10,11... | collective-permute-start | bytes 3932168 | tf_op jit(solution)/shard_map/ppermute | solution.py:42
  130.8 17.6 %copy-start.5 = (f32[8,5,2,16,256]{4,3,2,1,0:T(8,128)S(1)}, f32[8,5,2,16,256]{4,3,2,1,0:T(8,128)}, u32[]{:S(2)}) copy-start(f32[8,5,2,16,256]{4,3,2,1,0:T(8,128)} %get-tuple-element.19) | copy-start | bytes 3932164
  144.9 19.9 %all-to-all-start.3 = ((f16[8,112,256]{2,1,0:T(8,128)(2,1)}), f16[8,112,256]{2,1,0:T(8,128)(2,1)S(1)}, u32[]{:S(2)}, u32[]{:S(2)}) async-start(f16[8,112,256]{2,1,0:T(8,128)(2,1)} %pad_maximum_fusion.2), calls=%async_computation.3 | async-start | bytes 917504 | tf_op jit(solution)/shard_map/all_to_all | solution.py:233
  150.3 18.1 %copy-start.7 = (f16[8,80,256]{2,1,0:T(8,128)(2,1)S(1)}, f16[8,80,256]{2,1,0:T(8,128)(2,1)}, u32[]{:S(2)}) copy-start(f16[8,80,256]{2,1,0:T(8,128)(2,1)} %copy-done.6) | copy-start | bytes 983044
  164.8 25.6 %all-to-all-start.2 = ((f16[8,176,256]{2,1,0:T(8,128)(2,1)}), f16[8,176,256]{2,1,0:T(8,128)(2,1)S(1)}, u32[]{:S(2)}, u32[]{:S(2)}) async-start(f16[8,176,256]{2,1,0:T(8,128)(2,1)} %pad_maximum_fusion.1), calls=%async_computation.2 | async-start | bytes 1441792 | tf_op jit(solution)/shard_map/all_to_all | solution.py:233
  170.2 25.8 %collective-permute-start.16 = (f32[6,16,256]{2,1,0:T(8,128)S(1)}, f32[6,16,256]{2,1,0:T(8,128)S(1)}, u32[]{:S(2)}, u32[]{:S(2)}) collective-permute-start(f32[6,16,256]{2,1,0:T(8,128)S(1)} %get-tuple-element.35), channel_id=1, source_target_pairs={{0,2},{1,3},{2,0},{3,1},{4,6},{5,7},{6,4},{7,5},{8,10},{9,11},{10,... | collective-permute-start | bytes 294920 | tf_op jit(solution)/shard_map/ppermute | solution.py:42
  171.4 24.6 %collective-permute-start.18 = (f32[3,16,256]{2,1,0:T(8,128)S(1)}, f32[3,16,256]{2,1,0:T(8,128)S(1)}, u32[]{:S(2)}, u32[]{:S(2)}) collective-permute-start(f32[3,16,256]{2,1,0:T(8,128)S(1)} %get-tuple-element.39), channel_id=1, source_target_pairs={{0,2},{1,3},{2,0},{3,1},{4,6},{5,7},{6,4},{7,5},{8,10},{9,11},{10,... | collective-permute-start | bytes 147464 | tf_op jit(solution)/shard_map/ppermute | solution.py:42
  191.8 4.2 %collective-permute-start.17 = (f32[5,16,256]{2,1,0:T(8,128)S(1)}, f32[5,16,256]{2,1,0:T(8,128)S(1)}, u32[]{:S(2)}, u32[]{:S(2)}) collective-permute-start(f32[5,16,256]{2,1,0:T(8,128)S(1)} %get-tuple-element.37), channel_id=1, source_target_pairs={{0,2},{1,3},{2,0},{3,1},{4,6},{5,7},{6,4},{7,5},{8,10},{9,11},{10,... | collective-permute-start | bytes 245768 | tf_op jit(solution)/shard_map/ppermute | solution.py:42
  192.6 3.4 %collective-permute-start.15 = (f32[2,16,256]{2,1,0:T(8,128)S(1)}, f32[2,16,256]{2,1,0:T(8,128)S(1)}, u32[]{:S(2)}, u32[]{:S(2)}) collective-permute-start(f32[2,16,256]{2,1,0:T(8,128)S(1)} %get-tuple-element.41), channel_id=1, source_target_pairs={{0,2},{1,3},{2,0},{3,1},{4,6},{5,7},{6,4},{7,5},{8,10},{9,11},{10,... | collective-permute-start | bytes 98312 | tf_op jit(solution)/shard_map/ppermute | solution.py:42
  (11 other events, 33.4 us)
where the time goes:
time: 231 us; the launch traced here: 230 us
  waiting for transfers between devices  99.4 us (43%)
  starting transfers between devices  54.5 us (24%)
  blocking collectives  28.7 us (12%)
  Pallas kernels  26.1 us (11%)
  other arithmetic  10.8 us (5%)
  local copies, waits for them, and re-layouts  9.97 us (4%)
    ppermute x19, waiting for transfers between devices, send(): return lax.ppermute(x, AXES, moves(**by))  55.2 us
    all_to_all x4, waiting for transfers between devices, work(): arrived = lax.all_to_all(encode(keep + got), 'z', 0, 0, tiled=True)  44.2 us
    ppermute x19, starting transfers between devices, send(): return lax.ppermute(x, AXES, moves(**by))  33 us
    pallas_call x4, Pallas kernels, product(): pl.pallas_call(body, out_shape=(out, out), grid_spec=pltpu.PrefetchScalar...  21.7 us
    all_to_all x4, starting transfers between devices, work(): arrived = lax.all_to_all(encode(keep + got), 'z', 0, 0, tiled=True)  21.5 us
    all_to_all x1, blocking collectives, pipeline(): sums = jnp.sum(lax.all_to_all(sums, ('z', 'core'), 0, 0), axis=0)  16.4 us
    all_to_all x1, blocking collectives, pipeline(): lax.all_to_all(jnp.broadcast_to(sums[None], (16, 32, 128)), ('xh', 'y', '...  12.3 us
  transfers between devices with their start and end apart: 23, of which 6 were waited for; matrix products, arithmetic and copies ran while one was open for 8% of the time, Pallas kernels for 9%

commit v1 on v0

--- a/solution.py
+++ b/solution.py
@@ -27,7 +27,7 @@
     ((1, 3, (1,)), (1, 1, (1,)), (1, 2, (1,))),
 )
 PANELS = tuple(itertools.chain(*BATCHES))
-CORE = len(PANELS)
+CORE, XLO = len(PANELS), len(PANELS) + 1
 
 
 def moves(dxh=0, dy=0, dz=0, dxl=0, dc=0):
@@ -43,14 +43,15 @@
 
 
 def coordinates():
-    dx = np.array([p[0] for p in PANELS] + [0], np.int32)
-    dy = np.array([p[1] for p in PANELS] + [0], np.int32)
-    is_core = (np.arange(len(dx)) == CORE).astype(np.int32)
-    xh, y, core = (lax.axis_index(name).astype(jnp.int32) for name in ("xh", "y", "core"))
-    return ((xh ^ dx) * 4 + ((y + dy) & 3)) * (1 - is_core) + core * is_core
-
-
-def product(batch, scalars, walk, values):
+    dx = np.array([p[0] for p in PANELS] + [0, 0], np.int32)
+    dy = np.array([p[1] for p in PANELS] + [0, 0], np.int32)
+    spot = np.arange(len(dx), dtype=np.int32)
+    xh, y, xl, core = (lax.axis_index(name).astype(jnp.int32) for name in ("xh", "y", "xl", "core"))
+    panels = ((xh ^ dx) * 4 + ((y + dy) & 3)) * (spot < CORE).astype(np.int32)
+    return panels + core * (spot == CORE) + xl * (spot == XLO)
+
+
+def product(batch, scalars, walk, values, xl_first):
     panels = BATCHES[batch]
     first = sum(len(b) for b in BATCHES[:batch])
     rows = walk.shape[0]
@@ -98,7 +99,7 @@
 
                 each(k, s, begin)
 
-        core = meta[CORE]
+        core, xl = meta[CORE], meta[XLO]
         half = 0
         for k in range(n):
             for p in range(starts[k], starts[k + 1]):
@@ -119,11 +120,14 @@
 
                     each(k, s, add)
                 for column in range(0, width, HALF):
-                    keep_ref[:, half] = acc_ref[:, :, core, :, column : column + HALF]
-                    send_ref[:, half] = acc_ref[:, :, 1 - core, :, column : column + HALF]
+                    for r, at in ((0, xl), (1, 1 - xl)):
+                        to = (r, slice(None), half) if xl_first else (slice(None), r, half)
+                        keep_ref[to] = acc_ref[:, at, core, :, column : column + HALF]
+                        send_ref[to] = acc_ref[:, at, 1 - core, :, column : column + HALF]
                     half += 1
 
-    out = jax.ShapeDtypeStruct((rows // 64, halves, 2, 16, HALF), F32)
+    lead = (2, rows // 64) if xl_first else (rows // 64, 2)
+    out = jax.ShapeDtypeStruct((*lead, halves, 16, HALF), F32)
     blank = pl.BlockSpec(memory_space=pl.ANY)
     whole = pl.BlockSpec(memory_space=pltpu.VMEM)
     return pl.pallas_call(
@@ -144,16 +148,18 @@
     )(*scalars, walk, *arrays)
 
 
-def squares(meta, keeps, gots):
+def squares(meta, ends):
     spots = [(p, half) for p, panel in enumerate(PANELS) for half in panel[2]]
+    terms = [len(end) for end in ends]
 
     def body(meta, *refs):
-        m = len(keeps)
-        sq_ref, sum_ref, row_ref = refs[2 * m :]
-        e = 0
-        for b in range(m):
-            for j in range(keeps[b].shape[0]):
-                x = refs[b][j] + refs[m + b][j]
+        sq_ref, sum_ref, row_ref = refs[sum(terms) :]
+        e = first = 0
+        for m in terms:
+            for j in range(refs[first].shape[0]):
+                x = refs[first][j]
+                for k in range(1, m):
+                    x = x + refs[first + k][j]
                 x = x * x
                 p, half = spots[e]
                 at = pl.multiple_of(meta[p] * WIDTH + half * HALF, HALF)
@@ -162,6 +168,7 @@
                 row_ref[pl.ds(at // 128, 1)] = total[:, :128]
                 row_ref[pl.ds(at // 128 + 1, 1)] = total[:, 128:]
                 e += 1
+            first += m
         sum_ref[...] = jnp.broadcast_to(row_ref[...][None], sum_ref.shape)
 
     whole = pl.BlockSpec(memory_space=pltpu.VMEM)
@@ -170,12 +177,12 @@
         out_shape=(jax.ShapeDtypeStruct((16, 4096), F32), jax.ShapeDtypeStruct((16, 32, 128), F32)),
         grid_spec=pltpu.PrefetchScalarGridSpec(
             num_scalar_prefetch=1,
-            in_specs=[whole] * (2 * len(keeps)),
+            in_specs=[whole] * sum(terms),
             out_specs=(whole, whole),
             scratch_shapes=[pltpu.VMEM((32, 128), F32)],
         ),
         name="squares",
-    )(meta, *keeps, *gots)
+    )(meta, *itertools.chain(*ends))
 
 
 def scaled(squared, sums):
@@ -192,26 +199,27 @@
 
 
 def encode(total):
-    n = total.shape[1]
-    top = jnp.max(jnp.abs(total), axis=(0, 2, 3))
+    n = total.shape[-3]
+    top = jnp.max(jnp.abs(total), axis=(*range(total.ndim - 3), total.ndim - 2))
     scale = lax.reduce_precision(jnp.maximum(top * (SCALE * 1.002), 6.2e-05), 5, 10)
-    t = total * (SCALE / scale)[None, :, None, None]
-    codes = (t * jnp.abs(t) * TOP).astype(WIRE).reshape(8, n * 32, HALF)
+    t = total * (SCALE / scale)[:, None]
+    codes = (t * jnp.abs(t) * TOP).astype(WIRE).reshape(8, -1, HALF)
     rows = jnp.pad(scale.astype(WIRE), ((0, 16 - n), (0, 0)))
     return jnp.concatenate([codes, jnp.broadcast_to(rows[None], (8, 16, HALF))], axis=1)
 
 
-def decode(coded, n):
-    codes = coded[:, : n * 32].astype(F32).reshape(8, n, 2, 16, HALF)
-    scale = coded[:, n * 32 : n * 33].astype(F32) * (1 / SCALE)
+def decode(coded, shape):
+    end = coded.shape[1] - 16
+    codes = coded[:, :end].astype(F32).reshape(8, *shape)
+    scale = coded[:, end : end + shape[-3]].astype(F32) * (1 / SCALE)
+    scale = scale.reshape(8, *([1] * (len(shape) - 3)), shape[-3], 1, HALF)
     size = jnp.sqrt(jnp.abs(codes) * (1 / TOP))
-    return jnp.sum(jnp.where(codes < 0, -size, size) * scale[:, :, None, None], axis=0)
+    return jnp.sum(jnp.where(codes < 0, -size, size) * scale, axis=0)
 
 
 def pipeline(walk, values, col_index, col_count):
     meta = coordinates()
     scalars = (meta, col_index.reshape(-1), col_count.reshape(-1))
-    xl = lax.axis_index("xl")
 
     def move(x, **by):
         return send(x, **by)
@@ -227,14 +235,18 @@
 
     ends = []
 
-    def work(batch, given):
-        keep, give = product(batch, scalars, walk, given)
+    def work(batch, given, xl_first=False):
+        keep, give = product(batch, scalars, walk, given, xl_first)
         got = move(give, dc=1)
-        arrived = lax.all_to_all(encode(keep + got), "z", 0, 0, tiled=True)
-        total = decode(arrived, keep.shape[1])
-        mine = lax.dynamic_index_in_dim(total, xl, 1, keepdims=False)
-        other = lax.dynamic_index_in_dim(total, 1 - xl, 1, keepdims=False)
-        ends.append((mine, move(other, dxl=1)))
+        n = keep.shape[2]
+        if xl_first:
+            other = move(keep[1] + got[1], dxl=1)
+            arrived = lax.all_to_all(encode(keep[0] + got[0] + other), "z", 0, 0, tiled=True)
+            ends.append((decode(arrived, (n, 16, HALF)),))
+        else:
+            arrived = lax.all_to_all(encode(keep + got), "z", 0, 0, tiled=True)
+            total = decode(arrived, (2, n, 16, HALF))
+            ends.append((total[0], move(total[1], dxl=1)))
 
     up = move(values, dy=1)
     down = move(values, dy=3)
@@ -248,9 +260,9 @@
     work(0, [whole(values)])
     work(1, [whole(up), whole(down), whole(over)])
     work(2, [pair(*far), one(over_up[0]), one(over_down[0]), one(over_far[0])])
-    work(3, [one(over_up[1]), one(over_down[1]), one(over_far[1])])
-
-    squared, sums = squares(meta, [e[0] for e in ends], [e[1] for e in ends])
+    work(3, [one(over_up[1]), one(over_down[1]), one(over_far[1])], xl_first=True)
+
+    squared, sums = squares(meta, ends)
     sums = jnp.sum(lax.all_to_all(sums, ("z", "core"), 0, 0), axis=0)
     sums = lax.all_to_all(jnp.broadcast_to(sums[None], (16, 32, 128)), ("xh", "y", "xl"), 0, 0)
     return scaled(squared, sums)

time: 231 us -> 232 us (level)
  waiting for transfers between devices: 99.4 us -> 81.3 us
  starting transfers between devices: 54.5 us -> 68.9 us
  other arithmetic: 10.8 us -> 16.4 us
    ppermute x19, waiting for transfers between devices: 55.2 us -> 36.9 us  [send(): return lax.ppermute(x, AXES, moves(**by))]
    ppermute x19, starting transfers between devices: 33 us -> 45.2 us  [send(): return lax.ppermute(x, AXES, moves(**by))]
    all_to_all x0 -> x1, waiting for transfers between devices: none -> 8.67 us  [work(): lax.all_to_all(encode(keep[0] + got[0] + other), 'z', 0, 0, tiled=True)]
    all_to_all x4 -> x3, waiting for transfers between devices: 44.2 us -> 35.7 us  [work(): arrived = lax.all_to_all(encode(keep + got), 'z', 0, 0, tiled=True)]
    all_to_all x0 -> x1, starting transfers between devices: none -> 3.41 us  [work(): lax.all_to_all(encode(keep[0] + got[0] + other), 'z', 0, 0, tiled=True)]
    squeeze x4 -> x0, local copies, waits for them, and re-layouts: 2.55 us -> none  [work(): other = lax.dynamic_index_in_dim(total, 1 - xl, 1, keepdims=False)]
    all_to_all x4 -> x3, starting transfers between devices: 21.5 us -> 20.3 us  [work(): arrived = lax.all_to_all(encode(keep + got), 'z', 0, 0, tiled=True)]
  transfers between devices with their start and end apart: 23 -> 23, of which waited for: 6 -> 7; matrix products, arithmetic and copies ran while one was open for 8% -> 10% of each run, Pallas kernels for 9% -> 9%
where the time goes in v1:
time: 232 us; the launch traced here: 231 us
  waiting for transfers between devices  81.3 us (35%)
  starting transfers between devices  68.9 us (30%)
  blocking collectives  28.9 us (12%)
  Pallas kernels  25.6 us (11%)
  other arithmetic  16.4 us (7%)
  local copies, waits for them, and re-layouts  9.32 us (4%)
    ppermute x19, starting transfers between devices, send(): return lax.ppermute(x, AXES, moves(**by))  45.2 us
    ppermute x19, waiting for transfers between devices, send(): return lax.ppermute(x, AXES, moves(**by))  36.9 us
    all_to_all x3, waiting for transfers between devices, work(): arrived = lax.all_to_all(encode(keep + got), 'z', 0, 0, tiled=True)  35.7 us
    pallas_call x4, Pallas kernels, product(): pl.pallas_call(body, out_shape=(out, out), grid_spec=pltpu.PrefetchScalar...  21.2 us
    all_to_all x3, starting transfers between devices, work(): arrived = lax.all_to_all(encode(keep + got), 'z', 0, 0, tiled=True)  20.3 us
    all_to_all x1, blocking collectives, pipeline(): sums = jnp.sum(lax.all_to_all(sums, ('z', 'core'), 0, 0), axis=0)  15.7 us
    all_to_all x1, blocking collectives, pipeline(): lax.all_to_all(jnp.broadcast_to(sums[None], (16, 32, 128)), ('xh', 'y', '...  13.2 us
    all_to_all x1, waiting for transfers between devices, work(): lax.all_to_all(encode(keep[0] + got[0] + other), 'z', 0, 0, tiled=True)  8.67 us
  transfers between devices with their start and end apart: 23, of which 7 were waited for; matrix products, arithmetic and copies ran while one was open for 10% of the time, Pallas kernels for 9%

profile of v1, /device:TPU:1, one launch (start us, length us, event | category | flops | bytes accessed | tf_op | source)
XLA Modules:
  0.0 230.7 jit_solution(13432015061315181908)
XLA Ops:
  0.0 2.1 collective-permute-start.2
  3.6 2.7 %collective-permute-start.4 = (bf16[1536,512]{1,0:T(8,128)(2,1)}, bf16[1536,512]{1,0:T(8,128)(2,1)S(1)}, u32[]{:S(2)}, u32[]{:S(2)}) collective-permute-start(bf16[1536,512]{1,0:T(8,128)(2,1)} %refs_0_.1), channel_id=1, source_target_pairs={{0,128},{1,129},{2,130},{3,131},{4,132},{5,133},{6,134},{7,135},{8... | collective-permute-start | bytes 4718600 | tf_op jit(solution)/shard_map/ppermute | solution.py:42
  8.9 3.4 %shard_map.91 = (f32[8,2,2,16,256]{4,3,2,1,0:T(8,128)}, f32[8,2,2,16,256]{4,3,2,1,0:T(8,128)}) custom-call(s32[13]{0:T(128)} %select_add_fusion.meta, s32[24]{0:T(128)} %reshape.81.index, s32[8]{0:T(128)} %bitcast.40, bf16[512,4096]{1,0:T(8,128)(2,1)} %w_hbm.7, bf16[1536,512]{1,0:T(8,128)(2,1)} %refs_0_.1), custom_call_target="tpu_custom_call" | custom-call | tf_op jit(solution)/shard_map/pallas_call | solution.py:133
  12.3 2.4 %collective-permute-start = (f32[8,2,2,16,256]{4,3,2,1,0:T(8,128)}, f32[8,2,2,16,256]{4,3,2,1,0:T(8,128)}, u32[]{:S(2)}, u32[]{:S(2)}) collective-permute-start(f32[8,2,2,16,256]{4,3,2,1,0:T(8,128)} %get-tuple-element.16), channel_id=1, source_target_pairs={{0,1},{1,0},{2,3},{3,2},{4,5},{5,4},{6,7},{7,6},{8,9},{9,8},{10,11... | collective-permute-start | bytes 1572872 | tf_op jit(solution)/shard_map/ppermute | solution.py:42
  14.7 21.2 %collective-permute-done.2.refs_0_ = bf16[1536,512]{1,0:T(8,128)(2,1)S(1)} collective-permute-done((bf16[1536,512]{1,0:T(8,128)(2,1)}, bf16[1536,512]{1,0:T(8,128)(2,1)S(1)}, u32[]{:S(2)}, u32[]{:S(2)}) %collective-permute-start.2) | collective-permute-done | bytes 1572896 | tf_op jit(solution)/shard_map/ppermute | solution.py:42
  36.9 1.6 collective-permute-start.7
  38.6 2.1 slice.103
  43.6 2.7 %collective-permute-start.10 = (bf16[1536,256]{1,0:T(8,128)(2,1)}, bf16[1536,256]{1,0:T(8,128)(2,1)S(1)}, u32[]{:S(2)}, u32[]{:S(2)}) collective-permute-start(bf16[1536,256]{1,0:T(8,128)(2,1)} %get-tuple-element.32), channel_id=1, source_target_pairs={{0,96},{1,97},{2,98},{3,99},{4,100},{5,101},{6,102},{7,103},{8,104... | collective-permute-start | bytes 2359304 | tf_op jit(solution)/shard_map/ppermute | solution.py:42
  46.3 7.0 %shard_map.92 = (f32[8,2,6,16,256]{4,3,2,1,0:T(8,128)}, f32[8,2,6,16,256]{4,3,2,1,0:T(8,128)}) custom-call(s32[13]{0:T(128)} %select_add_fusion.meta, s32[24]{0:T(128)} %reshape.81.index, s32[8]{0:T(128)} %bitcast.41, bf16[512,4096]{1,0:T(8,128)(2,1)} %w_hbm.7, bf16[1536,512]{1,0:T(8,128)(2,1)} %copy-done.1, ...), custom_call_target="tpu_custom_call" | custom-call | tf_op jit(solution)/shard_map/pallas_call | solution.py:133
  53.3 2.1 collective-permute-start.5
  56.5 1.7 collective-permute-done.8.refs_1_
  58.2 1.7 collective-permute-start.15
  59.9 12.3 %collective-permute-done.9.refs_2_ = bf16[1536,256]{1,0:T(8,128)(2,1)S(1)} collective-permute-done((bf16[1536,256]{1,0:T(8,128)(2,1)}, bf16[1536,256]{1,0:T(8,128)(2,1)S(1)}, u32[]{:S(2)}, u32[]{:S(2)}) %collective-permute-start.9) | collective-permute-done | bytes 786464 | tf_op jit(solution)/shard_map/ppermute | solution.py:42
  72.2 5.1 %collective-permute-start.11 = (bf16[1536,256]{1,0:T(8,128)(2,1)}, bf16[1536,256]{1,0:T(8,128)(2,1)S(1)}, u32[]{:S(2)}, u32[]{:S(2)}) collective-permute-start(bf16[1536,256]{1,0:T(8,128)(2,1)} %collective-permute-done.7.refs_0_), channel_id=1, source_target_pairs={{0,128},{1,129},{2,130},{3,131},{4,132},{5,133},{6,134},{7,135},{8... | collective-permute-start | bytes 2359304 | tf_op jit(solution)/shard_map/ppermute | solution.py:42
  80.7 8.2 %all-to-all-start = ((f16[8,80,256]{2,1,0:T(8,128)(2,1)}), f16[8,80,256]{2,1,0:T(8,128)(2,1)S(1)}, u32[]{:S(2)}, u32[]{:S(2)}) async-start(f16[8,80,256]{2,1,0:T(8,128)(2,1)} %pad_maximum_fusion.2), calls=%async_computation | async-start | bytes 655360 | tf_op jit(solution)/shard_map/all_to_all | solution.py:247
  88.9 1.7 collective-permute-done.11.refs_4_
  91.5 6.7 %shard_map.93 = (f32[8,2,5,16,256]{4,3,2,1,0:T(8,128)}, f32[8,2,5,16,256]{4,3,2,1,0:T(8,128)}) custom-call(s32[13]{0:T(128)} %select_add_fusion.meta, s32[24]{0:T(128)} %reshape.81.index, s32[8]{0:T(128)} %bitcast.42, bf16[512,4096]{1,0:T(8,128)(2,1)} %w_hbm.7, bf16[1536,256]{1,0:T(8,128)(2,1)} %collective-permute-done.7.refs_0_, ...), custom_call_target="tpu_custom_call" | custom-call | tf_op jit(solution)/shard_map/pallas_call | solution.py:133
  98.2 10.9 %collective-permute-start.12 = (f32[8,2,5,16,256]{4,3,2,1,0:T(8,128)}, f32[8,2,5,16,256]{4,3,2,1,0:T(8,128)}, u32[]{:S(2)}, u32[]{:S(2)}) collective-permute-start(f32[8,2,5,16,256]{4,3,2,1,0:T(8,128)} %get-tuple-element.20), channel_id=1, source_target_pairs={{0,1},{1,0},{2,3},{3,2},{4,5},{5,4},{6,7},{7,6},{8,9},{9,8},{10,11... | collective-permute-start | bytes 3932168 | tf_op jit(solution)/shard_map/ppermute | solution.py:42
  109.1 4.2 %shard_map.94 = (f32[2,8,3,16,256]{4,3,2,1,0:T(8,128)}, f32[2,8,3,16,256]{4,3,2,1,0:T(8,128)}) custom-call(s32[13]{0:T(128)} %select_add_fusion.meta, s32[24]{0:T(128)} %reshape.81.index, s32[8]{0:T(128)} %bitcast.43, bf16[512,4096]{1,0:T(8,128)(2,1)} %w_hbm.7, bf16[1536,256]{1,0:T(8,128)(2,1)} %collective-permute-done.14.refs_0_, ...), custom_call_target="tpu_custom_call" | custom-call | tf_op jit(solution)/shard_map/pallas_call | solution.py:133
  113.3 4.5 %collective-permute-start.17 = (f32[2,8,3,16,256]{4,3,2,1,0:T(8,128)}, f32[2,8,3,16,256]{4,3,2,1,0:T(8,128)S(1)}, u32[]{:S(2)}, u32[]{:S(2)}) collective-permute-start(f32[2,8,3,16,256]{4,3,2,1,0:T(8,128)} %get-tuple-element.22), channel_id=1, source_target_pairs={{0,1},{1,0},{2,3},{3,2},{4,5},{5,4},{6,7},{7,6},{8,9},{9,8},{10,11... | collective-permute-start | bytes 2359304 | tf_op jit(solution)/shard_map/ppermute | solution.py:42
  117.8 1.8 abs_reduce_fusion
  121.1 8.6 %all-to-all-start.1 = ((f16[8,208,256]{2,1,0:T(8,128)(2,1)}), f16[8,208,256]{2,1,0:T(8,128)(2,1)S(1)}, u32[]{:S(2)}, u32[]{:S(2)}) async-start(f16[8,208,256]{2,1,0:T(8,128)(2,1)} %pad_maximum_fusion), calls=%async_computation.1 | async-start | bytes 1703936 | tf_op jit(solution)/shard_map/all_to_all | solution.py:247
  131.8 2.0 abs_reduce_fusion.1
  135.2 19.5 %all-to-all-done.1 = f16[8,208,256]{2,1,0:T(8,128)(2,1)S(1)} async-done(((f16[8,208,256]{2,1,0:T(8,128)(2,1)}), f16[8,208,256]{2,1,0:T(8,128)(2,1)S(1)}, u32[]{:S(2)}, u32[]{:S(2)}) %all-to-all-start.1) | async-done | bytes 852000 | tf_op jit(solution)/shard_map/all_to_all | solution.py:247
  154.7 3.5 %all-to-all-start.2 = ((f16[8,176,256]{2,1,0:T(8,128)(2,1)}), f16[8,176,256]{2,1,0:T(8,128)(2,1)S(1)}, u32[]{:S(2)}, u32[]{:S(2)}) async-start(f16[8,176,256]{2,1,0:T(8,128)(2,1)} %pad_maximum_fusion.1), calls=%async_computation.2 | async-start | bytes 1441792 | tf_op jit(solution)/shard_map/all_to_all | solution.py:247
  164.1 16.3 %all-to-all-done.2 = f16[8,176,256]{2,1,0:T(8,128)(2,1)S(1)} async-done(((f16[8,176,256]{2,1,0:T(8,128)(2,1)}), f16[8,176,256]{2,1,0:T(8,128)(2,1)S(1)}, u32[]{:S(2)}, u32[]{:S(2)}) %all-to-all-start.2) | async-done | bytes 720928 | tf_op jit(solution)/shard_map/all_to_all | solution.py:247
  180.3 3.4 %all-to-all-start.3 = ((f16[8,64,256]{2,1,0:T(8,128)(2,1)}), f16[8,64,256]{2,1,0:T(8,128)(2,1)S(1)}, u32[]{:S(2)}, u32[]{:S(2)}) async-start(f16[8,64,256]{2,1,0:T(8,128)(2,1)} %pad_maximum_fusion.3), calls=%async_computation.3 | async-start | bytes 524288 | tf_op jit(solution)/shard_map/all_to_all | solution.py:244
  187.2 8.7 %all-to-all-done.3 = f16[8,64,256]{2,1,0:T(8,128)(2,1)S(1)} async-done(((f16[8,64,256]{2,1,0:T(8,128)(2,1)}), f16[8,64,256]{2,1,0:T(8,128)(2,1)S(1)}, u32[]{:S(2)}, u32[]{:S(2)}) %all-to-all-start.3) | async-done | bytes 262176 | tf_op jit(solution)/shard_map/all_to_all | solution.py:244
  197.4 2.6 %squares.1 = (f32[16,4096]{1,0:T(8,128)}, f32[16,32,128]{2,1,0:T(8,128)}) custom-call(s32[13]{0:T(128)} %select_add_fusion.meta, f32[2,16,256]{2,1,0:T(8,128)} %bitcast.37, f32[2,16,256]{2,1,0:T(8,128)} %collective-permute-done.1.refs_1_, f32[6,16,256]{2,1,0:T(8,128)} %bitcast.34, f32[6,16,256]{2,1,0:T(8,128)} %copy-done.8, f32[5,16,256]{2,1,0:T(8,128)} %bitcast.35, ...), custom_call_target="tpu_custom_call" | custom-call | tf_op jit(solution)/shard_map/squares/pallas_call | solution.py:175
  200.0 15.7 %all_to_all.30 = f32[16,32,128]{2,1,0:T(8,128)S(1)} all-to-all(f32[16,32,128]{2,1,0:T(8,128)} %get-tuple-element.24), channel_id=1, replica_groups=mesh['xh'=2,'y'=4,'z'=8,'xl'=2,'core'=2] {'z','core'}, dimensions={0} | all-to-all | bytes 524288 | tf_op jit(solution)/shard_map/all_to_all | solution.py:266
  215.7 13.2 %all_to_all.31.sum_ref = f32[16,32,128]{2,1,0:T(8,128)} all-to-all(f32[16,32,128]{2,1,0:T(8,128)S(1)} %broadcast_in_dim.14), channel_id=1, replica_groups=mesh['xh'=2,'y'=4,'z'=8,'xl'=2,'core'=2] {'xh','y','xl'}, dimensions={0} | all-to-all | bytes 524288 | tf_op jit(solution)/shard_map/all_to_all | solution.py:267
  228.9 1.8 scaled.1
  (85 shorter events, 29.2 us)
Async XLA Ops:
  0.0 35.9 %collective-permute-start.2 = (bf16[1536,512]{1,0:T(8,128)(2,1)}, bf16[1536,512]{1,0:T(8,128)(2,1)S(1)}, u32[]{:S(2)}, u32[]{:S(2)}) collective-permute-start(bf16[1536,512]{1,0:T(8,128)(2,1)} %refs_0_.1), channel_id=1, source_target_pairs={{0,32},{1,33},{2,34},{3,35},{4,36},{5,37},{6,38},{7,39},{8,40},{9,... | collective-permute-start | bytes 4718600 | tf_op jit(solution)/shard_map/ppermute | solution.py:42
  2.1 36.4 %collective-permute-start.3 = (bf16[1536,512]{1,0:T(8,128)(2,1)}, bf16[1536,512]{1,0:T(8,128)(2,1)}, u32[]{:S(2)}, u32[]{:S(2)}) collective-permute-start(bf16[1536,512]{1,0:T(8,128)(2,1)} %refs_0_.1), channel_id=1, source_target_pairs={{0,96},{1,97},{2,98},{3,99},{4,100},{5,101},{6,102},{7,103},{8,104... | collective-permute-start | bytes 4718600 | tf_op jit(solution)/shard_map/ppermute | solution.py:42
  3.6 38.7 %collective-permute-start.4 = (bf16[1536,512]{1,0:T(8,128)(2,1)}, bf16[1536,512]{1,0:T(8,128)(2,1)S(1)}, u32[]{:S(2)}, u32[]{:S(2)}) collective-permute-start(bf16[1536,512]{1,0:T(8,128)(2,1)} %refs_0_.1), channel_id=1, source_target_pairs={{0,128},{1,129},{2,130},{3,131},{4,132},{5,133},{6,134},{7,135},{8... | collective-permute-start | bytes 4718600 | tf_op jit(solution)/shard_map/ppermute | solution.py:42
  12.3 41.0 %collective-permute-start = (f32[8,2,2,16,256]{4,3,2,1,0:T(8,128)}, f32[8,2,2,16,256]{4,3,2,1,0:T(8,128)}, u32[]{:S(2)}, u32[]{:S(2)}) collective-permute-start(f32[8,2,2,16,256]{4,3,2,1,0:T(8,128)} %get-tuple-element.16), channel_id=1, source_target_pairs={{0,1},{1,0},{2,3},{3,2},{4,5},{5,4},{6,7},{7,6},{8,9},{9,8},{10,11... | collective-permute-start | bytes 1572872 | tf_op jit(solution)/shard_map/ppermute | solution.py:42
  35.9 4.7 %copy-start.1 = (bf16[1536,512]{1,0:T(8,128)(2,1)}, bf16[1536,512]{1,0:T(8,128)(2,1)S(1)}, u32[]{:S(2)}) copy-start(bf16[1536,512]{1,0:T(8,128)(2,1)S(1)} %collective-permute-done.2.refs_0_) | copy-start | bytes 4718596
  36.9 18.5 %collective-permute-start.7 = (bf16[1536,256]{1,0:T(8,128)(2,1)}, bf16[1536,256]{1,0:T(8,128)(2,1)}, u32[]{:S(2)}, u32[]{:S(2)}) collective-permute-start(bf16[1536,256]{1,0:T(8,128)(2,1)} %slice.102), channel_id=1, source_target_pairs={{0,32},{1,33},{2,34},{3,35},{4,36},{5,37},{6,38},{7,39},{8,40},{9,... | collective-permute-start | bytes 2359304 | tf_op jit(solution)/shard_map/ppermute | solution.py:42
  40.6 17.6 %collective-permute-start.8 = (bf16[1536,256]{1,0:T(8,128)(2,1)}, bf16[1536,256]{1,0:T(8,128)(2,1)}, u32[]{:S(2)}, u32[]{:S(2)}) collective-permute-start(bf16[1536,256]{1,0:T(8,128)(2,1)} %slice.103), channel_id=1, source_target_pairs={{0,96},{1,97},{2,98},{3,99},{4,100},{5,101},{6,102},{7,103},{8,104... | collective-permute-start | bytes 2359304 | tf_op jit(solution)/shard_map/ppermute | solution.py:42
  42.2 1.4 copy-start
  43.6 28.5 %collective-permute-start.9 = (bf16[1536,256]{1,0:T(8,128)(2,1)}, bf16[1536,256]{1,0:T(8,128)(2,1)S(1)}, u32[]{:S(2)}, u32[]{:S(2)}) collective-permute-start(bf16[1536,256]{1,0:T(8,128)(2,1)} %get-tuple-element.32), channel_id=1, source_target_pairs={{0,32},{1,33},{2,34},{3,35},{4,36},{5,37},{6,38},{7,39},{8,40},{9,... | collective-permute-start | bytes 2359304 | tf_op jit(solution)/shard_map/ppermute | solution.py:42
  43.6 33.6 %collective-permute-start.10 = (bf16[1536,256]{1,0:T(8,128)(2,1)}, bf16[1536,256]{1,0:T(8,128)(2,1)S(1)}, u32[]{:S(2)}, u32[]{:S(2)}) collective-permute-start(bf16[1536,256]{1,0:T(8,128)(2,1)} %get-tuple-element.32), channel_id=1, source_target_pairs={{0,96},{1,97},{2,98},{3,99},{4,100},{5,101},{6,102},{7,103},{8,104... | collective-permute-start | bytes 2359304 | tf_op jit(solution)/shard_map/ppermute | solution.py:42
  53.3 64.5 %collective-permute-start.5 = (f32[8,2,6,16,256]{4,3,2,1,0:T(8,128)}, f32[8,2,6,16,256]{4,3,2,1,0:T(8,128)}, u32[]{:S(2)}, u32[]{:S(2)}) collective-permute-start(f32[8,2,6,16,256]{4,3,2,1,0:T(8,128)} %get-tuple-element.18), channel_id=1, source_target_pairs={{0,1},{1,0},{2,3},{3,2},{4,5},{5,4},{6,7},{7,6},{8,9},{9,8},{10,11... | collective-permute-start | bytes 4718600 | tf_op jit(solution)/shard_map/ppermute | solution.py:42
  55.4 53.7 %collective-permute-start.14 = (bf16[1536,256]{1,0:T(8,128)(2,1)S(1)}, bf16[1536,256]{1,0:T(8,128)(2,1)}, u32[]{:S(2)}, u32[]{:S(2)}) collective-permute-start(bf16[1536,256]{1,0:T(8,128)(2,1)S(1)} %get-tuple-element.31), channel_id=1, source_target_pairs={{0,32},{1,33},{2,34},{3,35},{4,36},{5,37},{6,38},{7,39},{8,40},{9,... | collective-permute-start | bytes 2359304 | tf_op jit(solution)/shard_map/ppermute | solution.py:42
  58.2 50.9 %collective-permute-start.15 = (bf16[1536,256]{1,0:T(8,128)(2,1)S(1)}, bf16[1536,256]{1,0:T(8,128)(2,1)}, u32[]{:S(2)}, u32[]{:S(2)}) collective-permute-start(bf16[1536,256]{1,0:T(8,128)(2,1)S(1)} %get-tuple-element.31), channel_id=1, source_target_pairs={{0,96},{1,97},{2,98},{3,99},{4,100},{5,101},{6,102},{7,103},{8,104... | collective-permute-start | bytes 2359304 | tf_op jit(solution)/shard_map/ppermute | solution.py:42
  72.2 8.5 %copy-start.5 = (bf16[1536,256]{1,0:T(8,128)(2,1)}, bf16[1536,256]{1,0:T(8,128)(2,1)S(1)}, u32[]{:S(2)}) copy-start(bf16[1536,256]{1,0:T(8,128)(2,1)S(1)} %collective-permute-done.9.refs_2_) | copy-start | bytes 2359300
  72.2 18.4 %collective-permute-start.11 = (bf16[1536,256]{1,0:T(8,128)(2,1)}, bf16[1536,256]{1,0:T(8,128)(2,1)S(1)}, u32[]{:S(2)}, u32[]{:S(2)}) collective-permute-start(bf16[1536,256]{1,0:T(8,128)(2,1)} %collective-permute-done.7.refs_0_), channel_id=1, source_target_pairs={{0,128},{1,129},{2,130},{3,131},{4,132},{5,133},{6,134},{7,135},{8... | collective-permute-start | bytes 2359304 | tf_op jit(solution)/shard_map/ppermute | solution.py:42
  77.3 3.4 %copy-start.6 = (bf16[1536,256]{1,0:T(8,128)(2,1)}, bf16[1536,256]{1,0:T(8,128)(2,1)S(1)}, u32[]{:S(2)}) copy-start(bf16[1536,256]{1,0:T(8,128)(2,1)S(1)} %collective-permute-done.10.refs_3_) | copy-start | bytes 2359300
  77.3 31.9 %collective-permute-start.16 = (bf16[1536,256]{1,0:T(8,128)(2,1)}, bf16[1536,256]{1,0:T(8,128)(2,1)}, u32[]{:S(2)}, u32[]{:S(2)}) collective-permute-start(bf16[1536,256]{1,0:T(8,128)(2,1)} %collective-permute-done.8.refs_1_), channel_id=1, source_target_pairs={{0,128},{1,129},{2,130},{3,131},{4,132},{5,133},{6,134},{7,135},{8... | collective-permute-start | bytes 2359304 | tf_op jit(solution)/shard_map/ppermute | solution.py:42
  80.7 40.4 %all-to-all-start = ((f16[8,80,256]{2,1,0:T(8,128)(2,1)}), f16[8,80,256]{2,1,0:T(8,128)(2,1)S(1)}, u32[]{:S(2)}, u32[]{:S(2)}) async-start(f16[8,80,256]{2,1,0:T(8,128)(2,1)} %pad_maximum_fusion.2), calls=%async_computation | async-start | bytes 655360 | tf_op jit(solution)/shard_map/all_to_all | solution.py:247
  90.6 0.9 copy-start.7
  98.2 19.6 %copy-start.3 = (f32[8,2,6,16,256]{4,3,2,1,0:T(8,128)S(1)}, f32[8,2,6,16,256]{4,3,2,1,0:T(8,128)}, u32[]{:S(2)}) copy-start(f32[8,2,6,16,256]{4,3,2,1,0:T(8,128)} %get-tuple-element.17) | copy-start | bytes 4718596
  98.2 33.6 %collective-permute-start.12 = (f32[8,2,5,16,256]{4,3,2,1,0:T(8,128)}, f32[8,2,5,16,256]{4,3,2,1,0:T(8,128)}, u32[]{:S(2)}, u32[]{:S(2)}) collective-permute-start(f32[8,2,5,16,256]{4,3,2,1,0:T(8,128)} %get-tuple-element.20), channel_id=1, source_target_pairs={{0,1},{1,0},{2,3},{3,2},{4,5},{5,4},{6,7},{7,6},{8,9},{9,8},{10,11... | collective-permute-start | bytes 3932168 | tf_op jit(solution)/shard_map/ppermute | solution.py:42
  113.3 16.4 %collective-permute-start.17 = (f32[2,8,3,16,256]{4,3,2,1,0:T(8,128)}, f32[2,8,3,16,256]{4,3,2,1,0:T(8,128)S(1)}, u32[]{:S(2)}, u32[]{:S(2)}) collective-permute-start(f32[2,8,3,16,256]{4,3,2,1,0:T(8,128)} %get-tuple-element.22), channel_id=1, source_target_pairs={{0,1},{1,0},{2,3},{3,2},{4,5},{5,4},{6,7},{7,6},{8,9},{9,8},{10,11... | collective-permute-start | bytes 2359304 | tf_op jit(solution)/shard_map/ppermute | solution.py:42
  120.0 9.7 %copy-start.2 = (f32[2,8,3,16,256]{4,3,2,1,0:T(8,128)S(1)}, f32[2,8,3,16,256]{4,3,2,1,0:T(8,128)}, u32[]{:S(2)}) copy-start(f32[2,8,3,16,256]{4,3,2,1,0:T(8,128)} %get-tuple-element.21) | copy-start | bytes 2359300
  121.1 8.6 %copy-start.4 = (f16[8,80,256]{2,1,0:T(8,128)(2,1)}, f16[8,80,256]{2,1,0:T(8,128)(2,1)S(1)}, u32[]{:S(2)}) copy-start(f16[8,80,256]{2,1,0:T(8,128)(2,1)S(1)} %all-to-all-done) | copy-start | bytes 983044
  121.1 33.6 %all-to-all-start.1 = ((f16[8,208,256]{2,1,0:T(8,128)(2,1)}), f16[8,208,256]{2,1,0:T(8,128)(2,1)S(1)}, u32[]{:S(2)}, u32[]{:S(2)}) async-start(f16[8,208,256]{2,1,0:T(8,128)(2,1)} %pad_maximum_fusion), calls=%async_computation.1 | async-start | bytes 1703936 | tf_op jit(solution)/shard_map/all_to_all | solution.py:247
  130.5 31.6 %collective-permute-start.18 = (f32[8,3,16,256]{3,2,1,0:T(8,128)}, f32[8,3,16,256]{3,2,1,0:T(8,128)S(1)}, u32[]{:S(2)}, u32[]{:S(2)}) collective-permute-start(f32[8,3,16,256]{3,2,1,0:T(8,128)} %fusion.24), channel_id=1, source_target_pairs={{0,2},{1,3},{2,0},{3,1},{4,6},{5,7},{6,4},{7,5},{8,10},{9,11},{10,... | collective-permute-start | bytes 1179656 | tf_op jit(solution)/shard_map/ppermute | solution.py:42
  154.7 25.6 %all-to-all-start.2 = ((f16[8,176,256]{2,1,0:T(8,128)(2,1)}), f16[8,176,256]{2,1,0:T(8,128)(2,1)S(1)}, u32[]{:S(2)}, u32[]{:S(2)}) async-start(f16[8,176,256]{2,1,0:T(8,128)(2,1)} %pad_maximum_fusion.1), calls=%async_computation.2 | async-start | bytes 1441792 | tf_op jit(solution)/shard_map/all_to_all | solution.py:247
  160.8 35.9 %collective-permute-start.1 = (f32[2,16,256]{2,1,0:T(8,128)}, f32[2,16,256]{2,1,0:T(8,128)}, u32[]{:S(2)}, u32[]{:S(2)}) collective-permute-start(f32[2,16,256]{2,1,0:T(8,128)} %bitcast.4), channel_id=1, source_target_pairs={{0,2},{1,3},{2,0},{3,1},{4,6},{5,7},{6,4},{7,5},{8,10},{9,11},{10,... | collective-permute-start | bytes 98312 | tf_op jit(solution)/shard_map/ppermute | solution.py:42
  180.3 15.5 %all-to-all-start.3 = ((f16[8,64,256]{2,1,0:T(8,128)(2,1)}), f16[8,64,256]{2,1,0:T(8,128)(2,1)S(1)}, u32[]{:S(2)}, u32[]{:S(2)}) async-start(f16[8,64,256]{2,1,0:T(8,128)(2,1)} %pad_maximum_fusion.3), calls=%async_computation.3 | async-start | bytes 524288 | tf_op jit(solution)/shard_map/all_to_all | solution.py:244
  184.4 12.3 %collective-permute-start.6 = (f32[6,16,256]{2,1,0:T(8,128)S(1)}, f32[6,16,256]{2,1,0:T(8,128)S(1)}, u32[]{:S(2)}, u32[]{:S(2)}) collective-permute-start(f32[6,16,256]{2,1,0:T(8,128)S(1)} %bitcast.38), channel_id=1, source_target_pairs={{0,2},{1,3},{2,0},{3,1},{4,6},{5,7},{6,4},{7,5},{8,10},{9,11},{10,... | collective-permute-start | bytes 294920 | tf_op jit(solution)/shard_map/ppermute | solution.py:42
  187.0 9.7 %collective-permute-start.13 = (f32[5,16,256]{2,1,0:T(8,128)S(1)}, f32[5,16,256]{2,1,0:T(8,128)S(1)}, u32[]{:S(2)}, u32[]{:S(2)}) collective-permute-start(f32[5,16,256]{2,1,0:T(8,128)S(1)} %bitcast.39), channel_id=1, source_target_pairs={{0,2},{1,3},{2,0},{3,1},{4,6},{5,7},{6,4},{7,5},{8,10},{9,11},{10,... | collective-permute-start | bytes 245768 | tf_op jit(solution)/shard_map/ppermute | solution.py:42
  196.7 0.7 copy-start.9
  (1 other events, 0.6 us)

commit v2 on v0

--- a/solution.py
+++ b/solution.py
@@ -111,7 +111,7 @@
                         v_copy(p, s).wait()
                         part = jnp.dot(
                             w_buf[k * SLOTS + s], v_buf[p * SLOTS + s, :, :width], preferred_element_type=F32
-                        ).reshape(rows // 64, 2, 2, 16, width)
+                        ).reshape(rows // 32, 2, 16, width)
                         if s == 0:
                             acc_ref[..., :width] = part
                         else:
@@ -119,11 +119,11 @@
 
                     each(k, s, add)
                 for column in range(0, width, HALF):
-                    keep_ref[:, half] = acc_ref[:, :, core, :, column : column + HALF]
-                    send_ref[:, half] = acc_ref[:, :, 1 - core, :, column : column + HALF]
+                    keep_ref[:, half] = acc_ref[:, core, :, column : column + HALF]
+                    send_ref[:, half] = acc_ref[:, 1 - core, :, column : column + HALF]
                     half += 1
 
-    out = jax.ShapeDtypeStruct((rows // 64, halves, 2, 16, HALF), F32)
+    out = jax.ShapeDtypeStruct((rows // 32, halves, 16, HALF), F32)
     blank = pl.BlockSpec(memory_space=pl.ANY)
     whole = pl.BlockSpec(memory_space=pltpu.VMEM)
     return pl.pallas_call(
@@ -136,7 +136,7 @@
             scratch_shapes=[
                 pltpu.VMEM((n * SLOTS, rows, WIDTH), walk.dtype),
                 pltpu.VMEM((len(pieces) * SLOTS, WIDTH, widest), walk.dtype),
-                pltpu.VMEM((rows // 64, 2, 2, 16, widest), F32),
+                pltpu.VMEM((rows // 32, 2, 16, widest), F32),
                 pltpu.SemaphoreType.DMA((n * SLOTS,)),
                 pltpu.SemaphoreType.DMA((len(pieces) * SLOTS,)),
             ],
@@ -144,16 +144,15 @@
     )(*scalars, walk, *arrays)
 
 
-def squares(meta, keeps, gots):
+def squares(meta, ends):
     spots = [(p, half) for p, panel in enumerate(PANELS) for half in panel[2]]
 
     def body(meta, *refs):
-        m = len(keeps)
-        sq_ref, sum_ref, row_ref = refs[2 * m :]
+        sq_ref, sum_ref, row_ref = refs[len(ends) :]
         e = 0
-        for b in range(m):
-            for j in range(keeps[b].shape[0]):
-                x = refs[b][j] + refs[m + b][j]
+        for end in refs[: len(ends)]:
+            for j in range(end.shape[0]):
+                x = end[j]
                 x = x * x
                 p, half = spots[e]
                 at = pl.multiple_of(meta[p] * WIDTH + half * HALF, HALF)
@@ -170,12 +169,12 @@
         out_shape=(jax.ShapeDtypeStruct((16, 4096), F32), jax.ShapeDtypeStruct((16, 32, 128), F32)),
         grid_spec=pltpu.PrefetchScalarGridSpec(
             num_scalar_prefetch=1,
-            in_specs=[whole] * (2 * len(keeps)),
+            in_specs=[whole] * len(ends),
             out_specs=(whole, whole),
             scratch_shapes=[pltpu.VMEM((32, 128), F32)],
         ),
         name="squares",
-    )(meta, *keeps, *gots)
+    )(meta, *ends)
 
 
 def scaled(squared, sums):
@@ -192,32 +191,29 @@
 
 
 def encode(total):
-    n = total.shape[1]
-    top = jnp.max(jnp.abs(total), axis=(0, 2, 3))
+    peers, n = total.shape[:2]
+    top = jnp.max(jnp.abs(total), axis=(0, 2))
     scale = lax.reduce_precision(jnp.maximum(top * (SCALE * 1.002), 6.2e-05), 5, 10)
-    t = total * (SCALE / scale)[None, :, None, None]
-    codes = (t * jnp.abs(t) * TOP).astype(WIRE).reshape(8, n * 32, HALF)
-    rows = jnp.pad(scale.astype(WIRE), ((0, 16 - n), (0, 0)))
-    return jnp.concatenate([codes, jnp.broadcast_to(rows[None], (8, 16, HALF))], axis=1)
-
-
-def decode(coded, n):
-    codes = coded[:, : n * 32].astype(F32).reshape(8, n, 2, 16, HALF)
-    scale = coded[:, n * 32 : n * 33].astype(F32) * (1 / SCALE)
+    t = total * (SCALE / scale)[None, :, None]
+    codes = (t * jnp.abs(t) * TOP).astype(WIRE).reshape(peers, n * 16, HALF)
+    rows = jnp.pad(scale.astype(WIRE), ((0, 8 - n), (0, 0)))
+    return jnp.concatenate([codes, jnp.broadcast_to(rows[None], (peers, 8, HALF))], axis=1)
+
+
+def decode(coded):
+    peers, n = coded.shape[0], (coded.shape[1] - 8) // 16
+    codes = coded[:, : n * 16].astype(F32).reshape(peers, n, 16, HALF)
+    scale = coded[:, n * 16 : n * 17].astype(F32) * (1 / SCALE)
     size = jnp.sqrt(jnp.abs(codes) * (1 / TOP))
-    return jnp.sum(jnp.where(codes < 0, -size, size) * scale[:, :, None, None], axis=0)
+    return jnp.sum(jnp.where(codes < 0, -size, size) * scale[:, :, None], axis=0)
 
 
 def pipeline(walk, values, col_index, col_count):
     meta = coordinates()
     scalars = (meta, col_index.reshape(-1), col_count.reshape(-1))
-    xl = lax.axis_index("xl")
 
     def move(x, **by):
         return send(x, **by)
-
-    def whole(array):
-        return [(array, 0, WIDTH)]
 
     def pair(left, right):
         return [(left, 0, HALF), (right, 0, HALF)]
@@ -230,27 +226,24 @@
     def work(batch, given):
         keep, give = product(batch, scalars, walk, given)
         got = move(give, dc=1)
-        arrived = lax.all_to_all(encode(keep + got), "z", 0, 0, tiled=True)
-        total = decode(arrived, keep.shape[1])
-        mine = lax.dynamic_index_in_dim(total, xl, 1, keepdims=False)
-        other = lax.dynamic_index_in_dim(total, 1 - xl, 1, keepdims=False)
-        ends.append((mine, move(other, dxl=1)))
-
-    up = move(values, dy=1)
-    down = move(values, dy=3)
-    over = move(values, dxh=1)
-    far = [move(up[:, :HALF], dy=1), move(down[:, HALF:], dy=3)]
-    over_half = (over[:, :HALF], over[:, HALF:])
-    over_up = [move(over_half[t], dy=1) for t in range(2)]
-    over_down = [move(over_half[t], dy=3) for t in range(2)]
+        arrived = lax.all_to_all(encode(keep + got), ("z", "xl"), 0, 0, tiled=True)
+        ends.append(decode(arrived))
+
+    own = (values[:, :HALF], values[:, HALF:])
+    up = [move(own[t], dy=1) for t in range(2)]
+    down = [move(own[t], dy=3) for t in range(2)]
+    over = [move(own[t], dxh=1) for t in range(2)]
+    far = [move(up[0], dy=1), move(down[1], dy=3)]
+    over_up = [move(over[t], dy=1) for t in range(2)]
+    over_down = [move(over[t], dy=3) for t in range(2)]
     over_far = [move(far[t], dxh=1) for t in range(2)]
 
-    work(0, [whole(values)])
-    work(1, [whole(up), whole(down), whole(over)])
+    work(0, [[(values, 0, WIDTH)]])
+    work(1, [pair(*up), pair(*down), pair(*over)])
     work(2, [pair(*far), one(over_up[0]), one(over_down[0]), one(over_far[0])])
     work(3, [one(over_up[1]), one(over_down[1]), one(over_far[1])])
 
-    squared, sums = squares(meta, [e[0] for e in ends], [e[1] for e in ends])
+    squared, sums = squares(meta, ends)
     sums = jnp.sum(lax.all_to_all(sums, ("z", "core"), 0, 0), axis=0)
     sums = lax.all_to_all(jnp.broadcast_to(sums[None], (16, 32, 128)), ("xh", "y", "xl"), 0, 0)
     return scaled(squared, sums)

time: 231 us -> 222 us (0.961)
  waiting for transfers between devices: 99.4 us -> 78.1 us
  starting transfers between devices: 54.5 us -> 63.5 us
  local copies, waits for them, and re-layouts: 9.97 us -> 3.31 us
  other arithmetic: 10.8 us -> 15.8 us
  blocking collectives: 28.7 us -> 32.6 us
    ppermute x19 -> x18, waiting for transfers between devices: 55.2 us -> 42.7 us  [send(): return lax.ppermute(x, AXES, moves(**by))]
    all_to_all x4, waiting for transfers between devices: 44.2 us -> 35.4 us  [work(): arrived = lax.all_to_all(encode(keep + got), ('z', 'xl'), 0, 0, tiled=True)]
    ppermute x19 -> x18, starting transfers between devices: 33 us -> 38.9 us  [send(): return lax.ppermute(x, AXES, moves(**by))]
    all_to_all x4, starting transfers between devices: 21.5 us -> 24.6 us  [work(): arrived = lax.all_to_all(encode(keep + got), ('z', 'xl'), 0, 0, tiled=True)]
    all_to_all x1, blocking collectives: 16.4 us -> 19.3 us  [pipeline(): sums = jnp.sum(lax.all_to_all(sums, ('z', 'core'), 0, 0), axis=0)]
    reduce_max x4, other arithmetic: 3.32 us -> 5.89 us  [encode(): top = jnp.max(jnp.abs(total), axis=(0, 2))]
    squeeze x4 -> x0, local copies, waits for them, and re-layouts: 2.55 us -> none  [work(): other = lax.dynamic_index_in_dim(total, 1 - xl, 1, keepdims=False)]
    reduce_sum x4, other arithmetic: 2.16 us -> 4.54 us  [decode(): jnp.sum(jnp.where(codes < 0, -size, size) * scale[:, :, None], axis=0)]
  transfers between devices with their start and end apart: 23 -> 22, of which waited for: 6 -> 10; matrix products, arithmetic and copies ran while one was open for 8% -> 7% of each run, Pallas kernels for 9% -> 7%
where the time goes in v2:
time: 222 us; the launch traced here: 221 us
  waiting for transfers between devices  78.1 us (35%)
  starting transfers between devices  63.5 us (29%)
  blocking collectives  32.6 us (15%)
  Pallas kernels  27.5 us (12%)
  other arithmetic  15.8 us (7%)
  local copies, waits for them, and re-layouts  3.31 us (1%)
    ppermute x18, waiting for transfers between devices, send(): return lax.ppermute(x, AXES, moves(**by))  42.7 us
    ppermute x18, starting transfers between devices, send(): return lax.ppermute(x, AXES, moves(**by))  38.9 us
    all_to_all x4, waiting for transfers between devices, work(): arrived = lax.all_to_all(encode(keep + got), ('z', 'xl'), 0, 0, tiled=True)  35.4 us
    all_to_all x4, starting transfers between devices, work(): arrived = lax.all_to_all(encode(keep + got), ('z', 'xl'), 0, 0, tiled=True)  24.6 us
    pallas_call x4, Pallas kernels, product(): pl.pallas_call(body, out_shape=(out, out), grid_spec=pltpu.PrefetchScalar...  23.2 us
    all_to_all x1, blocking collectives, pipeline(): sums = jnp.sum(lax.all_to_all(sums, ('z', 'core'), 0, 0), axis=0)  19.3 us
    all_to_all x1, blocking collectives, pipeline(): lax.all_to_all(jnp.broadcast_to(sums[None], (16, 32, 128)), ('xh', 'y', '...  13.3 us
    reduce_max x4, other arithmetic, encode(): top = jnp.max(jnp.abs(total), axis=(0, 2))  5.89 us
  transfers between devices with their start and end apart: 22, of which 10 were waited for; matrix products, arithmetic and copies ran while one was open for 7% of the time, Pallas kernels for 7%

profile of v2, /device:TPU:1, one launch (start us, length us, event | category | flops | bytes accessed | tf_op | source)
XLA Modules:
  0.0 221.1 jit_solution(16201933984450664979)
XLA Ops:
  1.5 2.2 collective-permute-start.1
  5.3 2.7 %collective-permute-start.4 = (bf16[1536,256]{1,0:T(8,128)(2,1)S(1)}, bf16[1536,256]{1,0:T(8,128)(2,1)}, u32[]{:S(2)}, u32[]{:S(2)}) collective-permute-start(bf16[1536,256]{1,0:T(8,128)(2,1)S(1)} %get-tuple-element.33), channel_id=1, source_target_pairs={{0,96},{1,97},{2,98},{3,99},{4,100},{5,101},{6,102},{7,103},{8,104... | collective-permute-start | bytes 2359304 | tf_op jit(solution)/shard_map/ppermute | solution.py:42
  7.9 2.7 %collective-permute-start.5 = (bf16[1536,256]{1,0:T(8,128)(2,1)S(1)}, bf16[1536,256]{1,0:T(8,128)(2,1)}, u32[]{:S(2)}, u32[]{:S(2)}) collective-permute-start(bf16[1536,256]{1,0:T(8,128)(2,1)S(1)} %get-tuple-element.34), channel_id=1, source_target_pairs={{0,128},{1,129},{2,130},{3,131},{4,132},{5,133},{6,134},{7,135},{8... | collective-permute-start | bytes 2359304 | tf_op jit(solution)/shard_map/ppermute | solution.py:42
  10.7 9.9 %collective-permute-done.1.refs_0_ = bf16[1536,256]{1,0:T(8,128)(2,1)} collective-permute-done((bf16[1536,256]{1,0:T(8,128)(2,1)S(1)}, bf16[1536,256]{1,0:T(8,128)(2,1)}, u32[]{:S(2)}, u32[]{:S(2)}) %collective-permute-start.1) | collective-permute-done | bytes 786464 | tf_op jit(solution)/shard_map/ppermute | solution.py:42
  20.6 4.4 %collective-permute-start.6 = (bf16[1536,256]{1,0:T(8,128)(2,1)S(1)}, bf16[1536,256]{1,0:T(8,128)(2,1)}, u32[]{:S(2)}, u32[]{:S(2)}) collective-permute-start(bf16[1536,256]{1,0:T(8,128)(2,1)S(1)} %get-tuple-element.33), channel_id=1, source_target_pairs={{0,128},{1,129},{2,130},{3,131},{4,132},{5,133},{6,134},{7,135},{8... | collective-permute-start | bytes 2359304 | tf_op jit(solution)/shard_map/ppermute | solution.py:42
  26.2 11.3 %collective-permute-done.2.refs_1_ = bf16[1536,256]{1,0:T(8,128)(2,1)S(1)} collective-permute-done((bf16[1536,256]{1,0:T(8,128)(2,1)S(1)}, bf16[1536,256]{1,0:T(8,128)(2,1)S(1)}, u32[]{:S(2)}, u32[]{:S(2)}) %collective-permute-start.2) | collective-permute-done | bytes 786464 | tf_op jit(solution)/shard_map/ppermute | solution.py:42
  38.6 4.6 %collective-permute-done.6.refs_5_ = bf16[1536,256]{1,0:T(8,128)(2,1)} collective-permute-done((bf16[1536,256]{1,0:T(8,128)(2,1)S(1)}, bf16[1536,256]{1,0:T(8,128)(2,1)}, u32[]{:S(2)}, u32[]{:S(2)}) %collective-permute-start.6) | collective-permute-done | bytes 786464 | tf_op jit(solution)/shard_map/ppermute | solution.py:42
  43.2 8.7 %shard_map.83 = (f32[16,6,16,256]{3,2,1,0:T(8,128)}, f32[16,6,16,256]{3,2,1,0:T(8,128)}) custom-call(s32[12]{0:T(128)} %multiply_add_fusion.meta, s32[24]{0:T(128)} %reshape.63.index, s32[8]{0:T(128)} %bitcast.25, bf16[512,4096]{1,0:T(8,128)(2,1)} %w_hbm.7, bf16[1536,256]{1,0:T(8,128)(2,1)} %collective-permute-done.1.refs_0_, bf16[1536,256]{1,0:T(8,128)(2,1)} %copy-done.4, ...), custom_call_target="tpu_custom_call" | custom-call | tf_op jit(solution)/shard_map/pallas_call | solution.py:129
  52.4 3.4 %shard_map.82 = (f32[16,2,16,256]{3,2,1,0:T(8,128)}, f32[16,2,16,256]{3,2,1,0:T(8,128)}) custom-call(s32[12]{0:T(128)} %multiply_add_fusion.meta, s32[24]{0:T(128)} %reshape.63.index, s32[8]{0:T(128)} %bitcast.26, bf16[512,4096]{1,0:T(8,128)(2,1)} %w_hbm.7, bf16[1536,512]{1,0:T(8,128)(2,1)} %refs_0_.1), custom_call_target="tpu_custom_call" | custom-call | tf_op jit(solution)/shard_map/pallas_call | solution.py:129
  57.0 3.1 %collective-permute-start.9 = (bf16[1536,256]{1,0:T(8,128)(2,1)}, bf16[1536,256]{1,0:T(8,128)(2,1)}, u32[]{:S(2)}, u32[]{:S(2)}) collective-permute-start(bf16[1536,256]{1,0:T(8,128)(2,1)} %collective-permute-done.4.refs_3_), channel_id=1, source_target_pairs={{0,96},{1,97},{2,98},{3,99},{4,100},{5,101},{6,102},{7,103},{8,104... | collective-permute-start | bytes 2359304 | tf_op jit(solution)/shard_map/ppermute | solution.py:42
  62.6 2.7 %collective-permute-start.15 = (bf16[1536,256]{1,0:T(8,128)(2,1)}, bf16[1536,256]{1,0:T(8,128)(2,1)}, u32[]{:S(2)}, u32[]{:S(2)}) collective-permute-start(bf16[1536,256]{1,0:T(8,128)(2,1)} %collective-permute-done.6.refs_5_), channel_id=1, source_target_pairs={{0,96},{1,97},{2,98},{3,99},{4,100},{5,101},{6,102},{7,103},{8,104... | collective-permute-start | bytes 2359304 | tf_op jit(solution)/shard_map/ppermute | solution.py:42
  65.3 11.6 %collective-permute-done.9.refs_1_ = bf16[1536,256]{1,0:T(8,128)(2,1)} collective-permute-done((bf16[1536,256]{1,0:T(8,128)(2,1)}, bf16[1536,256]{1,0:T(8,128)(2,1)}, u32[]{:S(2)}, u32[]{:S(2)}) %collective-permute-start.9) | collective-permute-done | bytes 786464 | tf_op jit(solution)/shard_map/ppermute | solution.py:42
  76.9 4.3 %collective-permute-start.16 = (bf16[1536,256]{1,0:T(8,128)(2,1)}, bf16[1536,256]{1,0:T(8,128)(2,1)}, u32[]{:S(2)}, u32[]{:S(2)}) collective-permute-start(bf16[1536,256]{1,0:T(8,128)(2,1)} %collective-permute-done.9.refs_1_), channel_id=1, source_target_pairs={{0,128},{1,129},{2,130},{3,131},{4,132},{5,133},{6,134},{7,135},{8... | collective-permute-start | bytes 2359304 | tf_op jit(solution)/shard_map/ppermute | solution.py:42
  82.1 7.4 %all-to-all-start = ((f16[16,40,256]{2,1,0:T(8,128)(2,1)}), f16[16,40,256]{2,1,0:T(8,128)(2,1)S(1)}, u32[]{:S(2)}, u32[]{:S(2)}) async-start(f16[16,40,256]{2,1,0:T(8,128)(2,1)} %pad_maximum_fusion.3), calls=%async_computation | async-start | bytes 655360 | tf_op jit(solution)/shard_map/all_to_all | solution.py:229
  90.7 1.8 abs_reduce_fusion
  92.5 2.2 %collective-permute-start.11 = (bf16[1536,256]{1,0:T(8,128)(2,1)}, bf16[1536,256]{1,0:T(8,128)(2,1)}, u32[]{:S(2)}, u32[]{:S(2)}) collective-permute-start(bf16[1536,256]{1,0:T(8,128)(2,1)} %collective-permute-done.5.refs_4_), channel_id=1, source_target_pairs={{0,96},{1,97},{2,98},{3,99},{4,100},{5,101},{6,102},{7,103},{8,104... | collective-permute-start | bytes 2359304 | tf_op jit(solution)/shard_map/ppermute | solution.py:42
  94.7 3.6 %collective-permute-done.14.refs_0_ = bf16[1536,256]{1,0:T(8,128)(2,1)} collective-permute-done((bf16[1536,256]{1,0:T(8,128)(2,1)}, bf16[1536,256]{1,0:T(8,128)(2,1)}, u32[]{:S(2)}, u32[]{:S(2)}) %collective-permute-start.14) | collective-permute-done | bytes 786464 | tf_op jit(solution)/shard_map/ppermute | solution.py:42
  98.4 4.7 %collective-permute-start.12 = (bf16[1536,256]{1,0:T(8,128)(2,1)}, bf16[1536,256]{1,0:T(8,128)(2,1)}, u32[]{:S(2)}, u32[]{:S(2)}) collective-permute-start(bf16[1536,256]{1,0:T(8,128)(2,1)} %collective-permute-done.8.refs_0_), channel_id=1, source_target_pairs={{0,128},{1,129},{2,130},{3,131},{4,132},{5,133},{6,134},{7,135},{8... | collective-permute-start | bytes 2359304 | tf_op jit(solution)/shard_map/ppermute | solution.py:42
  103.1 4.2 %shard_map.85 = (f32[16,3,16,256]{3,2,1,0:T(8,128)}, f32[16,3,16,256]{3,2,1,0:T(8,128)}) custom-call(s32[12]{0:T(128)} %multiply_add_fusion.meta, s32[24]{0:T(128)} %reshape.63.index, s32[8]{0:T(128)} %bitcast.27, bf16[512,4096]{1,0:T(8,128)(2,1)} %w_hbm.7, bf16[1536,256]{1,0:T(8,128)(2,1)} %collective-permute-done.14.refs_0_, ...), custom_call_target="tpu_custom_call" | custom-call | tf_op jit(solution)/shard_map/pallas_call | solution.py:129
  107.3 2.5 %collective-permute-start.17 = (f32[16,3,16,256]{3,2,1,0:T(8,128)}, f32[16,3,16,256]{3,2,1,0:T(8,128)}, u32[]{:S(2)}, u32[]{:S(2)}) collective-permute-start(f32[16,3,16,256]{3,2,1,0:T(8,128)} %get-tuple-element.22), channel_id=1, source_target_pairs={{0,1},{1,0},{2,3},{3,2},{4,5},{5,4},{6,7},{7,6},{8,9},{9,8},{10,11... | collective-permute-start | bytes 2359304 | tf_op jit(solution)/shard_map/ppermute | solution.py:42
  111.3 8.0 %all-to-all-start.1 = ((f16[16,104,256]{2,1,0:T(8,128)(2,1)}), f16[16,104,256]{2,1,0:T(8,128)(2,1)S(1)}, u32[]{:S(2)}, u32[]{:S(2)}) async-start(f16[16,104,256]{2,1,0:T(8,128)(2,1)} %pad_maximum_fusion), calls=%async_computation.1 | async-start | bytes 1703936 | tf_op jit(solution)/shard_map/all_to_all | solution.py:229
  119.7 6.9 %shard_map.84 = (f32[16,5,16,256]{3,2,1,0:T(8,128)}, f32[16,5,16,256]{3,2,1,0:T(8,128)}) custom-call(s32[12]{0:T(128)} %multiply_add_fusion.meta, s32[24]{0:T(128)} %reshape.63.index, s32[8]{0:T(128)} %bitcast.28, bf16[512,4096]{1,0:T(8,128)(2,1)} %w_hbm.7, bf16[1536,256]{1,0:T(8,128)(2,1)} %collective-permute-done.8.refs_0_, ...), custom_call_target="tpu_custom_call" | custom-call | tf_op jit(solution)/shard_map/pallas_call | solution.py:129
  126.7 2.8 %collective-permute-start.13 = (f32[16,5,16,256]{3,2,1,0:T(8,128)}, f32[16,5,16,256]{3,2,1,0:T(8,128)}, u32[]{:S(2)}, u32[]{:S(2)}) collective-permute-start(f32[16,5,16,256]{3,2,1,0:T(8,128)} %get-tuple-element.20), channel_id=1, source_target_pairs={{0,1},{1,0},{2,3},{3,2},{4,5},{5,4},{6,7},{7,6},{8,9},{9,8},{10,11... | collective-permute-start | bytes 3932168 | tf_op jit(solution)/shard_map/ppermute | solution.py:42
  131.8 9.7 %all-to-all-done.1 = f16[16,104,256]{2,1,0:T(8,128)(2,1)S(1)} async-done(((f16[16,104,256]{2,1,0:T(8,128)(2,1)}), f16[16,104,256]{2,1,0:T(8,128)(2,1)S(1)}, u32[]{:S(2)}, u32[]{:S(2)}) %all-to-all-start.1) | async-done | bytes 852000 | tf_op jit(solution)/shard_map/all_to_all | solution.py:229
  141.5 5.2 %all-to-all-start.3 = ((f16[16,56,256]{2,1,0:T(8,128)(2,1)}), f16[16,56,256]{2,1,0:T(8,128)(2,1)S(1)}, u32[]{:S(2)}, u32[]{:S(2)}) async-start(f16[16,56,256]{2,1,0:T(8,128)(2,1)} %pad_maximum_fusion.2), calls=%async_computation.3 | async-start | bytes 917504 | tf_op jit(solution)/shard_map/all_to_all | solution.py:229
  149.7 10.8 %all-to-all-done.3 = f16[16,56,256]{2,1,0:T(8,128)(2,1)S(1)} async-done(((f16[16,56,256]{2,1,0:T(8,128)(2,1)}), f16[16,56,256]{2,1,0:T(8,128)(2,1)S(1)}, u32[]{:S(2)}, u32[]{:S(2)}) %all-to-all-start.3) | async-done | bytes 458784 | tf_op jit(solution)/shard_map/all_to_all | solution.py:229
  160.5 4.1 %all-to-all-start.2 = ((f16[16,88,256]{2,1,0:T(8,128)(2,1)}), f16[16,88,256]{2,1,0:T(8,128)(2,1)S(1)}, u32[]{:S(2)}, u32[]{:S(2)}) async-start(f16[16,88,256]{2,1,0:T(8,128)(2,1)} %pad_maximum_fusion.1), calls=%async_computation.2 | async-start | bytes 1441792 | tf_op jit(solution)/shard_map/all_to_all | solution.py:229
  167.9 14.9 %all-to-all-done.2 = f16[16,88,256]{2,1,0:T(8,128)(2,1)S(1)} async-done(((f16[16,88,256]{2,1,0:T(8,128)(2,1)}), f16[16,88,256]{2,1,0:T(8,128)(2,1)S(1)}, u32[]{:S(2)}, u32[]{:S(2)}) %all-to-all-start.2) | async-done | bytes 720928 | tf_op jit(solution)/shard_map/all_to_all | solution.py:229
  184.1 2.5 %squares.1 = (f32[16,4096]{1,0:T(8,128)}, f32[16,32,128]{2,1,0:T(8,128)}) custom-call(s32[12]{0:T(128)} %multiply_add_fusion.meta, f32[2,16,256]{2,1,0:T(8,128)} %bitcast.24, f32[6,16,256]{2,1,0:T(8,128)} %bitcast.21, f32[5,16,256]{2,1,0:T(8,128)} %bitcast.22, f32[3,16,256]{2,1,0:T(8,128)} %bitcast.23), custom_call_target="tpu_custom_call" | custom-call | tf_op jit(solution)/shard_map/squares/pallas_call | solution.py:167
  186.6 19.3 %all_to_all.30 = f32[16,32,128]{2,1,0:T(8,128)S(1)} all-to-all(f32[16,32,128]{2,1,0:T(8,128)} %get-tuple-element.24), channel_id=1, replica_groups=mesh['xh'=2,'y'=4,'z'=8,'xl'=2,'core'=2] {'z','core'}, dimensions={0} | all-to-all | bytes 524288 | tf_op jit(solution)/shard_map/all_to_all | solution.py:247
  206.0 13.3 %all_to_all.31.sum_ref = f32[16,32,128]{2,1,0:T(8,128)} all-to-all(f32[16,32,128]{2,1,0:T(8,128)S(1)} %broadcast_in_dim.14), channel_id=1, replica_groups=mesh['xh'=2,'y'=4,'z'=8,'xl'=2,'core'=2] {'xh','y','xl'}, dimensions={0} | all-to-all | bytes 524288 | tf_op jit(solution)/shard_map/all_to_all | solution.py:248
  219.3 1.8 scaled.1
  (79 shorter events, 23.5 us)
Async XLA Ops:
  0.0 25.6 %copy-start.7 = (s32[12]{0:T(128)S(1)}, s32[12]{0:T(128)}, u32[]{:S(2)}) copy-start(s32[12]{0:T(128)} %constant.37.clone) | copy-start | bytes 148
  0.0 25.6 %copy-start.8 = (s32[12]{0:T(128)S(1)}, s32[12]{0:T(128)}, u32[]{:S(2)}) copy-start(s32[12]{0:T(128)} %constant.36.clone) | copy-start | bytes 148
  0.0 25.6 %copy-start.9 = (s32[12]{0:T(128)S(1)}, s32[12]{0:T(128)}, u32[]{:S(2)}) copy-start(s32[12]{0:T(128)} %constant.35.clone) | copy-start | bytes 148
  0.0 25.6 %copy-start.10 = (s32[12]{0:T(128)S(1)}, s32[12]{0:T(128)}, u32[]{:S(2)}) copy-start(s32[12]{0:T(128)} %constant.34.clone) | copy-start | bytes 148
  0.0 25.0 %copy-start.6 = (s32[3,8]{1,0:T(4,128)S(1)}, s32[3,8]{1,0:T(4,128)}, u32[]{:S(2)}) copy-start(s32[3,8]{1,0:T(4,128)} %param.10) | copy-start | bytes 292
  1.5 19.1 %collective-permute-start.1 = (bf16[1536,256]{1,0:T(8,128)(2,1)S(1)}, bf16[1536,256]{1,0:T(8,128)(2,1)}, u32[]{:S(2)}, u32[]{:S(2)}) collective-permute-start(bf16[1536,256]{1,0:T(8,128)(2,1)S(1)} %get-tuple-element.34), channel_id=1, source_target_pairs={{0,32},{1,33},{2,34},{3,35},{4,36},{5,37},{6,38},{7,39},{8,40},{9,... | collective-permute-start | bytes 2359304 | tf_op jit(solution)/shard_map/ppermute | solution.py:42
  3.7 33.7 %collective-permute-start.3 = (bf16[1536,256]{1,0:T(8,128)(2,1)S(1)}, bf16[1536,256]{1,0:T(8,128)(2,1)S(1)}, u32[]{:S(2)}, u32[]{:S(2)}) collective-permute-start(bf16[1536,256]{1,0:T(8,128)(2,1)S(1)} %get-tuple-element.34), channel_id=1, source_target_pairs={{0,96},{1,97},{2,98},{3,99},{4,100},{5,101},{6,102},{7,103},{8,104... | collective-permute-start | bytes 2359304 | tf_op jit(solution)/shard_map/ppermute | solution.py:42
  5.2 32.2 %collective-permute-start.2 = (bf16[1536,256]{1,0:T(8,128)(2,1)S(1)}, bf16[1536,256]{1,0:T(8,128)(2,1)S(1)}, u32[]{:S(2)}, u32[]{:S(2)}) collective-permute-start(bf16[1536,256]{1,0:T(8,128)(2,1)S(1)} %get-tuple-element.33), channel_id=1, source_target_pairs={{0,32},{1,33},{2,34},{3,35},{4,36},{5,37},{6,38},{7,39},{8,40},{9,... | collective-permute-start | bytes 2359304 | tf_op jit(solution)/shard_map/ppermute | solution.py:42
  5.3 33.4 %collective-permute-start.4 = (bf16[1536,256]{1,0:T(8,128)(2,1)S(1)}, bf16[1536,256]{1,0:T(8,128)(2,1)}, u32[]{:S(2)}, u32[]{:S(2)}) collective-permute-start(bf16[1536,256]{1,0:T(8,128)(2,1)S(1)} %get-tuple-element.33), channel_id=1, source_target_pairs={{0,96},{1,97},{2,98},{3,99},{4,100},{5,101},{6,102},{7,103},{8,104... | collective-permute-start | bytes 2359304 | tf_op jit(solution)/shard_map/ppermute | solution.py:42
  7.9 30.7 %collective-permute-start.5 = (bf16[1536,256]{1,0:T(8,128)(2,1)S(1)}, bf16[1536,256]{1,0:T(8,128)(2,1)}, u32[]{:S(2)}, u32[]{:S(2)}) collective-permute-start(bf16[1536,256]{1,0:T(8,128)(2,1)S(1)} %get-tuple-element.34), channel_id=1, source_target_pairs={{0,128},{1,129},{2,130},{3,131},{4,132},{5,133},{6,134},{7,135},{8... | collective-permute-start | bytes 2359304 | tf_op jit(solution)/shard_map/ppermute | solution.py:42
  20.6 22.6 %collective-permute-start.6 = (bf16[1536,256]{1,0:T(8,128)(2,1)S(1)}, bf16[1536,256]{1,0:T(8,128)(2,1)}, u32[]{:S(2)}, u32[]{:S(2)}) collective-permute-start(bf16[1536,256]{1,0:T(8,128)(2,1)S(1)} %get-tuple-element.33), channel_id=1, source_target_pairs={{0,128},{1,129},{2,130},{3,131},{4,132},{5,133},{6,134},{7,135},{8... | collective-permute-start | bytes 2359304 | tf_op jit(solution)/shard_map/ppermute | solution.py:42
  37.5 5.8 %copy-start.4 = (bf16[1536,256]{1,0:T(8,128)(2,1)}, bf16[1536,256]{1,0:T(8,128)(2,1)S(1)}, u32[]{:S(2)}) copy-start(bf16[1536,256]{1,0:T(8,128)(2,1)S(1)} %collective-permute-done.2.refs_1_) | copy-start | bytes 2359300
  37.5 5.8 %copy-start.3 = (bf16[1536,256]{1,0:T(8,128)(2,1)}, bf16[1536,256]{1,0:T(8,128)(2,1)S(1)}, u32[]{:S(2)}) copy-start(bf16[1536,256]{1,0:T(8,128)(2,1)S(1)} %collective-permute-done.3.refs_2_) | copy-start | bytes 2359300
  51.9 37.6 %collective-permute-start.7 = (f32[16,6,16,256]{3,2,1,0:T(8,128)}, f32[16,6,16,256]{3,2,1,0:T(8,128)S(1)}, u32[]{:S(2)}, u32[]{:S(2)}) collective-permute-start(f32[16,6,16,256]{3,2,1,0:T(8,128)} %get-tuple-element.18), channel_id=1, source_target_pairs={{0,1},{1,0},{2,3},{3,2},{4,5},{5,4},{6,7},{7,6},{8,9},{9,8},{10,11... | collective-permute-start | bytes 4718600 | tf_op jit(solution)/shard_map/ppermute | solution.py:42
  55.9 4.2 %collective-permute-start = (f32[16,2,16,256]{3,2,1,0:T(8,128)}, f32[16,2,16,256]{3,2,1,0:T(8,128)S(1)}, u32[]{:S(2)}, u32[]{:S(2)}) collective-permute-start(f32[16,2,16,256]{3,2,1,0:T(8,128)} %get-tuple-element.16), channel_id=1, source_target_pairs={{0,1},{1,0},{2,3},{3,2},{4,5},{5,4},{6,7},{7,6},{8,9},{9,8},{10,11... | collective-permute-start | bytes 1572872 | tf_op jit(solution)/shard_map/ppermute | solution.py:42
  57.0 19.9 %collective-permute-start.9 = (bf16[1536,256]{1,0:T(8,128)(2,1)}, bf16[1536,256]{1,0:T(8,128)(2,1)}, u32[]{:S(2)}, u32[]{:S(2)}) collective-permute-start(bf16[1536,256]{1,0:T(8,128)(2,1)} %collective-permute-done.4.refs_3_), channel_id=1, source_target_pairs={{0,96},{1,97},{2,98},{3,99},{4,100},{5,101},{6,102},{7,103},{8,104... | collective-permute-start | bytes 2359304 | tf_op jit(solution)/shard_map/ppermute | solution.py:42
  60.1 30.6 %copy-start = (f32[16,6,16,256]{3,2,1,0:T(8,128)S(1)}, f32[16,6,16,256]{3,2,1,0:T(8,128)}, u32[]{:S(2)}) copy-start(f32[16,6,16,256]{3,2,1,0:T(8,128)} %get-tuple-element.17) | copy-start | bytes 4718596
  61.3 31.2 %collective-permute-start.8 = (bf16[1536,256]{1,0:T(8,128)(2,1)}, bf16[1536,256]{1,0:T(8,128)(2,1)}, u32[]{:S(2)}, u32[]{:S(2)}) collective-permute-start(bf16[1536,256]{1,0:T(8,128)(2,1)} %collective-permute-done.1.refs_0_), channel_id=1, source_target_pairs={{0,32},{1,33},{2,34},{3,35},{4,36},{5,37},{6,38},{7,39},{8,40},{9,... | collective-permute-start | bytes 2359304 | tf_op jit(solution)/shard_map/ppermute | solution.py:42
  62.5 35.9 %collective-permute-start.14 = (bf16[1536,256]{1,0:T(8,128)(2,1)}, bf16[1536,256]{1,0:T(8,128)(2,1)}, u32[]{:S(2)}, u32[]{:S(2)}) collective-permute-start(bf16[1536,256]{1,0:T(8,128)(2,1)} %collective-permute-done.6.refs_5_), channel_id=1, source_target_pairs={{0,32},{1,33},{2,34},{3,35},{4,36},{5,37},{6,38},{7,39},{8,40},{9,... | collective-permute-start | bytes 2359304 | tf_op jit(solution)/shard_map/ppermute | solution.py:42
  62.6 40.5 %collective-permute-start.15 = (bf16[1536,256]{1,0:T(8,128)(2,1)}, bf16[1536,256]{1,0:T(8,128)(2,1)}, u32[]{:S(2)}, u32[]{:S(2)}) collective-permute-start(bf16[1536,256]{1,0:T(8,128)(2,1)} %collective-permute-done.6.refs_5_), channel_id=1, source_target_pairs={{0,96},{1,97},{2,98},{3,99},{4,100},{5,101},{6,102},{7,103},{8,104... | collective-permute-start | bytes 2359304 | tf_op jit(solution)/shard_map/ppermute | solution.py:42
  76.9 26.3 %collective-permute-start.16 = (bf16[1536,256]{1,0:T(8,128)(2,1)}, bf16[1536,256]{1,0:T(8,128)(2,1)}, u32[]{:S(2)}, u32[]{:S(2)}) collective-permute-start(bf16[1536,256]{1,0:T(8,128)(2,1)} %collective-permute-done.9.refs_1_), channel_id=1, source_target_pairs={{0,128},{1,129},{2,130},{3,131},{4,132},{5,133},{6,134},{7,135},{8... | collective-permute-start | bytes 2359304 | tf_op jit(solution)/shard_map/ppermute | solution.py:42
  82.1 29.1 %all-to-all-start = ((f16[16,40,256]{2,1,0:T(8,128)(2,1)}), f16[16,40,256]{2,1,0:T(8,128)(2,1)S(1)}, u32[]{:S(2)}, u32[]{:S(2)}) async-start(f16[16,40,256]{2,1,0:T(8,128)(2,1)} %pad_maximum_fusion.3), calls=%async_computation | async-start | bytes 655360 | tf_op jit(solution)/shard_map/all_to_all | solution.py:229
  89.5 29.7 %collective-permute-start.10 = (bf16[1536,256]{1,0:T(8,128)(2,1)}, bf16[1536,256]{1,0:T(8,128)(2,1)}, u32[]{:S(2)}, u32[]{:S(2)}) collective-permute-start(bf16[1536,256]{1,0:T(8,128)(2,1)} %collective-permute-done.5.refs_4_), channel_id=1, source_target_pairs={{0,32},{1,33},{2,34},{3,35},{4,36},{5,37},{6,38},{7,39},{8,40},{9,... | collective-permute-start | bytes 2359304 | tf_op jit(solution)/shard_map/ppermute | solution.py:42
  92.5 26.8 %collective-permute-start.11 = (bf16[1536,256]{1,0:T(8,128)(2,1)}, bf16[1536,256]{1,0:T(8,128)(2,1)}, u32[]{:S(2)}, u32[]{:S(2)}) collective-permute-start(bf16[1536,256]{1,0:T(8,128)(2,1)} %collective-permute-done.5.refs_4_), channel_id=1, source_target_pairs={{0,96},{1,97},{2,98},{3,99},{4,100},{5,101},{6,102},{7,103},{8,104... | collective-permute-start | bytes 2359304 | tf_op jit(solution)/shard_map/ppermute | solution.py:42
  98.4 21.4 %collective-permute-start.12 = (bf16[1536,256]{1,0:T(8,128)(2,1)}, bf16[1536,256]{1,0:T(8,128)(2,1)}, u32[]{:S(2)}, u32[]{:S(2)}) collective-permute-start(bf16[1536,256]{1,0:T(8,128)(2,1)} %collective-permute-done.8.refs_0_), channel_id=1, source_target_pairs={{0,128},{1,129},{2,130},{3,131},{4,132},{5,133},{6,134},{7,135},{8... | collective-permute-start | bytes 2359304 | tf_op jit(solution)/shard_map/ppermute | solution.py:42
  107.3 22.2 %collective-permute-start.17 = (f32[16,3,16,256]{3,2,1,0:T(8,128)}, f32[16,3,16,256]{3,2,1,0:T(8,128)}, u32[]{:S(2)}, u32[]{:S(2)}) collective-permute-start(f32[16,3,16,256]{3,2,1,0:T(8,128)} %get-tuple-element.22), channel_id=1, source_target_pairs={{0,1},{1,0},{2,3},{3,2},{4,5},{5,4},{6,7},{7,6},{8,9},{9,8},{10,11... | collective-permute-start | bytes 2359304 | tf_op jit(solution)/shard_map/ppermute | solution.py:42
  111.3 30.2 %all-to-all-start.1 = ((f16[16,104,256]{2,1,0:T(8,128)(2,1)}), f16[16,104,256]{2,1,0:T(8,128)(2,1)S(1)}, u32[]{:S(2)}, u32[]{:S(2)}) async-start(f16[16,104,256]{2,1,0:T(8,128)(2,1)} %pad_maximum_fusion), calls=%async_computation.1 | async-start | bytes 1703936 | tf_op jit(solution)/shard_map/all_to_all | solution.py:229
  119.2 10.2 %copy-start.5 = (f32[16,3,16,256]{3,2,1,0:T(8,128)S(1)}, f32[16,3,16,256]{3,2,1,0:T(8,128)}, u32[]{:S(2)}) copy-start(f32[16,3,16,256]{3,2,1,0:T(8,128)} %get-tuple-element.21) | copy-start | bytes 2359300
  126.7 20.0 %collective-permute-start.13 = (f32[16,5,16,256]{3,2,1,0:T(8,128)}, f32[16,5,16,256]{3,2,1,0:T(8,128)}, u32[]{:S(2)}, u32[]{:S(2)}) collective-permute-start(f32[16,5,16,256]{3,2,1,0:T(8,128)} %get-tuple-element.20), channel_id=1, source_target_pairs={{0,1},{1,0},{2,3},{3,2},{4,5},{5,4},{6,7},{7,6},{8,9},{9,8},{10,11... | collective-permute-start | bytes 3932168 | tf_op jit(solution)/shard_map/ppermute | solution.py:42
  130.7 16.0 %copy-start.2 = (f32[16,5,16,256]{3,2,1,0:T(8,128)S(1)}, f32[16,5,16,256]{3,2,1,0:T(8,128)}, u32[]{:S(2)}) copy-start(f32[16,5,16,256]{3,2,1,0:T(8,128)} %get-tuple-element.19) | copy-start | bytes 3932164
  141.5 19.0 %all-to-all-start.3 = ((f16[16,56,256]{2,1,0:T(8,128)(2,1)}), f16[16,56,256]{2,1,0:T(8,128)(2,1)S(1)}, u32[]{:S(2)}, u32[]{:S(2)}) async-start(f16[16,56,256]{2,1,0:T(8,128)(2,1)} %pad_maximum_fusion.2), calls=%async_computation.3 | async-start | bytes 917504 | tf_op jit(solution)/shard_map/all_to_all | solution.py:229
  160.5 22.4 %all-to-all-start.2 = ((f16[16,88,256]{2,1,0:T(8,128)(2,1)}), f16[16,88,256]{2,1,0:T(8,128)(2,1)S(1)}, u32[]{:S(2)}, u32[]{:S(2)}) async-start(f16[16,88,256]{2,1,0:T(8,128)(2,1)} %pad_maximum_fusion.1), calls=%async_computation.2 | async-start | bytes 1441792 | tf_op jit(solution)/shard_map/all_to_all | solution.py:229
  (1 other events, 1.2 us)

commit v3 on v1

--- a/solution.py
+++ b/solution.py
@@ -23,8 +23,8 @@
 BATCHES = (
     ((0, 0, (0, 1)),),
     ((0, 3, (0, 1)), (0, 1, (0, 1)), (1, 0, (0, 1))),
-    ((0, 2, (0, 1)), (1, 3, (0,)), (1, 1, (0,)), (1, 2, (0,))),
-    ((1, 3, (1,)), (1, 1, (1,)), (1, 2, (1,))),
+    ((0, 2, (0, 1)),),
+    ((1, 3, (0, 1)), (1, 1, (0, 1)), (1, 2, (0, 1))),
 )
 PANELS = tuple(itertools.chain(*BATCHES))
 CORE, XLO = len(PANELS), len(PANELS) + 1
@@ -51,7 +51,7 @@
     return panels + core * (spot == CORE) + xl * (spot == XLO)
 
 
-def product(batch, scalars, walk, values, xl_first):
+def product(batch, scalars, walk, values, both):
     panels = BATCHES[batch]
     first = sum(len(b) for b in BATCHES[:batch])
     rows = walk.shape[0]
@@ -120,14 +120,12 @@
 
                     each(k, s, add)
                 for column in range(0, width, HALF):
-                    for r, at in ((0, xl), (1, 1 - xl)):
-                        to = (r, slice(None), half) if xl_first else (slice(None), r, half)
-                        keep_ref[to] = acc_ref[:, at, core, :, column : column + HALF]
-                        send_ref[to] = acc_ref[:, at, 1 - core, :, column : column + HALF]
+                    for r, at in ((0, 0), (1, 1)) if both else ((0, xl), (1, 1 - xl)):
+                        keep_ref[:, r, half] = acc_ref[:, at, core, :, column : column + HALF]
+                        send_ref[:, r, half] = acc_ref[:, at, 1 - core, :, column : column + HALF]
                     half += 1
 
-    lead = (2, rows // 64) if xl_first else (rows // 64, 2)
-    out = jax.ShapeDtypeStruct((*lead, halves, 16, HALF), F32)
+    out = jax.ShapeDtypeStruct((rows // 64, 2, halves, 16, HALF), F32)
     blank = pl.BlockSpec(memory_space=pl.ANY)
     whole = pl.BlockSpec(memory_space=pltpu.VMEM)
     return pl.pallas_call(
@@ -199,20 +197,20 @@
 
 
 def encode(total):
-    n = total.shape[-3]
+    peers, n = total.shape[0], total.shape[-3]
     top = jnp.max(jnp.abs(total), axis=(*range(total.ndim - 3), total.ndim - 2))
     scale = lax.reduce_precision(jnp.maximum(top * (SCALE * 1.002), 6.2e-05), 5, 10)
     t = total * (SCALE / scale)[:, None]
-    codes = (t * jnp.abs(t) * TOP).astype(WIRE).reshape(8, -1, HALF)
-    rows = jnp.pad(scale.astype(WIRE), ((0, 16 - n), (0, 0)))
-    return jnp.concatenate([codes, jnp.broadcast_to(rows[None], (8, 16, HALF))], axis=1)
+    codes = (t * jnp.abs(t) * TOP).astype(WIRE).reshape(peers, -1, HALF)
+    rows = jnp.pad(scale.astype(WIRE), ((0, 8 - n), (0, 0)))
+    return jnp.concatenate([codes, jnp.broadcast_to(rows[None], (peers, 8, HALF))], axis=1)
 
 
 def decode(coded, shape):
-    end = coded.shape[1] - 16
-    codes = coded[:, :end].astype(F32).reshape(8, *shape)
+    peers, end = coded.shape[0], coded.shape[1] - 8
+    codes = coded[:, :end].astype(F32).reshape(peers, *shape)
     scale = coded[:, end : end + shape[-3]].astype(F32) * (1 / SCALE)
-    scale = scale.reshape(8, *([1] * (len(shape) - 3)), shape[-3], 1, HALF)
+    scale = scale.reshape(peers, *([1] * (len(shape) - 3)), shape[-3], 1, HALF)
     size = jnp.sqrt(jnp.abs(codes) * (1 / TOP))
     return jnp.sum(jnp.where(codes < 0, -size, size) * scale, axis=0)
 
@@ -230,18 +228,15 @@
     def pair(left, right):
         return [(left, 0, HALF), (right, 0, HALF)]
 
-    def one(array):
-        return [(array, 0, HALF)]
-
     ends = []
 
-    def work(batch, given, xl_first=False):
-        keep, give = product(batch, scalars, walk, given, xl_first)
+    def work(batch, given, both=False):
+        keep, give = product(batch, scalars, walk, given, both)
         got = move(give, dc=1)
         n = keep.shape[2]
-        if xl_first:
-            other = move(keep[1] + got[1], dxl=1)
-            arrived = lax.all_to_all(encode(keep[0] + got[0] + other), "z", 0, 0, tiled=True)
+        if both:
+            coded = encode((keep + got).reshape(16, n, 16, HALF))
+            arrived = lax.all_to_all(coded, ("z", "xl"), 0, 0, tiled=True)
             ends.append((decode(arrived, (n, 16, HALF)),))
         else:
             arrived = lax.all_to_all(encode(keep + got), "z", 0, 0, tiled=True)
@@ -252,19 +247,18 @@
     down = move(values, dy=3)
     over = move(values, dxh=1)
     far = [move(up[:, :HALF], dy=1), move(down[:, HALF:], dy=3)]
-    over_half = (over[:, :HALF], over[:, HALF:])
-    over_up = [move(over_half[t], dy=1) for t in range(2)]
-    over_down = [move(over_half[t], dy=3) for t in range(2)]
+    over_up = move(over, dy=1)
+    over_down = move(over, dy=3)
     over_far = [move(far[t], dxh=1) for t in range(2)]
 
     work(0, [whole(values)])
     work(1, [whole(up), whole(down), whole(over)])
-    work(2, [pair(*far), one(over_up[0]), one(over_down[0]), one(over_far[0])])
-    work(3, [one(over_up[1]), one(over_down[1]), one(over_far[1])], xl_first=True)
+    work(2, [pair(*far)])
+    work(3, [whole(over_up), whole(over_down), pair(*over_far)], both=True)
 
     squared, sums = squares(meta, ends)
-    sums = jnp.sum(lax.all_to_all(sums, ("z", "core"), 0, 0), axis=0)
-    sums = lax.all_to_all(jnp.broadcast_to(sums[None], (16, 32, 128)), ("xh", "y", "xl"), 0, 0)
+    sums = jnp.sum(lax.all_to_all(sums, ("z", "xl"), 0, 0), axis=0)
+    sums = lax.all_to_all(jnp.broadcast_to(sums[None], (16, 32, 128)), ("xh", "y", "core"), 0, 0)
     return scaled(squared, sums)
 
 

time: 232 us -> 240 us (1.034)
  waiting for transfers between devices: 81.3 us -> 106 us
  starting transfers between devices: 68.9 us -> 52.9 us
  local copies, waits for them, and re-layouts: 9.32 us -> 5.29 us
  blocking collectives: 28.9 us -> 32.8 us
    ppermute x19 -> x16, waiting for transfers between devices: 36.9 us -> 58.9 us  [send(): return lax.ppermute(x, AXES, moves(**by))]
    ppermute x19 -> x16, starting transfers between devices: 45.2 us -> 30.4 us  [send(): return lax.ppermute(x, AXES, moves(**by))]
    all_to_all x1, waiting for transfers between devices: 8.67 us -> 14.2 us  [work(): arrived = lax.all_to_all(coded, ('z', 'xl'), 0, 0, tiled=True)]
    all_to_all x1, blocking collectives: 13.2 us -> 17.8 us  [pipeline(): lax.all_to_all(jnp.broadcast_to(sums[None], (16, 32, 128)), ('xh', 'y', '...]
    all_to_all x3, waiting for transfers between devices: 35.7 us -> 32.6 us  [work(): arrived = lax.all_to_all(encode(keep + got), 'z', 0, 0, tiled=True)]
  transfers between devices with their start and end apart: 23 -> 20, of which waited for: 7 -> 10; matrix products, arithmetic and copies ran while one was open for 10% -> 9% of each run, Pallas kernels for 9% -> 9%
where the time goes in v3:
time: 240 us; the launch traced here: 239 us
  waiting for transfers between devices  106 us (44%)
  starting transfers between devices  52.9 us (22%)
  blocking collectives  32.8 us (14%)
  Pallas kernels  25.3 us (11%)
  other arithmetic  16.3 us (7%)
  local copies, waits for them, and re-layouts  5.29 us (2%)
    ppermute x16, waiting for transfers between devices, send(): return lax.ppermute(x, AXES, moves(**by))  58.9 us
    all_to_all x3, waiting for transfers between devices, work(): arrived = lax.all_to_all(encode(keep + got), 'z', 0, 0, tiled=True)  32.6 us
    ppermute x16, starting transfers between devices, send(): return lax.ppermute(x, AXES, moves(**by))  30.4 us
    pallas_call x4, Pallas kernels, product(): pl.pallas_call(body, out_shape=(out, out), grid_spec=pltpu.PrefetchScalar...  20.9 us
    all_to_all x3, starting transfers between devices, work(): arrived = lax.all_to_all(encode(keep + got), 'z', 0, 0, tiled=True)  18.8 us
    all_to_all x1, blocking collectives, pipeline(): lax.all_to_all(jnp.broadcast_to(sums[None], (16, 32, 128)), ('xh', 'y', '...  17.8 us
    all_to_all x1, blocking collectives, pipeline(): sums = jnp.sum(lax.all_to_all(sums, ('z', 'xl'), 0, 0), axis=0)  15.1 us
    all_to_all x1, waiting for transfers between devices, work(): arrived = lax.all_to_all(coded, ('z', 'xl'), 0, 0, tiled=True)  14.2 us
  transfers between devices with their start and end apart: 20, of which 10 were waited for; matrix products, arithmetic and copies ran while one was open for 9% of the time, Pallas kernels for 9%

profile of v3, /device:TPU:1, one launch (start us, length us, event | category | flops | bytes accessed | tf_op | source)
XLA Modules:
  0.0 238.7 jit_solution(1319435317608597175)
XLA Ops:
  0.0 2.2 collective-permute-start.2
  2.2 1.5 collective-permute-start.3
  3.8 2.7 %collective-permute-start.4 = (bf16[1536,512]{1,0:T(8,128)(2,1)}, bf16[1536,512]{1,0:T(8,128)(2,1)}, u32[]{:S(2)}, u32[]{:S(2)}) collective-permute-start(bf16[1536,512]{1,0:T(8,128)(2,1)} %refs_0_.1), channel_id=1, source_target_pairs={{0,128},{1,129},{2,130},{3,131},{4,132},{5,133},{6,134},{7,135},{8... | collective-permute-start | bytes 4718600 | tf_op jit(solution)/shard_map/ppermute | solution.py:42
  6.5 29.7 %collective-permute-done.2.refs_0_ = bf16[1536,512]{1,0:T(8,128)(2,1)S(1)} collective-permute-done((bf16[1536,512]{1,0:T(8,128)(2,1)}, bf16[1536,512]{1,0:T(8,128)(2,1)S(1)}, u32[]{:S(2)}, u32[]{:S(2)}) %collective-permute-start.2) | collective-permute-done | bytes 1572896 | tf_op jit(solution)/shard_map/ppermute | solution.py:42
  39.7 1.6 collective-permute-start.8
  42.5 3.4 %shard_map.91 = (f32[8,2,2,16,256]{4,3,2,1,0:T(8,128)}, f32[8,2,2,16,256]{4,3,2,1,0:T(8,128)}) custom-call(s32[10]{0:T(128)} %select_add_fusion.meta, s32[24]{0:T(128)} %reshape.82.index, s32[8]{0:T(128)} %bitcast.33, bf16[512,4096]{1,0:T(8,128)(2,1)} %w_hbm.7, bf16[1536,512]{1,0:T(8,128)(2,1)} %refs_0_.1), custom_call_target="tpu_custom_call" | custom-call | tf_op jit(solution)/shard_map/pallas_call | solution.py:131
  45.9 4.2 %collective-permute-start = (f32[8,2,2,16,256]{4,3,2,1,0:T(8,128)}, f32[8,2,2,16,256]{4,3,2,1,0:T(8,128)}, u32[]{:S(2)}, u32[]{:S(2)}) collective-permute-start(f32[8,2,2,16,256]{4,3,2,1,0:T(8,128)} %get-tuple-element.16), channel_id=1, source_target_pairs={{0,1},{1,0},{2,3},{3,2},{4,5},{5,4},{6,7},{7,6},{8,9},{9,8},{10,11... | collective-permute-start | bytes 1572872 | tf_op jit(solution)/shard_map/ppermute | solution.py:42
  50.1 2.7 %collective-permute-start.12 = (bf16[1536,512]{1,0:T(8,128)(2,1)}, bf16[1536,512]{1,0:T(8,128)(2,1)}, u32[]{:S(2)}, u32[]{:S(2)}) collective-permute-start(bf16[1536,512]{1,0:T(8,128)(2,1)} %collective-permute-done.4.refs_2_), channel_id=1, source_target_pairs={{0,96},{1,97},{2,98},{3,99},{4,100},{5,101},{6,102},{7,103},{8,104... | collective-permute-start | bytes 4718600 | tf_op jit(solution)/shard_map/ppermute | solution.py:42
  52.8 2.8 %collective-permute-done.7.refs_0_ = bf16[1536,256]{1,0:T(8,128)(2,1)} collective-permute-done((bf16[1536,256]{1,0:T(8,128)(2,1)}, bf16[1536,256]{1,0:T(8,128)(2,1)}, u32[]{:S(2)}, u32[]{:S(2)}) %collective-permute-start.7) | collective-permute-done | bytes 786464 | tf_op jit(solution)/shard_map/ppermute | solution.py:42
  55.6 1.7 collective-permute-done.8.refs_1_
  57.3 5.1 %shard_map.93 = (f32[8,2,2,16,256]{4,3,2,1,0:T(8,128)}, f32[8,2,2,16,256]{4,3,2,1,0:T(8,128)}) custom-call(s32[10]{0:T(128)} %select_add_fusion.meta, s32[24]{0:T(128)} %reshape.82.index, s32[8]{0:T(128)} %bitcast.34, bf16[512,4096]{1,0:T(8,128)(2,1)} %w_hbm.7, bf16[1536,256]{1,0:T(8,128)(2,1)} %collective-permute-done.7.refs_0_, ...), custom_call_target="tpu_custom_call" | custom-call | tf_op jit(solution)/shard_map/pallas_call | solution.py:131
  62.5 5.4 %collective-permute-start.9 = (f32[8,2,2,16,256]{4,3,2,1,0:T(8,128)}, f32[8,2,2,16,256]{4,3,2,1,0:T(8,128)S(1)}, u32[]{:S(2)}, u32[]{:S(2)}) collective-permute-start(f32[8,2,2,16,256]{4,3,2,1,0:T(8,128)} %get-tuple-element.20), channel_id=1, source_target_pairs={{0,1},{1,0},{2,3},{3,2},{4,5},{5,4},{6,7},{7,6},{8,9},{9,8},{10,11... | collective-permute-start | bytes 1572872 | tf_op jit(solution)/shard_map/ppermute | solution.py:42
  67.9 7.0 %shard_map.92 = (f32[8,2,6,16,256]{4,3,2,1,0:T(8,128)}, f32[8,2,6,16,256]{4,3,2,1,0:T(8,128)}) custom-call(s32[10]{0:T(128)} %select_add_fusion.meta, s32[24]{0:T(128)} %reshape.82.index, s32[8]{0:T(128)} %bitcast.35, bf16[512,4096]{1,0:T(8,128)(2,1)} %w_hbm.7, bf16[1536,512]{1,0:T(8,128)(2,1)} %copy-done, bf16[1536,512]{1,0:T(8,128)(2,1)} %copy-done.1, ...), custom_call_target="tpu_custom_call" | custom-call | tf_op jit(solution)/shard_map/pallas_call | solution.py:131
  76.2 1.8 collective-permute-start.13
  80.3 7.4 %all-to-all-start = ((f16[8,72,256]{2,1,0:T(8,128)(2,1)}), f16[8,72,256]{2,1,0:T(8,128)(2,1)S(1)}, u32[]{:S(2)}, u32[]{:S(2)}) async-start(f16[8,72,256]{2,1,0:T(8,128)(2,1)} %pad_maximum_fusion.2), calls=%async_computation | async-start | bytes 589824 | tf_op jit(solution)/shard_map/all_to_all | solution.py:242
  89.2 1.8 collective-permute-done.12.refs_1_
  91.0 5.7 %collective-permute-done.13.refs_2_ = bf16[1536,256]{1,0:T(8,128)(2,1)S(1)} collective-permute-done((bf16[1536,256]{1,0:T(8,128)(2,1)}, bf16[1536,256]{1,0:T(8,128)(2,1)S(1)}, u32[]{:S(2)}, u32[]{:S(2)}) %collective-permute-start.13) | collective-permute-done | bytes 786464 | tf_op jit(solution)/shard_map/ppermute | solution.py:42
  96.8 17.0 %collective-permute-done.14.refs_3_ = bf16[1536,256]{1,0:T(8,128)(2,1)} collective-permute-done((bf16[1536,256]{1,0:T(8,128)(2,1)}, bf16[1536,256]{1,0:T(8,128)(2,1)}, u32[]{:S(2)}, u32[]{:S(2)}) %collective-permute-start.14) | collective-permute-done | bytes 786464 | tf_op jit(solution)/shard_map/ppermute | solution.py:42
  113.7 5.4 %shard_map.94 = (f32[8,2,6,16,256]{4,3,2,1,0:T(8,128)}, f32[8,2,6,16,256]{4,3,2,1,0:T(8,128)}) custom-call(s32[10]{0:T(128)} %select_add_fusion.meta, s32[24]{0:T(128)} %reshape.82.index, s32[8]{0:T(128)} %bitcast.36, bf16[512,4096]{1,0:T(8,128)(2,1)} %w_hbm.7, bf16[1536,512]{1,0:T(8,128)(2,1)} %copy-done.2, ...), custom_call_target="tpu_custom_call" | custom-call | tf_op jit(solution)/shard_map/pallas_call | solution.py:131
  119.1 2.4 %collective-permute-start.15 = (f32[8,2,6,16,256]{4,3,2,1,0:T(8,128)}, f32[8,2,6,16,256]{4,3,2,1,0:T(8,128)}, u32[]{:S(2)}, u32[]{:S(2)}) collective-permute-start(f32[8,2,6,16,256]{4,3,2,1,0:T(8,128)} %get-tuple-element.22), channel_id=1, source_target_pairs={{0,1},{1,0},{2,3},{3,2},{4,5},{5,4},{6,7},{7,6},{8,9},{9,8},{10,11... | collective-permute-start | bytes 4718600 | tf_op jit(solution)/shard_map/ppermute | solution.py:42
  122.5 2.3 abs_reduce_fusion.1
  124.8 7.8 %all-to-all-start.2 = ((f16[8,72,256]{2,1,0:T(8,128)(2,1)}), f16[8,72,256]{2,1,0:T(8,128)(2,1)}, u32[]{:S(2)}, u32[]{:S(2)}) async-start(f16[8,72,256]{2,1,0:T(8,128)(2,1)} %pad_maximum_fusion.3), calls=%async_computation.2 | async-start | bytes 589824 | tf_op jit(solution)/shard_map/all_to_all | solution.py:242
  134.2 11.7 %all-to-all-done.2 = f16[8,72,256]{2,1,0:T(8,128)(2,1)} async-done(((f16[8,72,256]{2,1,0:T(8,128)(2,1)}), f16[8,72,256]{2,1,0:T(8,128)(2,1)}, u32[]{:S(2)}, u32[]{:S(2)}) %all-to-all-start.2) | async-done | bytes 294944 | tf_op jit(solution)/shard_map/all_to_all | solution.py:242
  145.8 3.5 %all-to-all-start.1 = ((f16[8,200,256]{2,1,0:T(8,128)(2,1)}), f16[8,200,256]{2,1,0:T(8,128)(2,1)S(1)}, u32[]{:S(2)}, u32[]{:S(2)}) async-start(f16[8,200,256]{2,1,0:T(8,128)(2,1)} %pad_maximum_fusion.1), calls=%async_computation.1 | async-start | bytes 1638400 | tf_op jit(solution)/shard_map/all_to_all | solution.py:242
  149.4 1.8 abs_reduce_fusion
  152.7 20.9 %all-to-all-done.1 = f16[8,200,256]{2,1,0:T(8,128)(2,1)S(1)} async-done(((f16[8,200,256]{2,1,0:T(8,128)(2,1)}), f16[8,200,256]{2,1,0:T(8,128)(2,1)S(1)}, u32[]{:S(2)}, u32[]{:S(2)}) %all-to-all-start.1) | async-done | bytes 819232 | tf_op jit(solution)/shard_map/all_to_all | solution.py:242
  173.6 3.6 %all-to-all-start.3 = ((f16[16,104,256]{2,1,0:T(8,128)(2,1)}), f16[16,104,256]{2,1,0:T(8,128)(2,1)S(1)}, u32[]{:S(2)}, u32[]{:S(2)}) async-start(f16[16,104,256]{2,1,0:T(8,128)(2,1)} %pad_maximum_fusion), calls=%async_computation.3 | async-start | bytes 1703936 | tf_op jit(solution)/shard_map/all_to_all | solution.py:239
  185.1 14.2 %all-to-all-done.3 = f16[16,104,256]{2,1,0:T(8,128)(2,1)S(1)} async-done(((f16[16,104,256]{2,1,0:T(8,128)(2,1)}), f16[16,104,256]{2,1,0:T(8,128)(2,1)S(1)}, u32[]{:S(2)}, u32[]{:S(2)}) %all-to-all-start.3) | async-done | bytes 852000 | tf_op jit(solution)/shard_map/all_to_all | solution.py:239
  201.4 2.6 %squares.1 = (f32[16,4096]{1,0:T(8,128)}, f32[16,32,128]{2,1,0:T(8,128)}) custom-call(s32[10]{0:T(128)} %select_add_fusion.meta, f32[2,16,256]{2,1,0:T(8,128)} %bitcast.28, f32[2,16,256]{2,1,0:T(8,128)} %copy-done.8, f32[6,16,256]{2,1,0:T(8,128)} %bitcast.26, f32[6,16,256]{2,1,0:T(8,128)} %copy-done.7, f32[2,16,256]{2,1,0:T(8,128)} %bitcast.29, ...), custom_call_target="tpu_custom_call" | custom-call | tf_op jit(solution)/shard_map/squares/pallas_call | solution.py:173
  204.0 15.1 %all_to_all.30 = f32[16,32,128]{2,1,0:T(8,128)S(1)} all-to-all(f32[16,32,128]{2,1,0:T(8,128)} %get-tuple-element.24), channel_id=1, replica_groups=mesh['xh'=2,'y'=4,'z'=8,'xl'=2,'core'=2] {'z','xl'}, dimensions={0} | all-to-all | bytes 524288 | tf_op jit(solution)/shard_map/all_to_all | solution.py:260
  219.2 17.8 %all_to_all.31.sum_ref = f32[16,32,128]{2,1,0:T(8,128)} all-to-all(f32[16,32,128]{2,1,0:T(8,128)S(1)} %broadcast_in_dim.14), channel_id=1, replica_groups=mesh['xh'=2,'y'=4,'z'=8,'xl'=2,'core'=2] {'xh','y','core'}, dimensions={0} | all-to-all | bytes 524288 | tf_op jit(solution)/shard_map/all_to_all | solution.py:261
  236.9 1.8 scaled.1
  (90 shorter events, 23.6 us)
Async XLA Ops:
  0.0 41.9 %copy-start.11 = (pred[10]{0:T(512)(128)(4,1)S(1)}, pred[10]{0:T(512)(128)(4,1)}, u32[]{:S(2)}) copy-start(pred[10]{0:T(512)(128)(4,1)} %constant.68.clone) | copy-start | bytes 34
  0.0 41.9 %copy-start.12 = (pred[10]{0:T(512)(128)(4,1)S(1)}, pred[10]{0:T(512)(128)(4,1)}, u32[]{:S(2)}) copy-start(pred[10]{0:T(512)(128)(4,1)} %constant.67.clone) | copy-start | bytes 34
  0.0 41.9 %copy-start.13 = (s32[10]{0:T(128)S(1)}, s32[10]{0:T(128)}, u32[]{:S(2)}) copy-start(s32[10]{0:T(128)} %constant.66.clone) | copy-start | bytes 124
  0.0 41.9 %copy-start.14 = (s32[10]{0:T(128)S(1)}, s32[10]{0:T(128)}, u32[]{:S(2)}) copy-start(s32[10]{0:T(128)} %constant.20.clone) | copy-start | bytes 124
  0.0 41.9 %copy-start.15 = (s32[10]{0:T(128)S(1)}, s32[10]{0:T(128)}, u32[]{:S(2)}) copy-start(s32[10]{0:T(128)} %constant.19.clone) | copy-start | bytes 124
  0.0 41.3 %copy-start.10 = (s32[3,8]{1,0:T(4,128)S(1)}, s32[3,8]{1,0:T(4,128)}, u32[]{:S(2)}) copy-start(s32[3,8]{1,0:T(4,128)} %param.11) | copy-start | bytes 292
  0.0 36.1 %collective-permute-start.2 = (bf16[1536,512]{1,0:T(8,128)(2,1)}, bf16[1536,512]{1,0:T(8,128)(2,1)S(1)}, u32[]{:S(2)}, u32[]{:S(2)}) collective-permute-start(bf16[1536,512]{1,0:T(8,128)(2,1)} %refs_0_.1), channel_id=1, source_target_pairs={{0,32},{1,33},{2,34},{3,35},{4,36},{5,37},{6,38},{7,39},{8,40},{9,... | collective-permute-start | bytes 4718600 | tf_op jit(solution)/shard_map/ppermute | solution.py:42
  2.2 36.5 %collective-permute-start.3 = (bf16[1536,512]{1,0:T(8,128)(2,1)}, bf16[1536,512]{1,0:T(8,128)(2,1)S(1)}, u32[]{:S(2)}, u32[]{:S(2)}) collective-permute-start(bf16[1536,512]{1,0:T(8,128)(2,1)} %refs_0_.1), channel_id=1, source_target_pairs={{0,96},{1,97},{2,98},{3,99},{4,100},{5,101},{6,102},{7,103},{8,104... | collective-permute-start | bytes 4718600 | tf_op jit(solution)/shard_map/ppermute | solution.py:42
  3.8 46.3 %collective-permute-start.4 = (bf16[1536,512]{1,0:T(8,128)(2,1)}, bf16[1536,512]{1,0:T(8,128)(2,1)}, u32[]{:S(2)}, u32[]{:S(2)}) collective-permute-start(bf16[1536,512]{1,0:T(8,128)(2,1)} %refs_0_.1), channel_id=1, source_target_pairs={{0,128},{1,129},{2,130},{3,131},{4,132},{5,133},{6,134},{7,135},{8... | collective-permute-start | bytes 4718600 | tf_op jit(solution)/shard_map/ppermute | solution.py:42
  37.2 18.4 %collective-permute-start.7 = (bf16[1536,256]{1,0:T(8,128)(2,1)}, bf16[1536,256]{1,0:T(8,128)(2,1)}, u32[]{:S(2)}, u32[]{:S(2)}) collective-permute-start(bf16[1536,256]{1,0:T(8,128)(2,1)} %slice.78), channel_id=1, source_target_pairs={{0,32},{1,33},{2,34},{3,35},{4,36},{5,37},{6,38},{7,39},{8,40},{9,... | collective-permute-start | bytes 2359304 | tf_op jit(solution)/shard_map/ppermute | solution.py:42
  38.7 7.2 %copy-start.1 = (bf16[1536,512]{1,0:T(8,128)(2,1)}, bf16[1536,512]{1,0:T(8,128)(2,1)S(1)}, u32[]{:S(2)}) copy-start(bf16[1536,512]{1,0:T(8,128)(2,1)S(1)} %collective-permute-done.3.refs_1_) | copy-start | bytes 4718596
  39.7 17.6 %collective-permute-start.8 = (bf16[1536,256]{1,0:T(8,128)(2,1)}, bf16[1536,256]{1,0:T(8,128)(2,1)}, u32[]{:S(2)}, u32[]{:S(2)}) collective-permute-start(bf16[1536,256]{1,0:T(8,128)(2,1)} %slice.79), channel_id=1, source_target_pairs={{0,96},{1,97},{2,98},{3,99},{4,100},{5,101},{6,102},{7,103},{8,104... | collective-permute-start | bytes 2359304 | tf_op jit(solution)/shard_map/ppermute | solution.py:42
  45.9 29.1 %collective-permute-start = (f32[8,2,2,16,256]{4,3,2,1,0:T(8,128)}, f32[8,2,2,16,256]{4,3,2,1,0:T(8,128)}, u32[]{:S(2)}, u32[]{:S(2)}) collective-permute-start(f32[8,2,2,16,256]{4,3,2,1,0:T(8,128)} %get-tuple-element.16), channel_id=1, source_target_pairs={{0,1},{1,0},{2,3},{3,2},{4,5},{5,4},{6,7},{7,6},{8,9},{9,8},{10,11... | collective-permute-start | bytes 1572872 | tf_op jit(solution)/shard_map/ppermute | solution.py:42
  50.1 39.1 %collective-permute-start.11 = (bf16[1536,512]{1,0:T(8,128)(2,1)}, bf16[1536,512]{1,0:T(8,128)(2,1)S(1)}, u32[]{:S(2)}, u32[]{:S(2)}) collective-permute-start(bf16[1536,512]{1,0:T(8,128)(2,1)} %collective-permute-done.4.refs_2_), channel_id=1, source_target_pairs={{0,32},{1,33},{2,34},{3,35},{4,36},{5,37},{6,38},{7,39},{8,40},{9,... | collective-permute-start | bytes 4718600 | tf_op jit(solution)/shard_map/ppermute | solution.py:42
  50.1 40.9 %collective-permute-start.12 = (bf16[1536,512]{1,0:T(8,128)(2,1)}, bf16[1536,512]{1,0:T(8,128)(2,1)}, u32[]{:S(2)}, u32[]{:S(2)}) collective-permute-start(bf16[1536,512]{1,0:T(8,128)(2,1)} %collective-permute-done.4.refs_2_), channel_id=1, source_target_pairs={{0,96},{1,97},{2,98},{3,99},{4,100},{5,101},{6,102},{7,103},{8,104... | collective-permute-start | bytes 4718600 | tf_op jit(solution)/shard_map/ppermute | solution.py:42
  62.4 12.6 %copy-start.6 = (f32[8,2,2,16,256]{4,3,2,1,0:T(8,128)S(1)}, f32[8,2,2,16,256]{4,3,2,1,0:T(8,128)}, u32[]{:S(2)}) copy-start(f32[8,2,2,16,256]{4,3,2,1,0:T(8,128)} %get-tuple-element.15) | copy-start | bytes 1572868
  62.5 15.5 %collective-permute-start.9 = (f32[8,2,2,16,256]{4,3,2,1,0:T(8,128)}, f32[8,2,2,16,256]{4,3,2,1,0:T(8,128)S(1)}, u32[]{:S(2)}, u32[]{:S(2)}) collective-permute-start(f32[8,2,2,16,256]{4,3,2,1,0:T(8,128)} %get-tuple-element.20), channel_id=1, source_target_pairs={{0,1},{1,0},{2,3},{3,2},{4,5},{5,4},{6,7},{7,6},{8,9},{9,8},{10,11... | collective-permute-start | bytes 1572872 | tf_op jit(solution)/shard_map/ppermute | solution.py:42
  74.9 47.6 %collective-permute-start.5 = (f32[8,2,6,16,256]{4,3,2,1,0:T(8,128)}, f32[8,2,6,16,256]{4,3,2,1,0:T(8,128)}, u32[]{:S(2)}, u32[]{:S(2)}) collective-permute-start(f32[8,2,6,16,256]{4,3,2,1,0:T(8,128)} %get-tuple-element.18), channel_id=1, source_target_pairs={{0,1},{1,0},{2,3},{3,2},{4,5},{5,4},{6,7},{7,6},{8,9},{9,8},{10,11... | collective-permute-start | bytes 4718600 | tf_op jit(solution)/shard_map/ppermute | solution.py:42
  76.2 20.6 %collective-permute-start.13 = (bf16[1536,256]{1,0:T(8,128)(2,1)}, bf16[1536,256]{1,0:T(8,128)(2,1)S(1)}, u32[]{:S(2)}, u32[]{:S(2)}) collective-permute-start(bf16[1536,256]{1,0:T(8,128)(2,1)} %collective-permute-done.7.refs_0_), channel_id=1, source_target_pairs={{0,128},{1,129},{2,130},{3,131},{4,132},{5,133},{6,134},{7,135},{8... | collective-permute-start | bytes 2359304 | tf_op jit(solution)/shard_map/ppermute | solution.py:42
  77.9 9.8 %copy-start.5 = (f32[8,2,2,16,256]{4,3,2,1,0:T(8,128)}, f32[8,2,2,16,256]{4,3,2,1,0:T(8,128)S(1)}, u32[]{:S(2)}) copy-start(f32[8,2,2,16,256]{4,3,2,1,0:T(8,128)S(1)} %collective-permute-done.9) | copy-start | bytes 1572868
  77.9 35.8 %collective-permute-start.14 = (bf16[1536,256]{1,0:T(8,128)(2,1)}, bf16[1536,256]{1,0:T(8,128)(2,1)}, u32[]{:S(2)}, u32[]{:S(2)}) collective-permute-start(bf16[1536,256]{1,0:T(8,128)(2,1)} %collective-permute-done.8.refs_1_), channel_id=1, source_target_pairs={{0,128},{1,129},{2,130},{3,131},{4,132},{5,133},{6,134},{7,135},{8... | collective-permute-start | bytes 2359304 | tf_op jit(solution)/shard_map/ppermute | solution.py:42
  80.3 44.5 %all-to-all-start = ((f16[8,72,256]{2,1,0:T(8,128)(2,1)}), f16[8,72,256]{2,1,0:T(8,128)(2,1)S(1)}, u32[]{:S(2)}, u32[]{:S(2)}) async-start(f16[8,72,256]{2,1,0:T(8,128)(2,1)} %pad_maximum_fusion.2), calls=%async_computation | async-start | bytes 589824 | tf_op jit(solution)/shard_map/all_to_all | solution.py:242
  89.2 24.5 %copy-start.2 = (bf16[1536,512]{1,0:T(8,128)(2,1)}, bf16[1536,512]{1,0:T(8,128)(2,1)S(1)}, u32[]{:S(2)}) copy-start(bf16[1536,512]{1,0:T(8,128)(2,1)S(1)} %collective-permute-done.11.refs_0_) | copy-start | bytes 4718596
  96.8 17.0 %copy-start.4 = (bf16[1536,256]{1,0:T(8,128)(2,1)}, bf16[1536,256]{1,0:T(8,128)(2,1)S(1)}, u32[]{:S(2)}) copy-start(bf16[1536,256]{1,0:T(8,128)(2,1)S(1)} %collective-permute-done.13.refs_2_) | copy-start | bytes 2359300
  119.1 30.2 %collective-permute-start.15 = (f32[8,2,6,16,256]{4,3,2,1,0:T(8,128)}, f32[8,2,6,16,256]{4,3,2,1,0:T(8,128)}, u32[]{:S(2)}, u32[]{:S(2)}) collective-permute-start(f32[8,2,6,16,256]{4,3,2,1,0:T(8,128)} %get-tuple-element.22), channel_id=1, source_target_pairs={{0,1},{1,0},{2,3},{3,2},{4,5},{5,4},{6,7},{7,6},{8,9},{9,8},{10,11... | collective-permute-start | bytes 4718600 | tf_op jit(solution)/shard_map/ppermute | solution.py:42
  124.8 21.0 %all-to-all-start.2 = ((f16[8,72,256]{2,1,0:T(8,128)(2,1)}), f16[8,72,256]{2,1,0:T(8,128)(2,1)}, u32[]{:S(2)}, u32[]{:S(2)}) async-start(f16[8,72,256]{2,1,0:T(8,128)(2,1)} %pad_maximum_fusion.3), calls=%async_computation.2 | async-start | bytes 589824 | tf_op jit(solution)/shard_map/all_to_all | solution.py:242
  133.0 16.4 %copy-start.3 = (f32[8,2,6,16,256]{4,3,2,1,0:T(8,128)S(1)}, f32[8,2,6,16,256]{4,3,2,1,0:T(8,128)}, u32[]{:S(2)}) copy-start(f32[8,2,6,16,256]{4,3,2,1,0:T(8,128)} %get-tuple-element.21) | copy-start | bytes 4718596
  145.8 27.8 %all-to-all-start.1 = ((f16[8,200,256]{2,1,0:T(8,128)(2,1)}), f16[8,200,256]{2,1,0:T(8,128)(2,1)S(1)}, u32[]{:S(2)}, u32[]{:S(2)}) async-start(f16[8,200,256]{2,1,0:T(8,128)(2,1)} %pad_maximum_fusion.1), calls=%async_computation.1 | async-start | bytes 1638400 | tf_op jit(solution)/shard_map/all_to_all | solution.py:242
  173.6 25.7 %all-to-all-start.3 = ((f16[16,104,256]{2,1,0:T(8,128)(2,1)}), f16[16,104,256]{2,1,0:T(8,128)(2,1)S(1)}, u32[]{:S(2)}, u32[]{:S(2)}) async-start(f16[16,104,256]{2,1,0:T(8,128)(2,1)} %pad_maximum_fusion), calls=%async_computation.3 | async-start | bytes 1703936 | tf_op jit(solution)/shard_map/all_to_all | solution.py:239
  178.1 22.6 %collective-permute-start.1 = (f32[2,16,256]{2,1,0:T(8,128)S(1)}, f32[2,16,256]{2,1,0:T(8,128)S(1)}, u32[]{:S(2)}, u32[]{:S(2)}) collective-permute-start(f32[2,16,256]{2,1,0:T(8,128)S(1)} %bitcast.31), channel_id=1, source_target_pairs={{0,2},{1,3},{2,0},{3,1},{4,6},{5,7},{6,4},{7,5},{8,10},{9,11},{10,... | collective-permute-start | bytes 98312 | tf_op jit(solution)/shard_map/ppermute | solution.py:42
  182.1 18.7 %collective-permute-start.10 = (f32[2,16,256]{2,1,0:T(8,128)S(1)}, f32[2,16,256]{2,1,0:T(8,128)S(1)}, u32[]{:S(2)}, u32[]{:S(2)}) collective-permute-start(f32[2,16,256]{2,1,0:T(8,128)S(1)} %bitcast.32), channel_id=1, source_target_pairs={{0,2},{1,3},{2,0},{3,1},{4,6},{5,7},{6,4},{7,5},{8,10},{9,11},{10,... | collective-permute-start | bytes 98312 | tf_op jit(solution)/shard_map/ppermute | solution.py:42
  183.7 17.1 %collective-permute-start.6 = (f32[6,16,256]{2,1,0:T(8,128)S(1)}, f32[6,16,256]{2,1,0:T(8,128)S(1)}, u32[]{:S(2)}, u32[]{:S(2)}) collective-permute-start(f32[6,16,256]{2,1,0:T(8,128)S(1)} %bitcast.30), channel_id=1, source_target_pairs={{0,2},{1,3},{2,0},{3,1},{4,6},{5,7},{6,4},{7,5},{8,10},{9,11},{10,... | collective-permute-start | bytes 294920 | tf_op jit(solution)/shard_map/ppermute | solution.py:42
  (4 other events, 5.4 us)

commit v4 on v3

--- a/solution.py
+++ b/solution.py
@@ -21,10 +21,11 @@
 SCALE = 64.0
 
 BATCHES = (
-    ((0, 0, (0, 1)),),
-    ((0, 3, (0, 1)), (0, 1, (0, 1)), (1, 0, (0, 1))),
+    ((0, 0, (0, 1)), (0, 3, (0,)), (0, 1, (0,))),
+    ((0, 3, (1,)), (0, 1, (1,)), (1, 0, (0, 1))),
     ((0, 2, (0, 1)),),
-    ((1, 3, (0, 1)), (1, 1, (0, 1)), (1, 2, (0, 1))),
+    ((1, 3, (0,)), (1, 1, (0,)), (1, 2, (0,))),
+    ((1, 3, (1,)), (1, 1, (1,)), (1, 2, (1,))),
 )
 PANELS = tuple(itertools.chain(*BATCHES))
 CORE, XLO = len(PANELS), len(PANELS) + 1
@@ -228,6 +229,9 @@
     def pair(left, right):
         return [(left, 0, HALF), (right, 0, HALF)]
 
+    def one(array):
+        return [(array, 0, HALF)]
+
     ends = []
 
     def work(batch, given, both=False):
@@ -243,18 +247,20 @@
             total = decode(arrived, (2, n, 16, HALF))
             ends.append((total[0], move(total[1], dxl=1)))
 
-    up = move(values, dy=1)
-    down = move(values, dy=3)
-    over = move(values, dxh=1)
-    far = [move(up[:, :HALF], dy=1), move(down[:, HALF:], dy=3)]
-    over_up = move(over, dy=1)
-    over_down = move(over, dy=3)
+    own = (values[:, :HALF], values[:, HALF:])
+    up = [move(own[t], dy=1) for t in range(2)]
+    down = [move(own[t], dy=3) for t in range(2)]
+    over = [move(own[t], dxh=1) for t in range(2)]
+    far = [move(up[0], dy=1), move(down[1], dy=3)]
+    over_up = [move(over[t], dy=1) for t in range(2)]
+    over_down = [move(over[t], dy=3) for t in range(2)]
     over_far = [move(far[t], dxh=1) for t in range(2)]
 
-    work(0, [whole(values)])
-    work(1, [whole(up), whole(down), whole(over)])
+    work(0, [whole(values), one(up[0]), one(down[0])])
+    work(1, [one(up[1]), one(down[1]), pair(*over)])
     work(2, [pair(*far)])
-    work(3, [whole(over_up), whole(over_down), pair(*over_far)], both=True)
+    work(3, [one(over_up[0]), one(over_down[0]), one(over_far[0])])
+    work(4, [one(over_up[1]), one(over_down[1]), one(over_far[1])], both=True)
 
     squared, sums = squares(meta, ends)
     sums = jnp.sum(lax.all_to_all(sums, ("z", "xl"), 0, 0), axis=0)

time: 240 us -> 221 us (0.921)
  waiting for transfers between devices: 106 us -> 69.4 us
  starting transfers between devices: 52.9 us -> 68.9 us
  Pallas kernels: 25.3 us -> 29.6 us
  other arithmetic: 16.3 us -> 12 us
  local copies, waits for them, and re-layouts: 5.29 us -> 8.85 us
    ppermute x16 -> x23, waiting for transfers between devices: 58.9 us -> 20.2 us  [send(): return lax.ppermute(x, AXES, moves(**by))]
    ppermute x16 -> x23, starting transfers between devices: 30.4 us -> 42.5 us  [send(): return lax.ppermute(x, AXES, moves(**by))]
    all_to_all x3 -> x4, waiting for transfers between devices: 32.6 us -> 38.1 us  [work(): arrived = lax.all_to_all(encode(keep + got), 'z', 0, 0, tiled=True)]
    pallas_call x4 -> x5, Pallas kernels: 20.9 us -> 25.3 us  [product(): pl.pallas_call(body, out_shape=(out, out), grid_spec=pltpu.PrefetchScalar...]
    all_to_all x3 -> x4, starting transfers between devices: 18.8 us -> 22.8 us  [work(): arrived = lax.all_to_all(encode(keep + got), 'z', 0, 0, tiled=True)]
    all_to_all x1, waiting for transfers between devices: 14.2 us -> 11.1 us  [work(): arrived = lax.all_to_all(coded, ('z', 'xl'), 0, 0, tiled=True)]
    reduce_max x4 -> x5, other arithmetic: 6.47 us -> 3.38 us  [encode(): top = jnp.max(jnp.abs(total), axis=(*range(total.ndim - 3), total.ndim - 2))]
    unnamed x32 -> x36, local copies, waits for them, and re-layouts: 0.71 us -> 3.27 us
  transfers between devices with their start and end apart: 20 -> 28, of which waited for: 10 -> 9; matrix products, arithmetic and copies ran while one was open for 9% -> 7% of each run, Pallas kernels for 9% -> 11%
where the time goes in v4:
time: 221 us; the launch traced here: 220 us
  waiting for transfers between devices  69.4 us (31%)
  starting transfers between devices  68.9 us (31%)
  blocking collectives  31.2 us (14%)
  Pallas kernels  29.6 us (13%)
  other arithmetic  12 us (5%)
  local copies, waits for them, and re-layouts  8.85 us (4%)
    ppermute x23, starting transfers between devices, send(): return lax.ppermute(x, AXES, moves(**by))  42.5 us
    all_to_all x4, waiting for transfers between devices, work(): arrived = lax.all_to_all(encode(keep + got), 'z', 0, 0, tiled=True)  38.1 us
    pallas_call x5, Pallas kernels, product(): pl.pallas_call(body, out_shape=(out, out), grid_spec=pltpu.PrefetchScalar...  25.3 us
    all_to_all x4, starting transfers between devices, work(): arrived = lax.all_to_all(encode(keep + got), 'z', 0, 0, tiled=True)  22.8 us
    ppermute x23, waiting for transfers between devices, send(): return lax.ppermute(x, AXES, moves(**by))  20.2 us
    all_to_all x1, blocking collectives, pipeline(): lax.all_to_all(jnp.broadcast_to(sums[None], (16, 32, 128)), ('xh', 'y', '...  17.3 us
    all_to_all x1, blocking collectives, pipeline(): sums = jnp.sum(lax.all_to_all(sums, ('z', 'xl'), 0, 0), axis=0)  13.9 us
    all_to_all x1, waiting for transfers between devices, work(): arrived = lax.all_to_all(coded, ('z', 'xl'), 0, 0, tiled=True)  11.1 us
  transfers between devices with their start and end apart: 28, of which 9 were waited for; matrix products, arithmetic and copies ran while one was open for 7% of the time, Pallas kernels for 11%

profile of v4, /device:TPU:1, one launch (start us, length us, event | category | flops | bytes accessed | tf_op | source)
XLA Modules:
  0.0 220.3 jit_solution(7657930327309604691)
XLA Ops:
  0.0 2.4 %fusion.39 = (bf16[1536,256]{1,0:T(8,128)(2,1)S(1)}, bf16[1536,256]{1,0:T(8,128)(2,1)}) fusion(bf16[1536,512]{1,0:T(8,128)(2,1)} %refs_0_.1), kind=kLoop, calls=%fused_computation.81 | loop fusion | bytes 3145728 | tf_op jit(solution)/shard_map/slice | solution.py:250
  2.5 2.1 collective-permute-start
  6.0 2.7 %collective-permute-start.5 = (bf16[1536,256]{1,0:T(8,128)(2,1)S(1)}, bf16[1536,256]{1,0:T(8,128)(2,1)}, u32[]{:S(2)}, u32[]{:S(2)}) collective-permute-start(bf16[1536,256]{1,0:T(8,128)(2,1)S(1)} %get-tuple-element.39), channel_id=1, source_target_pairs={{0,96},{1,97},{2,98},{3,99},{4,100},{5,101},{6,102},{7,103},{8,104... | collective-permute-start | bytes 2359304 | tf_op jit(solution)/shard_map/ppermute | solution.py:43
  8.7 2.7 %collective-permute-start.6 = (bf16[1536,256]{1,0:T(8,128)(2,1)}, bf16[1536,256]{1,0:T(8,128)(2,1)}, u32[]{:S(2)}, u32[]{:S(2)}) collective-permute-start(bf16[1536,256]{1,0:T(8,128)(2,1)} %get-tuple-element.40), channel_id=1, source_target_pairs={{0,128},{1,129},{2,130},{3,131},{4,132},{5,133},{6,134},{7,135},{8... | collective-permute-start | bytes 2359304 | tf_op jit(solution)/shard_map/ppermute | solution.py:43
  11.4 10.2 %collective-permute-done.refs_1_ = bf16[1536,256]{1,0:T(8,128)(2,1)} collective-permute-done((bf16[1536,256]{1,0:T(8,128)(2,1)}, bf16[1536,256]{1,0:T(8,128)(2,1)}, u32[]{:S(2)}, u32[]{:S(2)}) %collective-permute-start) | collective-permute-done | bytes 786464 | tf_op jit(solution)/shard_map/ppermute | solution.py:43
  21.7 4.4 %collective-permute-start.7 = (bf16[1536,256]{1,0:T(8,128)(2,1)S(1)}, bf16[1536,256]{1,0:T(8,128)(2,1)}, u32[]{:S(2)}, u32[]{:S(2)}) collective-permute-start(bf16[1536,256]{1,0:T(8,128)(2,1)S(1)} %get-tuple-element.39), channel_id=1, source_target_pairs={{0,128},{1,129},{2,130},{3,131},{4,132},{5,133},{6,134},{7,135},{8... | collective-permute-start | bytes 2359304 | tf_op jit(solution)/shard_map/ppermute | solution.py:43
  28.1 5.2 %shard_map.91 = (f32[8,2,4,16,256]{4,3,2,1,0:T(8,128)}, f32[8,2,4,16,256]{4,3,2,1,0:T(8,128)}) custom-call(s32[15]{0:T(128)} %select_add_fusion.meta, s32[24]{0:T(128)} %reshape.101.index, s32[8]{0:T(128)} %bitcast.41, bf16[512,4096]{1,0:T(8,128)(2,1)} %w_hbm.9, bf16[1536,512]{1,0:T(8,128)(2,1)} %refs_0_.1, bf16[1536,256]{1,0:T(8,128)(2,1)} %collective-permute-done.refs_1_, ...), custom_call_target="tpu_custom_call" | custom-call | tf_op jit(solution)/shard_map/pallas_call | solution.py:132
  33.3 3.2 %collective-permute-start.2 = (f32[8,2,4,16,256]{4,3,2,1,0:T(8,128)}, f32[8,2,4,16,256]{4,3,2,1,0:T(8,128)S(1)}, u32[]{:S(2)}, u32[]{:S(2)}) collective-permute-start(f32[8,2,4,16,256]{4,3,2,1,0:T(8,128)} %get-tuple-element.18), channel_id=1, source_target_pairs={{0,1},{1,0},{2,3},{3,2},{4,5},{5,4},{6,7},{7,6},{8,9},{9,8},{10,11... | collective-permute-start | bytes 3145736 | tf_op jit(solution)/shard_map/ppermute | solution.py:43
  36.5 2.0 collective-permute-done.4.refs_0_
  40.1 2.5 %collective-permute-start.11 = (bf16[1536,256]{1,0:T(8,128)(2,1)}, bf16[1536,256]{1,0:T(8,128)(2,1)S(1)}, u32[]{:S(2)}, u32[]{:S(2)}) collective-permute-start(bf16[1536,256]{1,0:T(8,128)(2,1)} %collective-permute-done.5.refs_1_), channel_id=1, source_target_pairs={{0,96},{1,97},{2,98},{3,99},{4,100},{5,101},{6,102},{7,103},{8,104... | collective-permute-start | bytes 2359304 | tf_op jit(solution)/shard_map/ppermute | solution.py:43
  44.3 6.6 %shard_map.92 = (f32[8,2,4,16,256]{4,3,2,1,0:T(8,128)}, f32[8,2,4,16,256]{4,3,2,1,0:T(8,128)}) custom-call(s32[15]{0:T(128)} %select_add_fusion.meta, s32[24]{0:T(128)} %reshape.101.index, s32[8]{0:T(128)} %bitcast.42, bf16[512,4096]{1,0:T(8,128)(2,1)} %w_hbm.9, bf16[1536,256]{1,0:T(8,128)(2,1)} %copy-done.5, ...), custom_call_target="tpu_custom_call" | custom-call | tf_op jit(solution)/shard_map/pallas_call | solution.py:132
  53.7 3.3 %collective-permute-done.10.refs_0_ = bf16[1536,256]{1,0:T(8,128)(2,1)} collective-permute-done((bf16[1536,256]{1,0:T(8,128)(2,1)}, bf16[1536,256]{1,0:T(8,128)(2,1)}, u32[]{:S(2)}, u32[]{:S(2)}) %collective-permute-start.10) | collective-permute-done | bytes 786464 | tf_op jit(solution)/shard_map/ppermute | solution.py:43
  56.9 2.7 %collective-permute-start.15 = (bf16[1536,256]{1,0:T(8,128)(2,1)}, bf16[1536,256]{1,0:T(8,128)(2,1)}, u32[]{:S(2)}, u32[]{:S(2)}) collective-permute-start(bf16[1536,256]{1,0:T(8,128)(2,1)} %collective-permute-done.6.refs_2_), channel_id=1, source_target_pairs={{0,96},{1,97},{2,98},{3,99},{4,100},{5,101},{6,102},{7,103},{8,104... | collective-permute-start | bytes 2359304 | tf_op jit(solution)/shard_map/ppermute | solution.py:43
  60.5 5.0 %shard_map.93 = (f32[8,2,2,16,256]{4,3,2,1,0:T(8,128)}, f32[8,2,2,16,256]{4,3,2,1,0:T(8,128)}) custom-call(s32[15]{0:T(128)} %select_add_fusion.meta, s32[24]{0:T(128)} %reshape.101.index, s32[8]{0:T(128)} %bitcast.43, bf16[512,4096]{1,0:T(8,128)(2,1)} %w_hbm.9, bf16[1536,256]{1,0:T(8,128)(2,1)} %collective-permute-done.10.refs_0_, bf16[1536,256]{1,0:T(8,128)(2,1)} %copy-done.2), custom_call_target="tpu_custom_call" | custom-call | tf_op jit(solution)/shard_map/pallas_call | solution.py:132
  65.5 5.1 %collective-permute-start.12 = (f32[8,2,2,16,256]{4,3,2,1,0:T(8,128)}, f32[8,2,2,16,256]{4,3,2,1,0:T(8,128)S(1)}, u32[]{:S(2)}, u32[]{:S(2)}) collective-permute-start(f32[8,2,2,16,256]{4,3,2,1,0:T(8,128)} %get-tuple-element.22), channel_id=1, source_target_pairs={{0,1},{1,0},{2,3},{3,2},{4,5},{5,4},{6,7},{7,6},{8,9},{9,8},{10,11... | collective-permute-start | bytes 1572872 | tf_op jit(solution)/shard_map/ppermute | solution.py:43
  73.3 3.4 %collective-permute-start.16 = (bf16[1536,256]{1,0:T(8,128)(2,1)}, bf16[1536,256]{1,0:T(8,128)(2,1)}, u32[]{:S(2)}, u32[]{:S(2)}) collective-permute-start(bf16[1536,256]{1,0:T(8,128)(2,1)} %collective-permute-done.10.refs_0_), channel_id=1, source_target_pairs={{0,128},{1,129},{2,130},{3,131},{4,132},{5,133},{6,134},{7,135},{8... | collective-permute-start | bytes 2359304 | tf_op jit(solution)/shard_map/ppermute | solution.py:43
  77.7 7.7 %all-to-all-start.2 = ((f16[8,72,256]{2,1,0:T(8,128)(2,1)}), f16[8,72,256]{2,1,0:T(8,128)(2,1)S(1)}, u32[]{:S(2)}, u32[]{:S(2)}) async-start(f16[8,72,256]{2,1,0:T(8,128)(2,1)} %pad_maximum_fusion.4), calls=%async_computation.2 | async-start | bytes 589824 | tf_op jit(solution)/shard_map/all_to_all | solution.py:246
  86.9 9.9 %all-to-all-done.2 = f16[8,72,256]{2,1,0:T(8,128)(2,1)S(1)} async-done(((f16[8,72,256]{2,1,0:T(8,128)(2,1)}), f16[8,72,256]{2,1,0:T(8,128)(2,1)S(1)}, u32[]{:S(2)}, u32[]{:S(2)}) %all-to-all-start.2) | async-done | bytes 294944 | tf_op jit(solution)/shard_map/all_to_all | solution.py:246
  96.8 3.5 %all-to-all-start = ((f16[8,136,256]{2,1,0:T(8,128)(2,1)}), f16[8,136,256]{2,1,0:T(8,128)(2,1)S(1)}, u32[]{:S(2)}, u32[]{:S(2)}) async-start(f16[8,136,256]{2,1,0:T(8,128)(2,1)} %pad_maximum_fusion), calls=%async_computation | async-start | bytes 1114112 | tf_op jit(solution)/shard_map/all_to_all | solution.py:246
  101.6 4.1 %shard_map.94 = (f32[8,2,3,16,256]{4,3,2,1,0:T(8,128)}, f32[8,2,3,16,256]{4,3,2,1,0:T(8,128)}) custom-call(s32[15]{0:T(128)} %select_add_fusion.meta, s32[24]{0:T(128)} %reshape.101.index, s32[8]{0:T(128)} %bitcast.44, bf16[512,4096]{1,0:T(8,128)(2,1)} %w_hbm.9, bf16[1536,256]{1,0:T(8,128)(2,1)} %collective-permute-done.14.refs_0_, ...), custom_call_target="tpu_custom_call" | custom-call | tf_op jit(solution)/shard_map/pallas_call | solution.py:132
  105.7 2.8 %collective-permute-start.17 = (f32[8,2,3,16,256]{4,3,2,1,0:T(8,128)}, f32[8,2,3,16,256]{4,3,2,1,0:T(8,128)}, u32[]{:S(2)}, u32[]{:S(2)}) collective-permute-start(f32[8,2,3,16,256]{4,3,2,1,0:T(8,128)} %get-tuple-element.24), channel_id=1, source_target_pairs={{0,1},{1,0},{2,3},{3,2},{4,5},{5,4},{6,7},{7,6},{8,9},{9,8},{10,11... | collective-permute-start | bytes 2359304 | tf_op jit(solution)/shard_map/ppermute | solution.py:43
  108.6 2.9 %collective-permute-done.21.refs_2_ = bf16[1536,256]{1,0:T(8,128)(2,1)} collective-permute-done((bf16[1536,256]{1,0:T(8,128)(2,1)S(1)}, bf16[1536,256]{1,0:T(8,128)(2,1)}, u32[]{:S(2)}, u32[]{:S(2)}) %collective-permute-start.21) | collective-permute-done | bytes 786464 | tf_op jit(solution)/shard_map/ppermute | solution.py:43
  111.5 4.4 %shard_map.95 = (f32[8,2,3,16,256]{4,3,2,1,0:T(8,128)}, f32[8,2,3,16,256]{4,3,2,1,0:T(8,128)}) custom-call(s32[15]{0:T(128)} %select_add_fusion.meta, s32[24]{0:T(128)} %reshape.101.index, s32[8]{0:T(128)} %bitcast.45, bf16[512,4096]{1,0:T(8,128)(2,1)} %w_hbm.9, bf16[1536,256]{1,0:T(8,128)(2,1)} %collective-permute-done.19.refs_0_, ...), custom_call_target="tpu_custom_call" | custom-call | tf_op jit(solution)/shard_map/pallas_call | solution.py:132
  118.7 8.1 %all-to-all-start.1 = ((f16[8,136,256]{2,1,0:T(8,128)(2,1)}), f16[8,136,256]{2,1,0:T(8,128)(2,1)S(1)}, u32[]{:S(2)}, u32[]{:S(2)}) async-start(f16[8,136,256]{2,1,0:T(8,128)(2,1)} %pad_maximum_fusion.1), calls=%async_computation.1 | async-start | bytes 1114112 | tf_op jit(solution)/shard_map/all_to_all | solution.py:246
  131.9 13.6 %all-to-all-done.1 = f16[8,136,256]{2,1,0:T(8,128)(2,1)S(1)} async-done(((f16[8,136,256]{2,1,0:T(8,128)(2,1)}), f16[8,136,256]{2,1,0:T(8,128)(2,1)S(1)}, u32[]{:S(2)}, u32[]{:S(2)}) %all-to-all-start.1) | async-done | bytes 557088 | tf_op jit(solution)/shard_map/all_to_all | solution.py:246
  145.5 3.5 %all-to-all-start.3 = ((f16[8,104,256]{2,1,0:T(8,128)(2,1)}), f16[8,104,256]{2,1,0:T(8,128)(2,1)S(1)}, u32[]{:S(2)}, u32[]{:S(2)}) async-start(f16[8,104,256]{2,1,0:T(8,128)(2,1)} %pad_maximum_fusion.3), calls=%async_computation.3 | async-start | bytes 851968 | tf_op jit(solution)/shard_map/all_to_all | solution.py:246
  150.2 14.5 %all-to-all-done.3 = f16[8,104,256]{2,1,0:T(8,128)(2,1)S(1)} async-done(((f16[8,104,256]{2,1,0:T(8,128)(2,1)}), f16[8,104,256]{2,1,0:T(8,128)(2,1)S(1)}, u32[]{:S(2)}, u32[]{:S(2)}) %all-to-all-start.3) | async-done | bytes 426016 | tf_op jit(solution)/shard_map/all_to_all | solution.py:246
  164.7 3.6 %all-to-all-start.4 = ((f16[16,56,256]{2,1,0:T(8,128)(2,1)}), f16[16,56,256]{2,1,0:T(8,128)(2,1)S(1)}, u32[]{:S(2)}, u32[]{:S(2)}) async-start(f16[16,56,256]{2,1,0:T(8,128)(2,1)} %pad_maximum_fusion.2), calls=%async_computation.4 | async-start | bytes 917504 | tf_op jit(solution)/shard_map/all_to_all | solution.py:243
  171.9 11.1 %all-to-all-done.4 = f16[16,56,256]{2,1,0:T(8,128)(2,1)S(1)} async-done(((f16[16,56,256]{2,1,0:T(8,128)(2,1)}), f16[16,56,256]{2,1,0:T(8,128)(2,1)S(1)}, u32[]{:S(2)}, u32[]{:S(2)}) %all-to-all-start.4) | async-done | bytes 458784 | tf_op jit(solution)/shard_map/all_to_all | solution.py:243
  184.8 2.5 %squares.1 = (f32[16,4096]{1,0:T(8,128)}, f32[16,32,128]{2,1,0:T(8,128)}) custom-call(s32[15]{0:T(128)} %select_add_fusion.meta, f32[4,16,256]{2,1,0:T(8,128)} %bitcast.31, f32[4,16,256]{2,1,0:T(8,128)} %copy-done.8, f32[4,16,256]{2,1,0:T(8,128)} %bitcast.32, f32[4,16,256]{2,1,0:T(8,128)} %copy-done.9, f32[2,16,256]{2,1,0:T(8,128)} %bitcast.36, ...), custom_call_target="tpu_custom_call" | custom-call | tf_op jit(solution)/shard_map/squares/pallas_call | solution.py:174
  187.3 13.9 %all_to_all.35 = f32[16,32,128]{2,1,0:T(8,128)S(1)} all-to-all(f32[16,32,128]{2,1,0:T(8,128)} %get-tuple-element.28), channel_id=1, replica_groups=mesh['xh'=2,'y'=4,'z'=8,'xl'=2,'core'=2] {'z','xl'}, dimensions={0} | all-to-all | bytes 524288 | tf_op jit(solution)/shard_map/all_to_all | solution.py:266
  201.3 17.3 %all_to_all.36.sum_ref = f32[16,32,128]{2,1,0:T(8,128)} all-to-all(f32[16,32,128]{2,1,0:T(8,128)S(1)} %broadcast_in_dim.17), channel_id=1, replica_groups=mesh['xh'=2,'y'=4,'z'=8,'xl'=2,'core'=2] {'xh','y','core'}, dimensions={0} | all-to-all | bytes 524288 | tf_op jit(solution)/shard_map/all_to_all | solution.py:267
  (119 shorter events, 32.9 us)
Async XLA Ops:
  0.0 26.7 %copy-start.13 = (pred[15]{0:T(512)(128)(4,1)S(1)}, pred[15]{0:T(512)(128)(4,1)}, u32[]{:S(2)}) copy-start(pred[15]{0:T(512)(128)(4,1)} %constant.16.clone) | copy-start | bytes 49
  0.0 26.7 %copy-start.14 = (pred[15]{0:T(512)(128)(4,1)S(1)}, pred[15]{0:T(512)(128)(4,1)}, u32[]{:S(2)}) copy-start(pred[15]{0:T(512)(128)(4,1)} %constant.15.clone) | copy-start | bytes 49
  0.0 26.7 %copy-start.15 = (s32[15]{0:T(128)S(1)}, s32[15]{0:T(128)}, u32[]{:S(2)}) copy-start(s32[15]{0:T(128)} %constant.39.clone) | copy-start | bytes 184
  0.0 26.7 %copy-start.16 = (s32[15]{0:T(128)S(1)}, s32[15]{0:T(128)}, u32[]{:S(2)}) copy-start(s32[15]{0:T(128)} %constant.38.clone) | copy-start | bytes 184
  2.5 19.2 %collective-permute-start = (bf16[1536,256]{1,0:T(8,128)(2,1)}, bf16[1536,256]{1,0:T(8,128)(2,1)}, u32[]{:S(2)}, u32[]{:S(2)}) collective-permute-start(bf16[1536,256]{1,0:T(8,128)(2,1)} %get-tuple-element.40), channel_id=1, source_target_pairs={{0,32},{1,33},{2,34},{3,35},{4,36},{5,37},{6,38},{7,39},{8,40},{9,... | collective-permute-start | bytes 2359304 | tf_op jit(solution)/shard_map/ppermute | solution.py:43
  4.6 22.7 %collective-permute-start.1 = (bf16[1536,256]{1,0:T(8,128)(2,1)}, bf16[1536,256]{1,0:T(8,128)(2,1)S(1)}, u32[]{:S(2)}, u32[]{:S(2)}) collective-permute-start(bf16[1536,256]{1,0:T(8,128)(2,1)} %get-tuple-element.40), channel_id=1, source_target_pairs={{0,96},{1,97},{2,98},{3,99},{4,100},{5,101},{6,102},{7,103},{8,104... | collective-permute-start | bytes 2359304 | tf_op jit(solution)/shard_map/ppermute | solution.py:43
  6.0 32.5 %collective-permute-start.4 = (bf16[1536,256]{1,0:T(8,128)(2,1)S(1)}, bf16[1536,256]{1,0:T(8,128)(2,1)S(1)}, u32[]{:S(2)}, u32[]{:S(2)}) collective-permute-start(bf16[1536,256]{1,0:T(8,128)(2,1)S(1)} %get-tuple-element.39), channel_id=1, source_target_pairs={{0,32},{1,33},{2,34},{3,35},{4,36},{5,37},{6,38},{7,39},{8,40},{9,... | collective-permute-start | bytes 2359304 | tf_op jit(solution)/shard_map/ppermute | solution.py:43
  6.0 34.0 %collective-permute-start.5 = (bf16[1536,256]{1,0:T(8,128)(2,1)S(1)}, bf16[1536,256]{1,0:T(8,128)(2,1)}, u32[]{:S(2)}, u32[]{:S(2)}) collective-permute-start(bf16[1536,256]{1,0:T(8,128)(2,1)S(1)} %get-tuple-element.39), channel_id=1, source_target_pairs={{0,96},{1,97},{2,98},{3,99},{4,100},{5,101},{6,102},{7,103},{8,104... | collective-permute-start | bytes 2359304 | tf_op jit(solution)/shard_map/ppermute | solution.py:43
  8.7 33.8 %collective-permute-start.6 = (bf16[1536,256]{1,0:T(8,128)(2,1)}, bf16[1536,256]{1,0:T(8,128)(2,1)}, u32[]{:S(2)}, u32[]{:S(2)}) collective-permute-start(bf16[1536,256]{1,0:T(8,128)(2,1)} %get-tuple-element.40), channel_id=1, source_target_pairs={{0,128},{1,129},{2,130},{3,131},{4,132},{5,133},{6,134},{7,135},{8... | collective-permute-start | bytes 2359304 | tf_op jit(solution)/shard_map/ppermute | solution.py:43
  21.7 22.6 %collective-permute-start.7 = (bf16[1536,256]{1,0:T(8,128)(2,1)S(1)}, bf16[1536,256]{1,0:T(8,128)(2,1)}, u32[]{:S(2)}, u32[]{:S(2)}) collective-permute-start(bf16[1536,256]{1,0:T(8,128)(2,1)S(1)} %get-tuple-element.39), channel_id=1, source_target_pairs={{0,128},{1,129},{2,130},{3,131},{4,132},{5,133},{6,134},{7,135},{8... | collective-permute-start | bytes 2359304 | tf_op jit(solution)/shard_map/ppermute | solution.py:43
  33.3 32.2 %collective-permute-start.2 = (f32[8,2,4,16,256]{4,3,2,1,0:T(8,128)}, f32[8,2,4,16,256]{4,3,2,1,0:T(8,128)S(1)}, u32[]{:S(2)}, u32[]{:S(2)}) collective-permute-start(f32[8,2,4,16,256]{4,3,2,1,0:T(8,128)} %get-tuple-element.18), channel_id=1, source_target_pairs={{0,1},{1,0},{2,3},{3,2},{4,5},{5,4},{6,7},{7,6},{8,9},{9,8},{10,11... | collective-permute-start | bytes 3145736 | tf_op jit(solution)/shard_map/ppermute | solution.py:43
  38.5 18.4 %collective-permute-start.10 = (bf16[1536,256]{1,0:T(8,128)(2,1)}, bf16[1536,256]{1,0:T(8,128)(2,1)}, u32[]{:S(2)}, u32[]{:S(2)}) collective-permute-start(bf16[1536,256]{1,0:T(8,128)(2,1)} %collective-permute-done.refs_1_), channel_id=1, source_target_pairs={{0,32},{1,33},{2,34},{3,35},{4,36},{5,37},{6,38},{7,39},{8,40},{9,... | collective-permute-start | bytes 2359304 | tf_op jit(solution)/shard_map/ppermute | solution.py:43
  40.1 19.5 %collective-permute-start.11 = (bf16[1536,256]{1,0:T(8,128)(2,1)}, bf16[1536,256]{1,0:T(8,128)(2,1)S(1)}, u32[]{:S(2)}, u32[]{:S(2)}) collective-permute-start(bf16[1536,256]{1,0:T(8,128)(2,1)} %collective-permute-done.5.refs_1_), channel_id=1, source_target_pairs={{0,96},{1,97},{2,98},{3,99},{4,100},{5,101},{6,102},{7,103},{8,104... | collective-permute-start | bytes 2359304 | tf_op jit(solution)/shard_map/ppermute | solution.py:43
  50.9 19.9 %collective-permute-start.8 = (f32[8,2,4,16,256]{4,3,2,1,0:T(8,128)}, f32[8,2,4,16,256]{4,3,2,1,0:T(8,128)}, u32[]{:S(2)}, u32[]{:S(2)}) collective-permute-start(f32[8,2,4,16,256]{4,3,2,1,0:T(8,128)} %get-tuple-element.20), channel_id=1, source_target_pairs={{0,1},{1,0},{2,3},{3,2},{4,5},{5,4},{6,7},{7,6},{8,9},{9,8},{10,11... | collective-permute-start | bytes 3145736 | tf_op jit(solution)/shard_map/ppermute | solution.py:43
  52.3 33.2 %collective-permute-start.14 = (bf16[1536,256]{1,0:T(8,128)(2,1)}, bf16[1536,256]{1,0:T(8,128)(2,1)}, u32[]{:S(2)}, u32[]{:S(2)}) collective-permute-start(bf16[1536,256]{1,0:T(8,128)(2,1)} %collective-permute-done.6.refs_2_), channel_id=1, source_target_pairs={{0,32},{1,33},{2,34},{3,35},{4,36},{5,37},{6,38},{7,39},{8,40},{9,... | collective-permute-start | bytes 2359304 | tf_op jit(solution)/shard_map/ppermute | solution.py:43
  56.9 44.7 %collective-permute-start.15 = (bf16[1536,256]{1,0:T(8,128)(2,1)}, bf16[1536,256]{1,0:T(8,128)(2,1)}, u32[]{:S(2)}, u32[]{:S(2)}) collective-permute-start(bf16[1536,256]{1,0:T(8,128)(2,1)} %collective-permute-done.6.refs_2_), channel_id=1, source_target_pairs={{0,96},{1,97},{2,98},{3,99},{4,100},{5,101},{6,102},{7,103},{8,104... | collective-permute-start | bytes 2359304 | tf_op jit(solution)/shard_map/ppermute | solution.py:43
  59.6 49.0 %collective-permute-start.19 = (bf16[1536,256]{1,0:T(8,128)(2,1)}, bf16[1536,256]{1,0:T(8,128)(2,1)}, u32[]{:S(2)}, u32[]{:S(2)}) collective-permute-start(bf16[1536,256]{1,0:T(8,128)(2,1)} %collective-permute-done.7.refs_3_), channel_id=1, source_target_pairs={{0,32},{1,33},{2,34},{3,35},{4,36},{5,37},{6,38},{7,39},{8,40},{9,... | collective-permute-start | bytes 2359304 | tf_op jit(solution)/shard_map/ppermute | solution.py:43
  65.5 7.8 %collective-permute-start.12 = (f32[8,2,2,16,256]{4,3,2,1,0:T(8,128)}, f32[8,2,2,16,256]{4,3,2,1,0:T(8,128)S(1)}, u32[]{:S(2)}, u32[]{:S(2)}) collective-permute-start(f32[8,2,2,16,256]{4,3,2,1,0:T(8,128)} %get-tuple-element.22), channel_id=1, source_target_pairs={{0,1},{1,0},{2,3},{3,2},{4,5},{5,4},{6,7},{7,6},{8,9},{9,8},{10,11... | collective-permute-start | bytes 1572872 | tf_op jit(solution)/shard_map/ppermute | solution.py:43
  70.9 37.7 %collective-permute-start.20 = (bf16[1536,256]{1,0:T(8,128)(2,1)}, bf16[1536,256]{1,0:T(8,128)(2,1)}, u32[]{:S(2)}, u32[]{:S(2)}) collective-permute-start(bf16[1536,256]{1,0:T(8,128)(2,1)} %collective-permute-done.7.refs_3_), channel_id=1, source_target_pairs={{0,96},{1,97},{2,98},{3,99},{4,100},{5,101},{6,102},{7,103},{8,104... | collective-permute-start | bytes 2359304 | tf_op jit(solution)/shard_map/ppermute | solution.py:43
  73.3 28.3 %collective-permute-start.16 = (bf16[1536,256]{1,0:T(8,128)(2,1)}, bf16[1536,256]{1,0:T(8,128)(2,1)}, u32[]{:S(2)}, u32[]{:S(2)}) collective-permute-start(bf16[1536,256]{1,0:T(8,128)(2,1)} %collective-permute-done.10.refs_0_), channel_id=1, source_target_pairs={{0,128},{1,129},{2,130},{3,131},{4,132},{5,133},{6,134},{7,135},{8... | collective-permute-start | bytes 2359304 | tf_op jit(solution)/shard_map/ppermute | solution.py:43
  77.7 19.1 %all-to-all-start.2 = ((f16[8,72,256]{2,1,0:T(8,128)(2,1)}), f16[8,72,256]{2,1,0:T(8,128)(2,1)S(1)}, u32[]{:S(2)}, u32[]{:S(2)}) async-start(f16[8,72,256]{2,1,0:T(8,128)(2,1)} %pad_maximum_fusion.4), calls=%async_computation.2 | async-start | bytes 589824 | tf_op jit(solution)/shard_map/all_to_all | solution.py:246
  85.5 26.0 %collective-permute-start.21 = (bf16[1536,256]{1,0:T(8,128)(2,1)S(1)}, bf16[1536,256]{1,0:T(8,128)(2,1)}, u32[]{:S(2)}, u32[]{:S(2)}) collective-permute-start(bf16[1536,256]{1,0:T(8,128)(2,1)S(1)} %copy-done.3), channel_id=1, source_target_pairs={{0,128},{1,129},{2,130},{3,131},{4,132},{5,133},{6,134},{7,135},{8... | collective-permute-start | bytes 2359304 | tf_op jit(solution)/shard_map/ppermute | solution.py:43
  96.8 21.9 %all-to-all-start = ((f16[8,136,256]{2,1,0:T(8,128)(2,1)}), f16[8,136,256]{2,1,0:T(8,128)(2,1)S(1)}, u32[]{:S(2)}, u32[]{:S(2)}) async-start(f16[8,136,256]{2,1,0:T(8,128)(2,1)} %pad_maximum_fusion), calls=%async_computation | async-start | bytes 1114112 | tf_op jit(solution)/shard_map/all_to_all | solution.py:246
  105.7 23.5 %collective-permute-start.17 = (f32[8,2,3,16,256]{4,3,2,1,0:T(8,128)}, f32[8,2,3,16,256]{4,3,2,1,0:T(8,128)}, u32[]{:S(2)}, u32[]{:S(2)}) collective-permute-start(f32[8,2,3,16,256]{4,3,2,1,0:T(8,128)} %get-tuple-element.24), channel_id=1, source_target_pairs={{0,1},{1,0},{2,3},{3,2},{4,5},{5,4},{6,7},{7,6},{8,9},{9,8},{10,11... | collective-permute-start | bytes 2359304 | tf_op jit(solution)/shard_map/ppermute | solution.py:43
  115.8 33.1 %collective-permute-start.22 = (f32[8,2,3,16,256]{4,3,2,1,0:T(8,128)}, f32[8,2,3,16,256]{4,3,2,1,0:T(8,128)S(1)}, u32[]{:S(2)}, u32[]{:S(2)}) collective-permute-start(f32[8,2,3,16,256]{4,3,2,1,0:T(8,128)} %get-tuple-element.26), channel_id=1, source_target_pairs={{0,1},{1,0},{2,3},{3,2},{4,5},{5,4},{6,7},{7,6},{8,9},{9,8},{10,11... | collective-permute-start | bytes 2359304 | tf_op jit(solution)/shard_map/ppermute | solution.py:43
  118.3 65.8 %collective-permute-start.13 = (f32[2,16,256]{2,1,0:T(8,128)S(1)}, f32[2,16,256]{2,1,0:T(8,128)S(1)}, u32[]{:S(2)}, u32[]{:S(2)}) collective-permute-start(f32[2,16,256]{2,1,0:T(8,128)S(1)} %bitcast.40), channel_id=1, source_target_pairs={{0,2},{1,3},{2,0},{3,1},{4,6},{5,7},{6,4},{7,5},{8,10},{9,11},{10,... | collective-permute-start | bytes 98312 | tf_op jit(solution)/shard_map/ppermute | solution.py:43
  118.7 26.7 %all-to-all-start.1 = ((f16[8,136,256]{2,1,0:T(8,128)(2,1)}), f16[8,136,256]{2,1,0:T(8,128)(2,1)S(1)}, u32[]{:S(2)}, u32[]{:S(2)}) async-start(f16[8,136,256]{2,1,0:T(8,128)(2,1)} %pad_maximum_fusion.1), calls=%async_computation.1 | async-start | bytes 1114112 | tf_op jit(solution)/shard_map/all_to_all | solution.py:246
  128.0 56.1 %collective-permute-start.3 = (f32[4,16,256]{2,1,0:T(8,128)S(1)}, f32[4,16,256]{2,1,0:T(8,128)S(1)}, u32[]{:S(2)}, u32[]{:S(2)}) collective-permute-start(f32[4,16,256]{2,1,0:T(8,128)S(1)} %bitcast.37), channel_id=1, source_target_pairs={{0,2},{1,3},{2,0},{3,1},{4,6},{5,7},{6,4},{7,5},{8,10},{9,11},{10,... | collective-permute-start | bytes 196616 | tf_op jit(solution)/shard_map/ppermute | solution.py:43
  145.5 19.2 %all-to-all-start.3 = ((f16[8,104,256]{2,1,0:T(8,128)(2,1)}), f16[8,104,256]{2,1,0:T(8,128)(2,1)S(1)}, u32[]{:S(2)}, u32[]{:S(2)}) async-start(f16[8,104,256]{2,1,0:T(8,128)(2,1)} %pad_maximum_fusion.3), calls=%async_computation.3 | async-start | bytes 851968 | tf_op jit(solution)/shard_map/all_to_all | solution.py:246
  164.7 18.4 %all-to-all-start.4 = ((f16[16,56,256]{2,1,0:T(8,128)(2,1)}), f16[16,56,256]{2,1,0:T(8,128)(2,1)S(1)}, u32[]{:S(2)}, u32[]{:S(2)}) async-start(f16[16,56,256]{2,1,0:T(8,128)(2,1)} %pad_maximum_fusion.2), calls=%async_computation.4 | async-start | bytes 917504 | tf_op jit(solution)/shard_map/all_to_all | solution.py:243
  169.4 14.7 %collective-permute-start.9 = (f32[4,16,256]{2,1,0:T(8,128)S(1)}, f32[4,16,256]{2,1,0:T(8,128)S(1)}, u32[]{:S(2)}, u32[]{:S(2)}) collective-permute-start(f32[4,16,256]{2,1,0:T(8,128)S(1)} %bitcast.38), channel_id=1, source_target_pairs={{0,2},{1,3},{2,0},{3,1},{4,6},{5,7},{6,4},{7,5},{8,10},{9,11},{10,... | collective-permute-start | bytes 196616 | tf_op jit(solution)/shard_map/ppermute | solution.py:43
  171.7 12.4 %collective-permute-start.18 = (f32[3,16,256]{2,1,0:T(8,128)S(1)}, f32[3,16,256]{2,1,0:T(8,128)S(1)}, u32[]{:S(2)}, u32[]{:S(2)}) collective-permute-start(f32[3,16,256]{2,1,0:T(8,128)S(1)} %bitcast.39), channel_id=1, source_target_pairs={{0,2},{1,3},{2,0},{3,1},{4,6},{5,7},{6,4},{7,5},{8,10},{9,11},{10,... | collective-permute-start | bytes 147464 | tf_op jit(solution)/shard_map/ppermute | solution.py:43
  (14 other events, 111.3 us)

commit v5 on v3

--- a/solution.py
+++ b/solution.py
@@ -1,4 +1,5 @@
 import itertools
+import math
 
 import jax
 import jax.numpy as jnp
@@ -23,8 +24,9 @@
 BATCHES = (
     ((0, 0, (0, 1)),),
     ((0, 3, (0, 1)), (0, 1, (0, 1)), (1, 0, (0, 1))),
+    ((1, 3, (0,)), (1, 1, (0,)), (1, 2, (0,))),
     ((0, 2, (0, 1)),),
-    ((1, 3, (0, 1)), (1, 1, (0, 1)), (1, 2, (0, 1))),
+    ((1, 3, (1,)), (1, 1, (1,)), (1, 2, (1,))),
 )
 PANELS = tuple(itertools.chain(*BATCHES))
 CORE, XLO = len(PANELS), len(PANELS) + 1
@@ -196,23 +198,32 @@
     return pl.pallas_call(body, out_shape=jax.ShapeDtypeStruct(squared.shape, F32), name="scaled")(squared, sums)
 
 
-def encode(total):
-    peers, n = total.shape[0], total.shape[-3]
-    top = jnp.max(jnp.abs(total), axis=(*range(total.ndim - 3), total.ndim - 2))
-    scale = lax.reduce_precision(jnp.maximum(top * (SCALE * 1.002), 6.2e-05), 5, 10)
-    t = total * (SCALE / scale)[:, None]
-    codes = (t * jnp.abs(t) * TOP).astype(WIRE).reshape(peers, -1, HALF)
-    rows = jnp.pad(scale.astype(WIRE), ((0, 8 - n), (0, 0)))
-    return jnp.concatenate([codes, jnp.broadcast_to(rows[None], (peers, 8, HALF))], axis=1)
-
-
-def decode(coded, shape):
+def encode(totals):
+    peers = totals[0].shape[0]
+    codes, scales = [], []
+    for total in totals:
+        top = jnp.max(jnp.abs(total), axis=(*range(total.ndim - 3), total.ndim - 2))
+        scale = lax.reduce_precision(jnp.maximum(top * (SCALE * 1.002), 6.2e-05), 5, 10)
+        t = total * (SCALE / scale)[:, None]
+        codes.append((t * jnp.abs(t) * TOP).astype(WIRE).reshape(peers, -1, HALF))
+        scales.append(scale.astype(WIRE))
+    rows = jnp.concatenate(scales)
+    rows = jnp.pad(rows, ((0, 8 - rows.shape[0]), (0, 0)))
+    return jnp.concatenate([*codes, jnp.broadcast_to(rows[None], (peers, 8, HALF))], axis=1)
+
+
+def decode(coded, shapes):
     peers, end = coded.shape[0], coded.shape[1] - 8
-    codes = coded[:, :end].astype(F32).reshape(peers, *shape)
-    scale = coded[:, end : end + shape[-3]].astype(F32) * (1 / SCALE)
-    scale = scale.reshape(peers, *([1] * (len(shape) - 3)), shape[-3], 1, HALF)
-    size = jnp.sqrt(jnp.abs(codes) * (1 / TOP))
-    return jnp.sum(jnp.where(codes < 0, -size, size) * scale, axis=0)
+    row, spot, sums = 0, end, []
+    for shape in shapes:
+        rows, n = math.prod(shape[:-1]), shape[-3]
+        codes = coded[:, row : row + rows].astype(F32).reshape(peers, *shape)
+        scale = coded[:, spot : spot + n].astype(F32) * (1 / SCALE)
+        scale = scale.reshape(peers, *([1] * (len(shape) - 3)), n, 1, HALF)
+        size = jnp.sqrt(jnp.abs(codes) * (1 / TOP))
+        sums.append(jnp.sum(jnp.where(codes < 0, -size, size) * scale, axis=0))
+        row, spot = row + rows, spot + n
+    return sums
 
 
 def pipeline(walk, values, col_index, col_count):
@@ -228,33 +239,38 @@
     def pair(left, right):
         return [(left, 0, HALF), (right, 0, HALF)]
 
+    def one(array):
+        return [(array, 0, HALF)]
+
     ends = []
 
-    def work(batch, given, both=False):
+    def partial(batch, given, both=False):
         keep, give = product(batch, scalars, walk, given, both)
-        got = move(give, dc=1)
-        n = keep.shape[2]
+        return keep + move(give, dc=1)
+
+    def exchange(totals, both=False):
         if both:
-            coded = encode((keep + got).reshape(16, n, 16, HALF))
-            arrived = lax.all_to_all(coded, ("z", "xl"), 0, 0, tiled=True)
-            ends.append((decode(arrived, (n, 16, HALF)),))
-        else:
-            arrived = lax.all_to_all(encode(keep + got), "z", 0, 0, tiled=True)
-            total = decode(arrived, (2, n, 16, HALF))
-            ends.append((total[0], move(total[1], dxl=1)))
+            totals = [t.reshape(16, *t.shape[2:]) for t in totals]
+        arrived = lax.all_to_all(encode(totals), ("z", "xl") if both else "z", 0, 0, tiled=True)
+        sums = decode(arrived, [t.shape[1:] for t in totals])
+        for total in sums:
+            ends.append((total,) if both else (total[0], move(total[1], dxl=1)))
 
     up = move(values, dy=1)
     down = move(values, dy=3)
     over = move(values, dxh=1)
     far = [move(up[:, :HALF], dy=1), move(down[:, HALF:], dy=3)]
-    over_up = move(over, dy=1)
-    over_down = move(over, dy=3)
+    over_half = (over[:, :HALF], over[:, HALF:])
+    over_up = [move(over_half[t], dy=1) for t in range(2)]
+    over_down = [move(over_half[t], dy=3) for t in range(2)]
     over_far = [move(far[t], dxh=1) for t in range(2)]
 
-    work(0, [whole(values)])
-    work(1, [whole(up), whole(down), whole(over)])
-    work(2, [pair(*far)])
-    work(3, [whole(over_up), whole(over_down), pair(*over_far)], both=True)
+    exchange([partial(0, [whole(values)])])
+    exchange([partial(1, [whole(up), whole(down), whole(over)])])
+    exchange([partial(2, [one(over_up[0]), one(over_down[0]), one(over_far[0])])])
+    last = [partial(3, [pair(*far)], both=True)]
+    last.append(partial(4, [one(over_up[1]), one(over_down[1]), one(over_far[1])], both=True))
+    exchange(last, both=True)
 
     squared, sums = squares(meta, ends)
     sums = jnp.sum(lax.all_to_all(sums, ("z", "xl"), 0, 0), axis=0)

time: 240 us -> 227 us (0.946)
  waiting for transfers between devices: 106 us -> 94.1 us
  other arithmetic: 16.3 us -> 11.8 us
  local copies, waits for them, and re-layouts: 5.29 us -> 8.38 us
  Pallas kernels: 25.3 us -> 28.3 us
  blocking collectives: 32.8 us -> 29.9 us
    all_to_all x4, waiting for transfers between devices: 46.8 us -> 40.7 us  [exchange(): lax.all_to_all(encode(totals), ('z', 'xl') if both else 'z', 0, 0, tiled=...]
    ppermute x16 -> x19, waiting for transfers between devices: 58.9 us -> 53.3 us  [send(): return lax.ppermute(x, AXES, moves(**by))]
    reduce_max x4 -> x5, other arithmetic: 6.47 us -> 2.94 us  [encode(): top = jnp.max(jnp.abs(total), axis=(*range(total.ndim - 3), total.ndim - 2))]
    pallas_call x4 -> x5, Pallas kernels: 20.9 us -> 23.9 us  [product(): pl.pallas_call(body, out_shape=(out, out), grid_spec=pltpu.PrefetchScalar...]
    all_to_all x1, blocking collectives: 17.8 us -> 15.2 us  [pipeline(): lax.all_to_all(jnp.broadcast_to(sums[None], (16, 32, 128)), ('xh', 'y', '...]
    ppermute x16 -> x19, starting transfers between devices: 30.4 us -> 29.4 us  [send(): return lax.ppermute(x, AXES, moves(**by))]
  transfers between devices with their start and end apart: 20 -> 23, of which waited for: 10 -> 6; matrix products, arithmetic and copies ran while one was open for 9% -> 8% of each run, Pallas kernels for 9% -> 11%
where the time goes in v5:
time: 227 us; the launch traced here: 226 us
  waiting for transfers between devices  94.1 us (41%)
  starting transfers between devices  52.8 us (23%)
  blocking collectives  29.9 us (13%)
  Pallas kernels  28.3 us (12%)
  other arithmetic  11.8 us (5%)
  local copies, waits for them, and re-layouts  8.38 us (4%)
    ppermute x19, waiting for transfers between devices, send(): return lax.ppermute(x, AXES, moves(**by))  53.3 us
    all_to_all x4, waiting for transfers between devices, exchange(): lax.all_to_all(encode(totals), ('z', 'xl') if both else 'z', 0, 0, tiled=...  40.7 us
    ppermute x19, starting transfers between devices, send(): return lax.ppermute(x, AXES, moves(**by))  29.4 us
    pallas_call x5, Pallas kernels, product(): pl.pallas_call(body, out_shape=(out, out), grid_spec=pltpu.PrefetchScalar...  23.9 us
    all_to_all x4, starting transfers between devices, exchange(): lax.all_to_all(encode(totals), ('z', 'xl') if both else 'z', 0, 0, tiled=...  23.4 us
    all_to_all x1, blocking collectives, pipeline(): lax.all_to_all(jnp.broadcast_to(sums[None], (16, 32, 128)), ('xh', 'y', '...  15.2 us
    all_to_all x1, blocking collectives, pipeline(): sums = jnp.sum(lax.all_to_all(sums, ('z', 'xl'), 0, 0), axis=0)  14.7 us
  transfers between devices with their start and end apart: 23, of which 6 were waited for; matrix products, arithmetic and copies ran while one was open for 8% of the time, Pallas kernels for 11%

profile of v5, /device:TPU:1, one launch (start us, length us, event | category | flops | bytes accessed | tf_op | source)
XLA Modules:
  0.0 225.6 jit_solution(15368164299081795950)
XLA Ops:
  0.0 2.2 collective-permute-start.2
  2.2 2.7 %collective-permute-start.4 = (bf16[1536,512]{1,0:T(8,128)(2,1)}, bf16[1536,512]{1,0:T(8,128)(2,1)S(1)}, u32[]{:S(2)}, u32[]{:S(2)}) collective-permute-start(bf16[1536,512]{1,0:T(8,128)(2,1)} %refs_0_.1), channel_id=1, source_target_pairs={{0,128},{1,129},{2,130},{3,131},{4,132},{5,133},{6,134},{7,135},{8... | collective-permute-start | bytes 4718600 | tf_op jit(solution)/shard_map/ppermute | solution.py:44
  5.0 1.5 collective-permute-start.3
  6.5 29.7 %collective-permute-done.2.refs_0_ = bf16[1536,512]{1,0:T(8,128)(2,1)} collective-permute-done((bf16[1536,512]{1,0:T(8,128)(2,1)}, bf16[1536,512]{1,0:T(8,128)(2,1)}, u32[]{:S(2)}, u32[]{:S(2)}) %collective-permute-start.2) | collective-permute-done | bytes 1572896 | tf_op jit(solution)/shard_map/ppermute | solution.py:44
  36.2 2.1 slice.95
  38.3 1.5 collective-permute-start.9
  42.6 7.0 %shard_map.92 = (f32[8,2,6,16,256]{4,3,2,1,0:T(8,128)}, f32[8,2,6,16,256]{4,3,2,1,0:T(8,128)}) custom-call(s32[13]{0:T(128)} %select_add_fusion.meta, s32[24]{0:T(128)} %reshape.99.index, s32[8]{0:T(128)} %bitcast.41, bf16[512,4096]{1,0:T(8,128)(2,1)} %w_hbm.9, bf16[1536,512]{1,0:T(8,128)(2,1)} %collective-permute-done.2.refs_0_, ...), custom_call_target="tpu_custom_call" | custom-call | tf_op jit(solution)/shard_map/pallas_call | solution.py:133
  49.8 3.6 %shard_map.91 = (f32[8,2,2,16,256]{4,3,2,1,0:T(8,128)}, f32[8,2,2,16,256]{4,3,2,1,0:T(8,128)}) custom-call(s32[13]{0:T(128)} %select_add_fusion.meta, s32[24]{0:T(128)} %reshape.99.index, s32[8]{0:T(128)} %bitcast.42, bf16[512,4096]{1,0:T(8,128)(2,1)} %w_hbm.9, bf16[1536,512]{1,0:T(8,128)(2,1)} %refs_0_.1), custom_call_target="tpu_custom_call" | custom-call | tf_op jit(solution)/shard_map/pallas_call | solution.py:133
  53.4 1.3 collective-permute-start
  54.7 1.3 fusion.41
  56.0 2.7 %collective-permute-start.7 = (bf16[1536,256]{1,0:T(8,128)(2,1)}, bf16[1536,256]{1,0:T(8,128)(2,1)}, u32[]{:S(2)}, u32[]{:S(2)}) collective-permute-start(bf16[1536,256]{1,0:T(8,128)(2,1)} %get-tuple-element.40), channel_id=1, source_target_pairs={{0,32},{1,33},{2,34},{3,35},{4,36},{5,37},{6,38},{7,39},{8,40},{9,... | collective-permute-start | bytes 2359304 | tf_op jit(solution)/shard_map/ppermute | solution.py:44
  60.1 1.5 collective-permute-start.13
  61.6 1.4 collective-permute-start.10
  64.1 8.8 %all-to-all-start = ((f16[8,72,256]{2,1,0:T(8,128)(2,1)}), f16[8,72,256]{2,1,0:T(8,128)(2,1)S(1)}, u32[]{:S(2)}, u32[]{:S(2)}) async-start(f16[8,72,256]{2,1,0:T(8,128)(2,1)} %pad_maximum_fusion.3), calls=%async_computation | async-start | bytes 589824 | tf_op jit(solution)/shard_map/all_to_all | solution.py:254
  72.9 21.4 %collective-permute-done.13.refs_1_ = bf16[1536,256]{1,0:T(8,128)(2,1)S(1)} collective-permute-done((bf16[1536,256]{1,0:T(8,128)(2,1)S(1)}, bf16[1536,256]{1,0:T(8,128)(2,1)S(1)}, u32[]{:S(2)}, u32[]{:S(2)}) %collective-permute-start.13) | collective-permute-done | bytes 786464 | tf_op jit(solution)/shard_map/ppermute | solution.py:44
  95.2 5.1 %shard_map.94 = (f32[8,2,2,16,256]{4,3,2,1,0:T(8,128)}, f32[8,2,2,16,256]{4,3,2,1,0:T(8,128)}) custom-call(s32[13]{0:T(128)} %select_add_fusion.meta, s32[24]{0:T(128)} %reshape.99.index, s32[8]{0:T(128)} %bitcast.43, bf16[512,4096]{1,0:T(8,128)(2,1)} %w_hbm.9, bf16[1536,256]{1,0:T(8,128)(2,1)} %collective-permute-done.9.refs_0_, bf16[1536,256]{1,0:T(8,128)(2,1)} %copy-done.5), custom_call_target="tpu_custom_call" | custom-call | tf_op jit(solution)/shard_map/pallas_call | solution.py:133
  101.5 1.6 collective-permute-start.14
  103.1 4.1 %collective-permute-start.17 = (bf16[1536,256]{1,0:T(8,128)(2,1)}, bf16[1536,256]{1,0:T(8,128)(2,1)}, u32[]{:S(2)}, u32[]{:S(2)}) collective-permute-start(bf16[1536,256]{1,0:T(8,128)(2,1)} %copy-done.5), channel_id=1, source_target_pairs={{0,128},{1,129},{2,130},{3,131},{4,132},{5,133},{6,134},{7,135},{8... | collective-permute-start | bytes 2359304 | tf_op jit(solution)/shard_map/ppermute | solution.py:44
  107.3 4.1 %shard_map.93 = (f32[8,2,3,16,256]{4,3,2,1,0:T(8,128)}, f32[8,2,3,16,256]{4,3,2,1,0:T(8,128)}) custom-call(s32[13]{0:T(128)} %select_add_fusion.meta, s32[24]{0:T(128)} %reshape.99.index, s32[8]{0:T(128)} %bitcast.44, bf16[512,4096]{1,0:T(8,128)(2,1)} %w_hbm.9, bf16[1536,256]{1,0:T(8,128)(2,1)} %collective-permute-done.7.refs_0_, ...), custom_call_target="tpu_custom_call" | custom-call | tf_op jit(solution)/shard_map/pallas_call | solution.py:133
  114.4 7.6 %all-to-all-start.1 = ((f16[8,200,256]{2,1,0:T(8,128)(2,1)}), f16[8,200,256]{2,1,0:T(8,128)(2,1)S(1)}, u32[]{:S(2)}, u32[]{:S(2)}) async-start(f16[8,200,256]{2,1,0:T(8,128)(2,1)} %pad_maximum_fusion), calls=%async_computation.1 | async-start | bytes 1638400 | tf_op jit(solution)/shard_map/all_to_all | solution.py:254
  123.2 2.2 collective-permute-done.17.refs_2_
  125.4 4.2 %shard_map.95 = (f32[8,2,3,16,256]{4,3,2,1,0:T(8,128)}, f32[8,2,3,16,256]{4,3,2,1,0:T(8,128)}) custom-call(s32[13]{0:T(128)} %select_add_fusion.meta, s32[24]{0:T(128)} %reshape.99.index, s32[8]{0:T(128)} %bitcast.45, bf16[512,4096]{1,0:T(8,128)(2,1)} %w_hbm.9, bf16[1536,256]{1,0:T(8,128)(2,1)} %collective-permute-done.15.refs_0_, ...), custom_call_target="tpu_custom_call" | custom-call | tf_op jit(solution)/shard_map/pallas_call | solution.py:133
  129.6 1.4 collective-permute-start.18
  133.3 13.0 %all-to-all-done.1 = f16[8,200,256]{2,1,0:T(8,128)(2,1)S(1)} async-done(((f16[8,200,256]{2,1,0:T(8,128)(2,1)}), f16[8,200,256]{2,1,0:T(8,128)(2,1)S(1)}, u32[]{:S(2)}, u32[]{:S(2)}) %all-to-all-start.1) | async-done | bytes 819232 | tf_op jit(solution)/shard_map/all_to_all | solution.py:254
  146.3 3.5 %all-to-all-start.2 = ((f16[8,104,256]{2,1,0:T(8,128)(2,1)}), f16[8,104,256]{2,1,0:T(8,128)(2,1)S(1)}, u32[]{:S(2)}, u32[]{:S(2)}) async-start(f16[8,104,256]{2,1,0:T(8,128)(2,1)} %pad_maximum_fusion.2), calls=%async_computation.2 | async-start | bytes 851968 | tf_op jit(solution)/shard_map/all_to_all | solution.py:254
  151.2 14.3 %all-to-all-done.2 = f16[8,104,256]{2,1,0:T(8,128)(2,1)S(1)} async-done(((f16[8,104,256]{2,1,0:T(8,128)(2,1)}), f16[8,104,256]{2,1,0:T(8,128)(2,1)S(1)}, u32[]{:S(2)}, u32[]{:S(2)}) %all-to-all-start.2) | async-done | bytes 426016 | tf_op jit(solution)/shard_map/all_to_all | solution.py:254
  165.5 3.6 %all-to-all-start.3 = ((f16[16,88,256]{2,1,0:T(8,128)(2,1)}), f16[16,88,256]{2,1,0:T(8,128)(2,1)S(1)}, u32[]{:S(2)}, u32[]{:S(2)}) async-start(f16[16,88,256]{2,1,0:T(8,128)(2,1)} %pad_maximum_fusion.1), calls=%async_computation.3 | async-start | bytes 1441792 | tf_op jit(solution)/shard_map/all_to_all | solution.py:254
  175.3 13.5 %all-to-all-done.3 = f16[16,88,256]{2,1,0:T(8,128)(2,1)S(1)} async-done(((f16[16,88,256]{2,1,0:T(8,128)(2,1)}), f16[16,88,256]{2,1,0:T(8,128)(2,1)S(1)}, u32[]{:S(2)}, u32[]{:S(2)}) %all-to-all-start.3) | async-done | bytes 720928 | tf_op jit(solution)/shard_map/all_to_all | solution.py:254
  191.3 2.6 %squares.1 = (f32[16,4096]{1,0:T(8,128)}, f32[16,32,128]{2,1,0:T(8,128)}) custom-call(s32[13]{0:T(128)} %select_add_fusion.meta, f32[2,16,256]{2,1,0:T(8,128)} %bitcast.37, f32[2,16,256]{2,1,0:T(8,128)} %copy-done.12, f32[6,16,256]{2,1,0:T(8,128)} %bitcast.31, f32[6,16,256]{2,1,0:T(8,128)} %copy-done.10, f32[3,16,256]{2,1,0:T(8,128)} %bitcast.33, ...), custom_call_target="tpu_custom_call" | custom-call | tf_op jit(solution)/shard_map/squares/pallas_call | solution.py:175
  193.9 14.7 %all_to_all.30 = f32[16,32,128]{2,1,0:T(8,128)S(1)} all-to-all(f32[16,32,128]{2,1,0:T(8,128)} %get-tuple-element.28), channel_id=1, replica_groups=mesh['xh'=2,'y'=4,'z'=8,'xl'=2,'core'=2] {'z','xl'}, dimensions={0} | all-to-all | bytes 524288 | tf_op jit(solution)/shard_map/all_to_all | solution.py:276
  208.6 15.2 %all_to_all.31.sum_ref = f32[16,32,128]{2,1,0:T(8,128)} all-to-all(f32[16,32,128]{2,1,0:T(8,128)S(1)} %broadcast_in_dim.14), channel_id=1, replica_groups=mesh['xh'=2,'y'=4,'z'=8,'xl'=2,'core'=2] {'xh','y','core'}, dimensions={0} | all-to-all | bytes 524288 | tf_op jit(solution)/shard_map/all_to_all | solution.py:277
  223.9 1.8 scaled.1
  (110 shorter events, 24.1 us)
Async XLA Ops:
  0.0 39.8 %copy-start.14 = (s32[13]{0:T(128)S(1)}, s32[13]{0:T(128)}, u32[]{:S(2)}) copy-start(s32[13]{0:T(128)} %constant.37.clone) | copy-start | bytes 160
  0.0 39.8 %copy-start.15 = (s32[13]{0:T(128)S(1)}, s32[13]{0:T(128)}, u32[]{:S(2)}) copy-start(s32[13]{0:T(128)} %constant.38.clone) | copy-start | bytes 160
  0.0 39.8 %copy-start.16 = (s32[13]{0:T(128)S(1)}, s32[13]{0:T(128)}, u32[]{:S(2)}) copy-start(s32[13]{0:T(128)} %constant.39.clone) | copy-start | bytes 160
  0.0 39.8 %copy-start.17 = (pred[13]{0:T(512)(128)(4,1)S(1)}, pred[13]{0:T(512)(128)(4,1)}, u32[]{:S(2)}) copy-start(pred[13]{0:T(512)(128)(4,1)} %constant.40.clone) | copy-start | bytes 43
  0.0 39.8 %copy-start.18 = (pred[13]{0:T(512)(128)(4,1)S(1)}, pred[13]{0:T(512)(128)(4,1)}, u32[]{:S(2)}) copy-start(pred[13]{0:T(512)(128)(4,1)} %constant.41.clone) | copy-start | bytes 43
  0.0 40.3 %copy-start.13 = (s32[3,8]{1,0:T(4,128)S(1)}, s32[3,8]{1,0:T(4,128)}, u32[]{:S(2)}) copy-start(s32[3,8]{1,0:T(4,128)} %param.11) | copy-start | bytes 292
  0.0 36.1 %collective-permute-start.2 = (bf16[1536,512]{1,0:T(8,128)(2,1)}, bf16[1536,512]{1,0:T(8,128)(2,1)}, u32[]{:S(2)}, u32[]{:S(2)}) collective-permute-start(bf16[1536,512]{1,0:T(8,128)(2,1)} %refs_0_.1), channel_id=1, source_target_pairs={{0,32},{1,33},{2,34},{3,35},{4,36},{5,37},{6,38},{7,39},{8,40},{9,... | collective-permute-start | bytes 4718600 | tf_op jit(solution)/shard_map/ppermute | solution.py:44
  2.2 38.7 %collective-permute-start.4 = (bf16[1536,512]{1,0:T(8,128)(2,1)}, bf16[1536,512]{1,0:T(8,128)(2,1)S(1)}, u32[]{:S(2)}, u32[]{:S(2)}) collective-permute-start(bf16[1536,512]{1,0:T(8,128)(2,1)} %refs_0_.1), channel_id=1, source_target_pairs={{0,128},{1,129},{2,130},{3,131},{4,132},{5,133},{6,134},{7,135},{8... | collective-permute-start | bytes 4718600 | tf_op jit(solution)/shard_map/ppermute | solution.py:44
  5.0 36.0 %collective-permute-start.3 = (bf16[1536,512]{1,0:T(8,128)(2,1)}, bf16[1536,512]{1,0:T(8,128)(2,1)S(1)}, u32[]{:S(2)}, u32[]{:S(2)}) collective-permute-start(bf16[1536,512]{1,0:T(8,128)(2,1)} %refs_0_.1), channel_id=1, source_target_pairs={{0,96},{1,97},{2,98},{3,99},{4,100},{5,101},{6,102},{7,103},{8,104... | collective-permute-start | bytes 4718600 | tf_op jit(solution)/shard_map/ppermute | solution.py:44
  38.3 23.4 %collective-permute-start.9 = (bf16[1536,256]{1,0:T(8,128)(2,1)}, bf16[1536,256]{1,0:T(8,128)(2,1)}, u32[]{:S(2)}, u32[]{:S(2)}) collective-permute-start(bf16[1536,256]{1,0:T(8,128)(2,1)} %slice.95), channel_id=1, source_target_pairs={{0,32},{1,33},{2,34},{3,35},{4,36},{5,37},{6,38},{7,39},{8,40},{9,... | collective-permute-start | bytes 2359304 | tf_op jit(solution)/shard_map/ppermute | solution.py:44
  49.6 61.9 %collective-permute-start.5 = (f32[8,2,6,16,256]{4,3,2,1,0:T(8,128)}, f32[8,2,6,16,256]{4,3,2,1,0:T(8,128)S(1)}, u32[]{:S(2)}, u32[]{:S(2)}) collective-permute-start(f32[8,2,6,16,256]{4,3,2,1,0:T(8,128)} %get-tuple-element.20), channel_id=1, source_target_pairs={{0,1},{1,0},{2,3},{3,2},{4,5},{5,4},{6,7},{7,6},{8,9},{9,8},{10,11... | collective-permute-start | bytes 4718600 | tf_op jit(solution)/shard_map/ppermute | solution.py:44
  53.4 6.6 %collective-permute-start = (f32[8,2,2,16,256]{4,3,2,1,0:T(8,128)}, f32[8,2,2,16,256]{4,3,2,1,0:T(8,128)S(1)}, u32[]{:S(2)}, u32[]{:S(2)}) collective-permute-start(f32[8,2,2,16,256]{4,3,2,1,0:T(8,128)} %get-tuple-element.18), channel_id=1, source_target_pairs={{0,1},{1,0},{2,3},{3,2},{4,5},{5,4},{6,7},{7,6},{8,9},{9,8},{10,11... | collective-permute-start | bytes 1572872 | tf_op jit(solution)/shard_map/ppermute | solution.py:44
  56.0 44.3 %collective-permute-start.7 = (bf16[1536,256]{1,0:T(8,128)(2,1)}, bf16[1536,256]{1,0:T(8,128)(2,1)}, u32[]{:S(2)}, u32[]{:S(2)}) collective-permute-start(bf16[1536,256]{1,0:T(8,128)(2,1)} %get-tuple-element.40), channel_id=1, source_target_pairs={{0,32},{1,33},{2,34},{3,35},{4,36},{5,37},{6,38},{7,39},{8,40},{9,... | collective-permute-start | bytes 2359304 | tf_op jit(solution)/shard_map/ppermute | solution.py:44
  58.8 42.7 %collective-permute-start.8 = (bf16[1536,256]{1,0:T(8,128)(2,1)}, bf16[1536,256]{1,0:T(8,128)(2,1)}, u32[]{:S(2)}, u32[]{:S(2)}) collective-permute-start(bf16[1536,256]{1,0:T(8,128)(2,1)} %get-tuple-element.40), channel_id=1, source_target_pairs={{0,96},{1,97},{2,98},{3,99},{4,100},{5,101},{6,102},{7,103},{8,104... | collective-permute-start | bytes 2359304 | tf_op jit(solution)/shard_map/ppermute | solution.py:44
  60.1 34.2 %collective-permute-start.13 = (bf16[1536,256]{1,0:T(8,128)(2,1)S(1)}, bf16[1536,256]{1,0:T(8,128)(2,1)S(1)}, u32[]{:S(2)}, u32[]{:S(2)}) collective-permute-start(bf16[1536,256]{1,0:T(8,128)(2,1)S(1)} %slice.100), channel_id=1, source_target_pairs={{0,96},{1,97},{2,98},{3,99},{4,100},{5,101},{6,102},{7,103},{8,104... | collective-permute-start | bytes 2359304 | tf_op jit(solution)/shard_map/ppermute | solution.py:44
  61.6 41.5 %collective-permute-start.10 = (bf16[1536,256]{1,0:T(8,128)(2,1)}, bf16[1536,256]{1,0:T(8,128)(2,1)}, u32[]{:S(2)}, u32[]{:S(2)}) collective-permute-start(bf16[1536,256]{1,0:T(8,128)(2,1)} %collective-permute-done.9.refs_0_), channel_id=1, source_target_pairs={{0,128},{1,129},{2,130},{3,131},{4,132},{5,133},{6,134},{7,135},{8... | collective-permute-start | bytes 2359304 | tf_op jit(solution)/shard_map/ppermute | solution.py:44
  64.1 50.3 %all-to-all-start = ((f16[8,72,256]{2,1,0:T(8,128)(2,1)}), f16[8,72,256]{2,1,0:T(8,128)(2,1)S(1)}, u32[]{:S(2)}, u32[]{:S(2)}) async-start(f16[8,72,256]{2,1,0:T(8,128)(2,1)} %pad_maximum_fusion.3), calls=%async_computation | async-start | bytes 589824 | tf_op jit(solution)/shard_map/all_to_all | solution.py:254
  94.3 28.9 %collective-permute-start.15 = (bf16[1536,256]{1,0:T(8,128)(2,1)}, bf16[1536,256]{1,0:T(8,128)(2,1)}, u32[]{:S(2)}, u32[]{:S(2)}) collective-permute-start(bf16[1536,256]{1,0:T(8,128)(2,1)} %get-tuple-element.39), channel_id=1, source_target_pairs={{0,32},{1,33},{2,34},{3,35},{4,36},{5,37},{6,38},{7,39},{8,40},{9,... | collective-permute-start | bytes 2359304 | tf_op jit(solution)/shard_map/ppermute | solution.py:44
  100.3 22.9 %collective-permute-start.16 = (bf16[1536,256]{1,0:T(8,128)(2,1)}, bf16[1536,256]{1,0:T(8,128)(2,1)}, u32[]{:S(2)}, u32[]{:S(2)}) collective-permute-start(bf16[1536,256]{1,0:T(8,128)(2,1)} %get-tuple-element.39), channel_id=1, source_target_pairs={{0,96},{1,97},{2,98},{3,99},{4,100},{5,101},{6,102},{7,103},{8,104... | collective-permute-start | bytes 2359304 | tf_op jit(solution)/shard_map/ppermute | solution.py:44
  101.5 11.0 %copy-start.4 = (f32[8,2,6,16,256]{4,3,2,1,0:T(8,128)S(1)}, f32[8,2,6,16,256]{4,3,2,1,0:T(8,128)}, u32[]{:S(2)}) copy-start(f32[8,2,6,16,256]{4,3,2,1,0:T(8,128)} %get-tuple-element.19) | copy-start | bytes 4718596
  101.5 20.4 %collective-permute-start.14 = (f32[8,2,2,16,256]{4,3,2,1,0:T(8,128)}, f32[8,2,2,16,256]{4,3,2,1,0:T(8,128)}, u32[]{:S(2)}, u32[]{:S(2)}) collective-permute-start(f32[8,2,2,16,256]{4,3,2,1,0:T(8,128)} %get-tuple-element.24), channel_id=1, source_target_pairs={{0,1},{1,0},{2,3},{3,2},{4,5},{5,4},{6,7},{7,6},{8,9},{9,8},{10,11... | collective-permute-start | bytes 1572872 | tf_op jit(solution)/shard_map/ppermute | solution.py:44
  103.1 22.3 %collective-permute-start.17 = (bf16[1536,256]{1,0:T(8,128)(2,1)}, bf16[1536,256]{1,0:T(8,128)(2,1)}, u32[]{:S(2)}, u32[]{:S(2)}) collective-permute-start(bf16[1536,256]{1,0:T(8,128)(2,1)} %copy-done.5), channel_id=1, source_target_pairs={{0,128},{1,129},{2,130},{3,131},{4,132},{5,133},{6,134},{7,135},{8... | collective-permute-start | bytes 2359304 | tf_op jit(solution)/shard_map/ppermute | solution.py:44
  111.4 19.5 %collective-permute-start.11 = (f32[8,2,3,16,256]{4,3,2,1,0:T(8,128)}, f32[8,2,3,16,256]{4,3,2,1,0:T(8,128)}, u32[]{:S(2)}, u32[]{:S(2)}) collective-permute-start(f32[8,2,3,16,256]{4,3,2,1,0:T(8,128)} %get-tuple-element.22), channel_id=1, source_target_pairs={{0,1},{1,0},{2,3},{3,2},{4,5},{5,4},{6,7},{7,6},{8,9},{9,8},{10,11... | collective-permute-start | bytes 2359304 | tf_op jit(solution)/shard_map/ppermute | solution.py:44
  113.2 8.7 %copy-start.8 = (f32[8,2,2,16,256]{4,3,2,1,0:T(8,128)S(1)}, f32[8,2,2,16,256]{4,3,2,1,0:T(8,128)}, u32[]{:S(2)}) copy-start(f32[8,2,2,16,256]{4,3,2,1,0:T(8,128)} %get-tuple-element.23) | copy-start | bytes 1572868
  114.4 31.9 %all-to-all-start.1 = ((f16[8,200,256]{2,1,0:T(8,128)(2,1)}), f16[8,200,256]{2,1,0:T(8,128)(2,1)S(1)}, u32[]{:S(2)}, u32[]{:S(2)}) async-start(f16[8,200,256]{2,1,0:T(8,128)(2,1)} %pad_maximum_fusion), calls=%async_computation.1 | async-start | bytes 1638400 | tf_op jit(solution)/shard_map/all_to_all | solution.py:254
  129.6 20.2 %collective-permute-start.18 = (f32[8,2,3,16,256]{4,3,2,1,0:T(8,128)}, f32[8,2,3,16,256]{4,3,2,1,0:T(8,128)S(1)}, u32[]{:S(2)}, u32[]{:S(2)}) collective-permute-start(f32[8,2,3,16,256]{4,3,2,1,0:T(8,128)} %get-tuple-element.26), channel_id=1, source_target_pairs={{0,1},{1,0},{2,3},{3,2},{4,5},{5,4},{6,7},{7,6},{8,9},{9,8},{10,11... | collective-permute-start | bytes 2359304 | tf_op jit(solution)/shard_map/ppermute | solution.py:44
  132.2 17.6 %copy-start.7 = (f32[8,2,3,16,256]{4,3,2,1,0:T(8,128)S(1)}, f32[8,2,3,16,256]{4,3,2,1,0:T(8,128)}, u32[]{:S(2)}) copy-start(f32[8,2,3,16,256]{4,3,2,1,0:T(8,128)} %get-tuple-element.25) | copy-start | bytes 2359300
  146.3 19.2 %all-to-all-start.2 = ((f16[8,104,256]{2,1,0:T(8,128)(2,1)}), f16[8,104,256]{2,1,0:T(8,128)(2,1)S(1)}, u32[]{:S(2)}, u32[]{:S(2)}) async-start(f16[8,104,256]{2,1,0:T(8,128)(2,1)} %pad_maximum_fusion.2), calls=%async_computation.2 | async-start | bytes 851968 | tf_op jit(solution)/shard_map/all_to_all | solution.py:254
  165.5 23.2 %all-to-all-start.3 = ((f16[16,88,256]{2,1,0:T(8,128)(2,1)}), f16[16,88,256]{2,1,0:T(8,128)(2,1)S(1)}, u32[]{:S(2)}, u32[]{:S(2)}) async-start(f16[16,88,256]{2,1,0:T(8,128)(2,1)} %pad_maximum_fusion.1), calls=%async_computation.3 | async-start | bytes 1441792 | tf_op jit(solution)/shard_map/all_to_all | solution.py:254
  170.0 20.6 %collective-permute-start.1 = (f32[2,16,256]{2,1,0:T(8,128)S(1)}, f32[2,16,256]{2,1,0:T(8,128)S(1)}, u32[]{:S(2)}, u32[]{:S(2)}) collective-permute-start(f32[2,16,256]{2,1,0:T(8,128)S(1)} %bitcast.40), channel_id=1, source_target_pairs={{0,2},{1,3},{2,0},{3,1},{4,6},{5,7},{6,4},{7,5},{8,10},{9,11},{10,... | collective-permute-start | bytes 98312 | tf_op jit(solution)/shard_map/ppermute | solution.py:44
  172.8 17.9 %collective-permute-start.6 = (f32[6,16,256]{2,1,0:T(8,128)S(1)}, f32[6,16,256]{2,1,0:T(8,128)S(1)}, u32[]{:S(2)}, u32[]{:S(2)}) collective-permute-start(f32[6,16,256]{2,1,0:T(8,128)S(1)} %bitcast.38), channel_id=1, source_target_pairs={{0,2},{1,3},{2,0},{3,1},{4,6},{5,7},{6,4},{7,5},{8,10},{9,11},{10,... | collective-permute-start | bytes 294920 | tf_op jit(solution)/shard_map/ppermute | solution.py:44
  174.0 16.7 %collective-permute-start.12 = (f32[3,16,256]{2,1,0:T(8,128)S(1)}, f32[3,16,256]{2,1,0:T(8,128)S(1)}, u32[]{:S(2)}, u32[]{:S(2)}) collective-permute-start(f32[3,16,256]{2,1,0:T(8,128)S(1)} %bitcast.39), channel_id=1, source_target_pairs={{0,2},{1,3},{2,0},{3,1},{4,6},{5,7},{6,4},{7,5},{8,10},{9,11},{10,... | collective-permute-start | bytes 147464 | tf_op jit(solution)/shard_map/ppermute | solution.py:44
  (10 other events, 32.1 us)

commit v6 on v5

--- a/solution.py
+++ b/solution.py
@@ -148,18 +148,24 @@
     )(*scalars, walk, *arrays)
 
 
-def squares(meta, ends):
+def squares(meta, ends, first, before=()):
     spots = [(p, half) for p, panel in enumerate(PANELS) for half in panel[2]]
     terms = [len(end) for end in ends]
+    last = bool(before)
 
     def body(meta, *refs):
-        sq_ref, sum_ref, row_ref = refs[sum(terms) :]
-        e = first = 0
+        olds, refs = refs[: len(before)], refs[len(before) :]
+        sq_ref, sum_ref = refs[sum(terms) : sum(terms) + 2]
+        row_ref = refs[-1] if last else sum_ref
+        if last:
+            sq_ref[...] = olds[0][...]
+            row_ref[...] = olds[1][...]
+        e, ref = first, 0
         for m in terms:
-            for j in range(refs[first].shape[0]):
-                x = refs[first][j]
+            for j in range(refs[ref].shape[0]):
+                x = refs[ref][j]
                 for k in range(1, m):
-                    x = x + refs[first + k][j]
+                    x = x + refs[ref + k][j]
                 x = x * x
                 p, half = spots[e]
                 at = pl.multiple_of(meta[p] * WIDTH + half * HALF, HALF)
@@ -168,21 +174,22 @@
                 row_ref[pl.ds(at // 128, 1)] = total[:, :128]
                 row_ref[pl.ds(at // 128 + 1, 1)] = total[:, 128:]
                 e += 1
-            first += m
-        sum_ref[...] = jnp.broadcast_to(row_ref[...][None], sum_ref.shape)
+            ref += m
+        if last:
+            sum_ref[...] = jnp.broadcast_to(row_ref[...][None], sum_ref.shape)
 
     whole = pl.BlockSpec(memory_space=pltpu.VMEM)
+    sums = jax.ShapeDtypeStruct((16, 32, 128) if last else (32, 128), F32)
     return pl.pallas_call(
         body,
-        out_shape=(jax.ShapeDtypeStruct((16, 4096), F32), jax.ShapeDtypeStruct((16, 32, 128), F32)),
+        out_shape=(jax.ShapeDtypeStruct((16, 4096), F32), sums),
         grid_spec=pltpu.PrefetchScalarGridSpec(
             num_scalar_prefetch=1,
-            in_specs=[whole] * sum(terms),
+            in_specs=[whole] * (len(before) + sum(terms)),
             out_specs=(whole, whole),
-            scratch_shapes=[pltpu.VMEM((32, 128), F32)],
+            scratch_shapes=[pltpu.VMEM((32, 128), F32)] if last else [],
         ),
-        name="squares",
-    )(meta, *itertools.chain(*ends))
+    )(meta, *before, *itertools.chain(*ends))
 
 
 def scaled(squared, sums):
@@ -256,23 +263,24 @@
         for total in sums:
             ends.append((total,) if both else (total[0], move(total[1], dxl=1)))
 
-    up = move(values, dy=1)
-    down = move(values, dy=3)
-    over = move(values, dxh=1)
-    far = [move(up[:, :HALF], dy=1), move(down[:, HALF:], dy=3)]
-    over_half = (over[:, :HALF], over[:, HALF:])
-    over_up = [move(over_half[t], dy=1) for t in range(2)]
-    over_down = [move(over_half[t], dy=3) for t in range(2)]
+    own = (values[:, :HALF], values[:, HALF:])
+    up = [move(own[t], dy=1) for t in range(2)]
+    down = [move(own[t], dy=3) for t in range(2)]
+    over = [move(own[t], dxh=1) for t in range(2)]
+    far = [move(up[0], dy=1), move(down[1], dy=3)]
+    over_up = [move(over[t], dy=1) for t in range(2)]
+    over_down = [move(over[t], dy=3) for t in range(2)]
     over_far = [move(far[t], dxh=1) for t in range(2)]
 
     exchange([partial(0, [whole(values)])])
-    exchange([partial(1, [whole(up), whole(down), whole(over)])])
+    exchange([partial(1, [pair(*up), pair(*down), pair(*over)])])
     exchange([partial(2, [one(over_up[0]), one(over_down[0]), one(over_far[0])])])
     last = [partial(3, [pair(*far)], both=True)]
     last.append(partial(4, [one(over_up[1]), one(over_down[1]), one(over_far[1])], both=True))
     exchange(last, both=True)
 
-    squared, sums = squares(meta, ends)
+    before = squares(meta, ends[:3], 0)
+    squared, sums = squares(meta, ends[3:], sum(end[0].shape[0] for end in ends[:3]), before)
     sums = jnp.sum(lax.all_to_all(sums, ("z", "xl"), 0, 0), axis=0)
     sums = lax.all_to_all(jnp.broadcast_to(sums[None], (16, 32, 128)), ("xh", "y", "core"), 0, 0)
     return scaled(squared, sums)

time: 227 us -> 223 us (0.982)
  waiting for transfers between devices: 94.1 us -> 78.9 us
  starting transfers between devices: 52.8 us -> 59.7 us
  Pallas kernels: 28.3 us -> 32.5 us
  local copies, waits for them, and re-layouts: 8.38 us -> 5.67 us
  other arithmetic: 11.8 us -> 14.1 us
    ppermute x19 -> x22, starting transfers between devices: 29.4 us -> 38.7 us  [send(): return lax.ppermute(x, AXES, moves(**by))]
    ppermute x19 -> x22, waiting for transfers between devices: 53.3 us -> 45.3 us  [send(): return lax.ppermute(x, AXES, moves(**by))]
    all_to_all x4, waiting for transfers between devices: 40.7 us -> 33.6 us  [exchange(): lax.all_to_all(encode(totals), ('z', 'xl') if both else 'z', 0, 0, tiled=...]
    reduce_max x5, other arithmetic: 2.94 us -> 5.4 us  [encode(): top = jnp.max(jnp.abs(total), axis=(*range(total.ndim - 3), total.ndim - 2))]
    all_to_all x4, starting transfers between devices: 23.4 us -> 21.1 us  [exchange(): lax.all_to_all(encode(totals), ('z', 'xl') if both else 'z', 0, 0, tiled=...]
    pallas_call x1 -> x2, Pallas kernels: 2.55 us -> 4.87 us  [squares(): pl.pallas_call(body, out_shape=(jax.ShapeDtypeStruct((16, 4096), F32), su...]
  transfers between devices with their start and end apart: 23 -> 26, of which waited for: 6 -> 10; matrix products, arithmetic and copies ran while one was open for 8% -> 7% of each run, Pallas kernels for 11% -> 9%
where the time goes in v6:
time: 223 us; the launch traced here: 222 us
  waiting for transfers between devices  78.9 us (35%)
  starting transfers between devices  59.7 us (27%)
  Pallas kernels  32.5 us (15%)
  blocking collectives  31 us (14%)
  other arithmetic  14.1 us (6%)
  local copies, waits for them, and re-layouts  5.67 us (3%)
    ppermute x22, waiting for transfers between devices, send(): return lax.ppermute(x, AXES, moves(**by))  45.3 us
    ppermute x22, starting transfers between devices, send(): return lax.ppermute(x, AXES, moves(**by))  38.7 us
    all_to_all x4, waiting for transfers between devices, exchange(): lax.all_to_all(encode(totals), ('z', 'xl') if both else 'z', 0, 0, tiled=...  33.6 us
    pallas_call x5, Pallas kernels, product(): pl.pallas_call(body, out_shape=(out, out), grid_spec=pltpu.PrefetchScalar...  25.9 us
    all_to_all x4, starting transfers between devices, exchange(): lax.all_to_all(encode(totals), ('z', 'xl') if both else 'z', 0, 0, tiled=...  21.1 us
    all_to_all x1, blocking collectives, pipeline(): lax.all_to_all(jnp.broadcast_to(sums[None], (16, 32, 128)), ('xh', 'y', '...  16.3 us
    all_to_all x1, blocking collectives, pipeline(): sums = jnp.sum(lax.all_to_all(sums, ('z', 'xl'), 0, 0), axis=0)  14.7 us
    reduce_max x5, other arithmetic, encode(): top = jnp.max(jnp.abs(total), axis=(*range(total.ndim - 3), total.ndim - 2))  5.4 us
  transfers between devices with their start and end apart: 26, of which 10 were waited for; matrix products, arithmetic and copies ran while one was open for 7% of the time, Pallas kernels for 9%

profile of v6, /device:TPU:1, one launch (start us, length us, event | category | flops | bytes accessed | tf_op | source)
XLA Modules:
  0.0 222.3 jit_solution(6614992985201828544)
XLA Ops:
  0.0 2.4 %fusion.41 = (bf16[1536,256]{1,0:T(8,128)(2,1)S(1)}, bf16[1536,256]{1,0:T(8,128)(2,1)}) fusion(bf16[1536,512]{1,0:T(8,128)(2,1)} %refs_0_.1), kind=kLoop, calls=%fused_computation.84 | loop fusion | bytes 3145728 | tf_op jit(solution)/shard_map/slice | solution.py:266
  2.4 2.1 collective-permute-start.2
  6.0 2.7 %collective-permute-start.5 = (bf16[1536,256]{1,0:T(8,128)(2,1)S(1)}, bf16[1536,256]{1,0:T(8,128)(2,1)}, u32[]{:S(2)}, u32[]{:S(2)}) collective-permute-start(bf16[1536,256]{1,0:T(8,128)(2,1)S(1)} %get-tuple-element.43), channel_id=1, source_target_pairs={{0,96},{1,97},{2,98},{3,99},{4,100},{5,101},{6,102},{7,103},{8,104... | collective-permute-start | bytes 2359304 | tf_op jit(solution)/shard_map/ppermute | solution.py:44
  8.7 2.7 %collective-permute-start.6 = (bf16[1536,256]{1,0:T(8,128)(2,1)}, bf16[1536,256]{1,0:T(8,128)(2,1)}, u32[]{:S(2)}, u32[]{:S(2)}) collective-permute-start(bf16[1536,256]{1,0:T(8,128)(2,1)} %get-tuple-element.44), channel_id=1, source_target_pairs={{0,128},{1,129},{2,130},{3,131},{4,132},{5,133},{6,134},{7,135},{8... | collective-permute-start | bytes 2359304 | tf_op jit(solution)/shard_map/ppermute | solution.py:44
  11.4 10.2 %collective-permute-done.2.refs_0_ = bf16[1536,256]{1,0:T(8,128)(2,1)S(1)} collective-permute-done((bf16[1536,256]{1,0:T(8,128)(2,1)}, bf16[1536,256]{1,0:T(8,128)(2,1)S(1)}, u32[]{:S(2)}, u32[]{:S(2)}) %collective-permute-start.2) | collective-permute-done | bytes 786464 | tf_op jit(solution)/shard_map/ppermute | solution.py:44
  21.6 4.3 %collective-permute-start.7 = (bf16[1536,256]{1,0:T(8,128)(2,1)S(1)}, bf16[1536,256]{1,0:T(8,128)(2,1)}, u32[]{:S(2)}, u32[]{:S(2)}) collective-permute-start(bf16[1536,256]{1,0:T(8,128)(2,1)S(1)} %get-tuple-element.43), channel_id=1, source_target_pairs={{0,128},{1,129},{2,130},{3,131},{4,132},{5,133},{6,134},{7,135},{8... | collective-permute-start | bytes 2359304 | tf_op jit(solution)/shard_map/ppermute | solution.py:44
  27.1 11.4 %collective-permute-done.3.refs_1_ = bf16[1536,256]{1,0:T(8,128)(2,1)S(1)} collective-permute-done((bf16[1536,256]{1,0:T(8,128)(2,1)S(1)}, bf16[1536,256]{1,0:T(8,128)(2,1)S(1)}, u32[]{:S(2)}, u32[]{:S(2)}) %collective-permute-start.3) | collective-permute-done | bytes 786464 | tf_op jit(solution)/shard_map/ppermute | solution.py:44
  39.7 4.4 %collective-permute-done.7.refs_5_ = bf16[1536,256]{1,0:T(8,128)(2,1)} collective-permute-done((bf16[1536,256]{1,0:T(8,128)(2,1)S(1)}, bf16[1536,256]{1,0:T(8,128)(2,1)}, u32[]{:S(2)}, u32[]{:S(2)}) %collective-permute-start.7) | collective-permute-done | bytes 786464 | tf_op jit(solution)/shard_map/ppermute | solution.py:44
  44.2 8.7 %shard_map.92 = (f32[8,2,6,16,256]{4,3,2,1,0:T(8,128)}, f32[8,2,6,16,256]{4,3,2,1,0:T(8,128)}) custom-call(s32[13]{0:T(128)} %select_add_fusion.meta, s32[24]{0:T(128)} %reshape.99.index, s32[8]{0:T(128)} %bitcast.41, bf16[512,4096]{1,0:T(8,128)(2,1)} %w_hbm.9, bf16[1536,256]{1,0:T(8,128)(2,1)} %copy-done.2, bf16[1536,256]{1,0:T(8,128)(2,1)} %copy-done.5, ...), custom_call_target="tpu_custom_call" | custom-call | tf_op jit(solution)/shard_map/pallas_call | solution.py:133
  53.4 3.5 %shard_map.91 = (f32[8,2,2,16,256]{4,3,2,1,0:T(8,128)}, f32[8,2,2,16,256]{4,3,2,1,0:T(8,128)}) custom-call(s32[13]{0:T(128)} %select_add_fusion.meta, s32[24]{0:T(128)} %reshape.99.index, s32[8]{0:T(128)} %bitcast.42, bf16[512,4096]{1,0:T(8,128)(2,1)} %w_hbm.9, bf16[1536,512]{1,0:T(8,128)(2,1)} %refs_0_.1), custom_call_target="tpu_custom_call" | custom-call | tf_op jit(solution)/shard_map/pallas_call | solution.py:133
  58.0 1.9 collective-permute-start.12
  63.2 2.0 collective-permute-start.11
  65.2 13.4 %collective-permute-done.12.refs_0_ = bf16[1536,256]{1,0:T(8,128)(2,1)} collective-permute-done((bf16[1536,256]{1,0:T(8,128)(2,1)S(1)}, bf16[1536,256]{1,0:T(8,128)(2,1)}, u32[]{:S(2)}, u32[]{:S(2)}) %collective-permute-start.12) | collective-permute-done | bytes 786464 | tf_op jit(solution)/shard_map/ppermute | solution.py:44
  78.7 4.5 %collective-permute-start.13 = (bf16[1536,256]{1,0:T(8,128)(2,1)}, bf16[1536,256]{1,0:T(8,128)(2,1)}, u32[]{:S(2)}, u32[]{:S(2)}) collective-permute-start(bf16[1536,256]{1,0:T(8,128)(2,1)} %collective-permute-done.12.refs_0_), channel_id=1, source_target_pairs={{0,128},{1,129},{2,130},{3,131},{4,132},{5,133},{6,134},{7,135},{8... | collective-permute-start | bytes 2359304 | tf_op jit(solution)/shard_map/ppermute | solution.py:44
  84.1 7.4 %all-to-all-start = ((f16[8,72,256]{2,1,0:T(8,128)(2,1)}), f16[8,72,256]{2,1,0:T(8,128)(2,1)S(1)}, u32[]{:S(2)}, u32[]{:S(2)}) async-start(f16[8,72,256]{2,1,0:T(8,128)(2,1)} %pad_maximum_fusion.3), calls=%async_computation | async-start | bytes 589824 | tf_op jit(solution)/shard_map/all_to_all | solution.py:261
  91.5 5.2 %shard_map.95 = (f32[8,2,2,16,256]{4,3,2,1,0:T(8,128)}, f32[8,2,2,16,256]{4,3,2,1,0:T(8,128)}) custom-call(s32[13]{0:T(128)} %select_add_fusion.meta, s32[24]{0:T(128)} %reshape.99.index, s32[8]{0:T(128)} %bitcast.43, bf16[512,4096]{1,0:T(8,128)(2,1)} %w_hbm.9, bf16[1536,256]{1,0:T(8,128)(2,1)} %collective-permute-done.12.refs_0_, ...), custom_call_target="tpu_custom_call" | custom-call | tf_op jit(solution)/shard_map/pallas_call | solution.py:133
  96.8 2.6 %collective-permute-start.17 = (f32[8,2,2,16,256]{4,3,2,1,0:T(8,128)}, f32[8,2,2,16,256]{4,3,2,1,0:T(8,128)}, u32[]{:S(2)}, u32[]{:S(2)}) collective-permute-start(f32[8,2,2,16,256]{4,3,2,1,0:T(8,128)} %get-tuple-element.28), channel_id=1, source_target_pairs={{0,1},{1,0},{2,3},{3,2},{4,5},{5,4},{6,7},{7,6},{8,9},{9,8},{10,11... | collective-permute-start | bytes 1572872 | tf_op jit(solution)/shard_map/ppermute | solution.py:44
  103.8 4.1 %shard_map.93 = (f32[8,2,3,16,256]{4,3,2,1,0:T(8,128)}, f32[8,2,3,16,256]{4,3,2,1,0:T(8,128)}) custom-call(s32[13]{0:T(128)} %select_add_fusion.meta, s32[24]{0:T(128)} %reshape.99.index, s32[8]{0:T(128)} %bitcast.44, bf16[512,4096]{1,0:T(8,128)(2,1)} %w_hbm.9, bf16[1536,256]{1,0:T(8,128)(2,1)} %collective-permute-done.10.refs_0_, ...), custom_call_target="tpu_custom_call" | custom-call | tf_op jit(solution)/shard_map/pallas_call | solution.py:133
  108.0 2.3 %collective-permute-start.14 = (f32[8,2,3,16,256]{4,3,2,1,0:T(8,128)}, f32[8,2,3,16,256]{4,3,2,1,0:T(8,128)S(1)}, u32[]{:S(2)}, u32[]{:S(2)}) collective-permute-start(f32[8,2,3,16,256]{4,3,2,1,0:T(8,128)} %get-tuple-element.24), channel_id=1, source_target_pairs={{0,1},{1,0},{2,3},{3,2},{4,5},{5,4},{6,7},{7,6},{8,9},{9,8},{10,11... | collective-permute-start | bytes 2359304 | tf_op jit(solution)/shard_map/ppermute | solution.py:44
  111.7 6.6 %all-to-all-start.1 = ((f16[8,200,256]{2,1,0:T(8,128)(2,1)}), f16[8,200,256]{2,1,0:T(8,128)(2,1)S(1)}, u32[]{:S(2)}, u32[]{:S(2)}) async-start(f16[8,200,256]{2,1,0:T(8,128)(2,1)} %pad_maximum_fusion), calls=%async_computation.1 | async-start | bytes 1638400 | tf_op jit(solution)/shard_map/all_to_all | solution.py:261
  119.7 2.7 %collective-permute-done.20.refs_2_ = bf16[1536,256]{1,0:T(8,128)(2,1)} collective-permute-done((bf16[1536,256]{1,0:T(8,128)(2,1)}, bf16[1536,256]{1,0:T(8,128)(2,1)}, u32[]{:S(2)}, u32[]{:S(2)}) %collective-permute-start.20) | collective-permute-done | bytes 786464 | tf_op jit(solution)/shard_map/ppermute | solution.py:44
  122.3 4.4 %shard_map.96 = (f32[8,2,3,16,256]{4,3,2,1,0:T(8,128)}, f32[8,2,3,16,256]{4,3,2,1,0:T(8,128)}) custom-call(s32[13]{0:T(128)} %select_add_fusion.meta, s32[24]{0:T(128)} %reshape.99.index, s32[8]{0:T(128)} %bitcast.45, bf16[512,4096]{1,0:T(8,128)(2,1)} %w_hbm.9, bf16[1536,256]{1,0:T(8,128)(2,1)} %collective-permute-done.18.refs_0_, ...), custom_call_target="tpu_custom_call" | custom-call | tf_op jit(solution)/shard_map/pallas_call | solution.py:133
  126.7 2.9 %collective-permute-start.21 = (f32[8,2,3,16,256]{4,3,2,1,0:T(8,128)}, f32[8,2,3,16,256]{4,3,2,1,0:T(8,128)}, u32[]{:S(2)}, u32[]{:S(2)}) collective-permute-start(f32[8,2,3,16,256]{4,3,2,1,0:T(8,128)} %get-tuple-element.30), channel_id=1, source_target_pairs={{0,1},{1,0},{2,3},{3,2},{4,5},{5,4},{6,7},{7,6},{8,9},{9,8},{10,11... | collective-permute-start | bytes 2359304 | tf_op jit(solution)/shard_map/ppermute | solution.py:44
  130.8 11.9 %all-to-all-done.1 = f16[8,200,256]{2,1,0:T(8,128)(2,1)S(1)} async-done(((f16[8,200,256]{2,1,0:T(8,128)(2,1)}), f16[8,200,256]{2,1,0:T(8,128)(2,1)S(1)}, u32[]{:S(2)}, u32[]{:S(2)}) %all-to-all-start.1) | async-done | bytes 819232 | tf_op jit(solution)/shard_map/all_to_all | solution.py:261
  142.7 3.5 %all-to-all-start.2 = ((f16[8,104,256]{2,1,0:T(8,128)(2,1)}), f16[8,104,256]{2,1,0:T(8,128)(2,1)S(1)}, u32[]{:S(2)}, u32[]{:S(2)}) async-start(f16[8,104,256]{2,1,0:T(8,128)(2,1)} %pad_maximum_fusion.2), calls=%async_computation.2 | async-start | bytes 851968 | tf_op jit(solution)/shard_map/all_to_all | solution.py:261
  148.7 13.2 %all-to-all-done.2 = f16[8,104,256]{2,1,0:T(8,128)(2,1)S(1)} async-done(((f16[8,104,256]{2,1,0:T(8,128)(2,1)}), f16[8,104,256]{2,1,0:T(8,128)(2,1)S(1)}, u32[]{:S(2)}, u32[]{:S(2)}) %all-to-all-start.2) | async-done | bytes 426016 | tf_op jit(solution)/shard_map/all_to_all | solution.py:261
  161.9 3.6 %all-to-all-start.3 = ((f16[16,88,256]{2,1,0:T(8,128)(2,1)}), f16[16,88,256]{2,1,0:T(8,128)(2,1)S(1)}, u32[]{:S(2)}, u32[]{:S(2)}) async-start(f16[16,88,256]{2,1,0:T(8,128)(2,1)} %pad_maximum_fusion.1), calls=%async_computation.3 | async-start | bytes 1441792 | tf_op jit(solution)/shard_map/all_to_all | solution.py:261
  174.2 2.4 %shard_map.94 = (f32[16,4096]{1,0:T(8,128)}, f32[32,128]{1,0:T(8,128)}) custom-call(s32[13]{0:T(128)} %select_add_fusion.meta, f32[2,16,256]{2,1,0:T(8,128)} %bitcast.37, f32[2,16,256]{2,1,0:T(8,128)} %copy-done.11, f32[6,16,256]{2,1,0:T(8,128)} %bitcast.31, f32[6,16,256]{2,1,0:T(8,128)} %copy-done.9, f32[3,16,256]{2,1,0:T(8,128)} %bitcast.33, ...), custom_call_target="tpu_custom_call" | custom-call | tf_op jit(solution)/shard_map/pallas_call | solution.py:183
  176.6 8.5 %all-to-all-done.3 = f16[16,88,256]{2,1,0:T(8,128)(2,1)S(1)} async-done(((f16[16,88,256]{2,1,0:T(8,128)(2,1)}), f16[16,88,256]{2,1,0:T(8,128)(2,1)S(1)}, u32[]{:S(2)}, u32[]{:S(2)}) %all-to-all-start.3) | async-done | bytes 720928 | tf_op jit(solution)/shard_map/all_to_all | solution.py:261
  187.1 2.5 %shard_map.97 = (f32[16,4096]{1,0:T(8,128)}, f32[16,32,128]{2,1,0:T(8,128)}) custom-call(s32[13]{0:T(128)} %select_add_fusion.meta, f32[16,4096]{1,0:T(8,128)} %get-tuple-element.25.refs_0_, f32[32,128]{1,0:T(8,128)} %get-tuple-element.26.refs_1_, f32[2,16,256]{2,1,0:T(8,128)} %bitcast.36, f32[3,16,256]{2,1,0:T(8,128)} %bitcast.34), custom_call_target="tpu_custom_call" | custom-call | tf_op jit(solution)/shard_map/pallas_call | solution.py:183
  189.5 14.7 %all_to_all.30 = f32[16,32,128]{2,1,0:T(8,128)S(1)} all-to-all(f32[16,32,128]{2,1,0:T(8,128)} %get-tuple-element.32), channel_id=1, replica_groups=mesh['xh'=2,'y'=4,'z'=8,'xl'=2,'core'=2] {'z','xl'}, dimensions={0} | all-to-all | bytes 524288 | tf_op jit(solution)/shard_map/all_to_all | solution.py:284
  204.3 16.3 %all_to_all.31.sum_ref = f32[16,32,128]{2,1,0:T(8,128)} all-to-all(f32[16,32,128]{2,1,0:T(8,128)S(1)} %broadcast_in_dim.14), channel_id=1, replica_groups=mesh['xh'=2,'y'=4,'z'=8,'xl'=2,'core'=2] {'xh','y','core'}, dimensions={0} | all-to-all | bytes 524288 | tf_op jit(solution)/shard_map/all_to_all | solution.py:285
  (113 shorter events, 32.9 us)
Async XLA Ops:
  0.0 26.6 %copy-start.13 = (pred[13]{0:T(512)(128)(4,1)S(1)}, pred[13]{0:T(512)(128)(4,1)}, u32[]{:S(2)}) copy-start(pred[13]{0:T(512)(128)(4,1)} %constant.41.clone) | copy-start | bytes 43
  0.0 26.6 %copy-start.14 = (pred[13]{0:T(512)(128)(4,1)S(1)}, pred[13]{0:T(512)(128)(4,1)}, u32[]{:S(2)}) copy-start(pred[13]{0:T(512)(128)(4,1)} %constant.40.clone) | copy-start | bytes 43
  0.0 26.6 %copy-start.15 = (s32[13]{0:T(128)S(1)}, s32[13]{0:T(128)}, u32[]{:S(2)}) copy-start(s32[13]{0:T(128)} %constant.39.clone) | copy-start | bytes 160
  0.0 26.6 %copy-start.16 = (s32[13]{0:T(128)S(1)}, s32[13]{0:T(128)}, u32[]{:S(2)}) copy-start(s32[13]{0:T(128)} %constant.38.clone) | copy-start | bytes 160
  0.0 26.5 %copy-start.17 = (s32[13]{0:T(128)S(1)}, s32[13]{0:T(128)}, u32[]{:S(2)}) copy-start(s32[13]{0:T(128)} %constant.37.clone) | copy-start | bytes 160
  0.0 25.9 %copy-start.12 = (s32[3,8]{1,0:T(4,128)S(1)}, s32[3,8]{1,0:T(4,128)}, u32[]{:S(2)}) copy-start(s32[3,8]{1,0:T(4,128)} %param.11) | copy-start | bytes 292
  2.4 19.2 %collective-permute-start.2 = (bf16[1536,256]{1,0:T(8,128)(2,1)}, bf16[1536,256]{1,0:T(8,128)(2,1)S(1)}, u32[]{:S(2)}, u32[]{:S(2)}) collective-permute-start(bf16[1536,256]{1,0:T(8,128)(2,1)} %get-tuple-element.44), channel_id=1, source_target_pairs={{0,32},{1,33},{2,34},{3,35},{4,36},{5,37},{6,38},{7,39},{8,40},{9,... | collective-permute-start | bytes 2359304 | tf_op jit(solution)/shard_map/ppermute | solution.py:44
  4.5 33.9 %collective-permute-start.4 = (bf16[1536,256]{1,0:T(8,128)(2,1)}, bf16[1536,256]{1,0:T(8,128)(2,1)S(1)}, u32[]{:S(2)}, u32[]{:S(2)}) collective-permute-start(bf16[1536,256]{1,0:T(8,128)(2,1)} %get-tuple-element.44), channel_id=1, source_target_pairs={{0,96},{1,97},{2,98},{3,99},{4,100},{5,101},{6,102},{7,103},{8,104... | collective-permute-start | bytes 2359304 | tf_op jit(solution)/shard_map/ppermute | solution.py:44
  6.0 32.5 %collective-permute-start.3 = (bf16[1536,256]{1,0:T(8,128)(2,1)S(1)}, bf16[1536,256]{1,0:T(8,128)(2,1)S(1)}, u32[]{:S(2)}, u32[]{:S(2)}) collective-permute-start(bf16[1536,256]{1,0:T(8,128)(2,1)S(1)} %get-tuple-element.43), channel_id=1, source_target_pairs={{0,32},{1,33},{2,34},{3,35},{4,36},{5,37},{6,38},{7,39},{8,40},{9,... | collective-permute-start | bytes 2359304 | tf_op jit(solution)/shard_map/ppermute | solution.py:44
  6.0 33.7 %collective-permute-start.5 = (bf16[1536,256]{1,0:T(8,128)(2,1)S(1)}, bf16[1536,256]{1,0:T(8,128)(2,1)}, u32[]{:S(2)}, u32[]{:S(2)}) collective-permute-start(bf16[1536,256]{1,0:T(8,128)(2,1)S(1)} %get-tuple-element.43), channel_id=1, source_target_pairs={{0,96},{1,97},{2,98},{3,99},{4,100},{5,101},{6,102},{7,103},{8,104... | collective-permute-start | bytes 2359304 | tf_op jit(solution)/shard_map/ppermute | solution.py:44
  8.7 31.1 %collective-permute-start.6 = (bf16[1536,256]{1,0:T(8,128)(2,1)}, bf16[1536,256]{1,0:T(8,128)(2,1)}, u32[]{:S(2)}, u32[]{:S(2)}) collective-permute-start(bf16[1536,256]{1,0:T(8,128)(2,1)} %get-tuple-element.44), channel_id=1, source_target_pairs={{0,128},{1,129},{2,130},{3,131},{4,132},{5,133},{6,134},{7,135},{8... | collective-permute-start | bytes 2359304 | tf_op jit(solution)/shard_map/ppermute | solution.py:44
  21.6 22.5 %collective-permute-start.7 = (bf16[1536,256]{1,0:T(8,128)(2,1)S(1)}, bf16[1536,256]{1,0:T(8,128)(2,1)}, u32[]{:S(2)}, u32[]{:S(2)}) collective-permute-start(bf16[1536,256]{1,0:T(8,128)(2,1)S(1)} %get-tuple-element.43), channel_id=1, source_target_pairs={{0,128},{1,129},{2,130},{3,131},{4,132},{5,133},{6,134},{7,135},{8... | collective-permute-start | bytes 2359304 | tf_op jit(solution)/shard_map/ppermute | solution.py:44
  52.8 43.9 %collective-permute-start.8 = (f32[8,2,6,16,256]{4,3,2,1,0:T(8,128)}, f32[8,2,6,16,256]{4,3,2,1,0:T(8,128)S(1)}, u32[]{:S(2)}, u32[]{:S(2)}) collective-permute-start(f32[8,2,6,16,256]{4,3,2,1,0:T(8,128)} %get-tuple-element.22), channel_id=1, source_target_pairs={{0,1},{1,0},{2,3},{3,2},{4,5},{5,4},{6,7},{7,6},{8,9},{9,8},{10,11... | collective-permute-start | bytes 4718600 | tf_op jit(solution)/shard_map/ppermute | solution.py:44
  56.9 4.5 %collective-permute-start = (f32[8,2,2,16,256]{4,3,2,1,0:T(8,128)}, f32[8,2,2,16,256]{4,3,2,1,0:T(8,128)S(1)}, u32[]{:S(2)}, u32[]{:S(2)}) collective-permute-start(f32[8,2,2,16,256]{4,3,2,1,0:T(8,128)} %get-tuple-element.20), channel_id=1, source_target_pairs={{0,1},{1,0},{2,3},{3,2},{4,5},{5,4},{6,7},{7,6},{8,9},{9,8},{10,11... | collective-permute-start | bytes 1572872 | tf_op jit(solution)/shard_map/ppermute | solution.py:44
  58.0 20.6 %collective-permute-start.12 = (bf16[1536,256]{1,0:T(8,128)(2,1)S(1)}, bf16[1536,256]{1,0:T(8,128)(2,1)}, u32[]{:S(2)}, u32[]{:S(2)}) collective-permute-start(bf16[1536,256]{1,0:T(8,128)(2,1)S(1)} %copy-done.3), channel_id=1, source_target_pairs={{0,32},{1,33},{2,34},{3,35},{4,36},{5,37},{6,38},{7,39},{8,40},{9,... | collective-permute-start | bytes 2359304 | tf_op jit(solution)/shard_map/ppermute | solution.py:44
  60.0 31.5 %collective-permute-start.16 = (bf16[1536,256]{1,0:T(8,128)(2,1)}, bf16[1536,256]{1,0:T(8,128)(2,1)}, u32[]{:S(2)}, u32[]{:S(2)}) collective-permute-start(bf16[1536,256]{1,0:T(8,128)(2,1)} %collective-permute-done.5.refs_3_), channel_id=1, source_target_pairs={{0,96},{1,97},{2,98},{3,99},{4,100},{5,101},{6,102},{7,103},{8,104... | collective-permute-start | bytes 2359304 | tf_op jit(solution)/shard_map/ppermute | solution.py:44
  62.5 38.7 %collective-permute-start.10 = (bf16[1536,256]{1,0:T(8,128)(2,1)}, bf16[1536,256]{1,0:T(8,128)(2,1)}, u32[]{:S(2)}, u32[]{:S(2)}) collective-permute-start(bf16[1536,256]{1,0:T(8,128)(2,1)} %collective-permute-done.6.refs_4_), channel_id=1, source_target_pairs={{0,32},{1,33},{2,34},{3,35},{4,36},{5,37},{6,38},{7,39},{8,40},{9,... | collective-permute-start | bytes 2359304 | tf_op jit(solution)/shard_map/ppermute | solution.py:44
  63.2 39.6 %collective-permute-start.11 = (bf16[1536,256]{1,0:T(8,128)(2,1)}, bf16[1536,256]{1,0:T(8,128)(2,1)}, u32[]{:S(2)}, u32[]{:S(2)}) collective-permute-start(bf16[1536,256]{1,0:T(8,128)(2,1)} %collective-permute-done.6.refs_4_), channel_id=1, source_target_pairs={{0,96},{1,97},{2,98},{3,99},{4,100},{5,101},{6,102},{7,103},{8,104... | collective-permute-start | bytes 2359304 | tf_op jit(solution)/shard_map/ppermute | solution.py:44
  78.7 25.2 %collective-permute-start.13 = (bf16[1536,256]{1,0:T(8,128)(2,1)}, bf16[1536,256]{1,0:T(8,128)(2,1)}, u32[]{:S(2)}, u32[]{:S(2)}) collective-permute-start(bf16[1536,256]{1,0:T(8,128)(2,1)} %collective-permute-done.12.refs_0_), channel_id=1, source_target_pairs={{0,128},{1,129},{2,130},{3,131},{4,132},{5,133},{6,134},{7,135},{8... | collective-permute-start | bytes 2359304 | tf_op jit(solution)/shard_map/ppermute | solution.py:44
  84.1 27.7 %all-to-all-start = ((f16[8,72,256]{2,1,0:T(8,128)(2,1)}), f16[8,72,256]{2,1,0:T(8,128)(2,1)S(1)}, u32[]{:S(2)}, u32[]{:S(2)}) async-start(f16[8,72,256]{2,1,0:T(8,128)(2,1)} %pad_maximum_fusion.3), calls=%async_computation | async-start | bytes 589824 | tf_op jit(solution)/shard_map/all_to_all | solution.py:261
  91.5 28.2 %collective-permute-start.18 = (bf16[1536,256]{1,0:T(8,128)(2,1)}, bf16[1536,256]{1,0:T(8,128)(2,1)}, u32[]{:S(2)}, u32[]{:S(2)}) collective-permute-start(bf16[1536,256]{1,0:T(8,128)(2,1)} %collective-permute-done.7.refs_5_), channel_id=1, source_target_pairs={{0,32},{1,33},{2,34},{3,35},{4,36},{5,37},{6,38},{7,39},{8,40},{9,... | collective-permute-start | bytes 2359304 | tf_op jit(solution)/shard_map/ppermute | solution.py:44
  96.8 21.6 %collective-permute-start.17 = (f32[8,2,2,16,256]{4,3,2,1,0:T(8,128)}, f32[8,2,2,16,256]{4,3,2,1,0:T(8,128)}, u32[]{:S(2)}, u32[]{:S(2)}) collective-permute-start(f32[8,2,2,16,256]{4,3,2,1,0:T(8,128)} %get-tuple-element.28), channel_id=1, source_target_pairs={{0,1},{1,0},{2,3},{3,2},{4,5},{5,4},{6,7},{7,6},{8,9},{9,8},{10,11... | collective-permute-start | bytes 1572872 | tf_op jit(solution)/shard_map/ppermute | solution.py:44
  101.2 18.4 %collective-permute-start.19 = (bf16[1536,256]{1,0:T(8,128)(2,1)}, bf16[1536,256]{1,0:T(8,128)(2,1)}, u32[]{:S(2)}, u32[]{:S(2)}) collective-permute-start(bf16[1536,256]{1,0:T(8,128)(2,1)} %collective-permute-done.7.refs_5_), channel_id=1, source_target_pairs={{0,96},{1,97},{2,98},{3,99},{4,100},{5,101},{6,102},{7,103},{8,104... | collective-permute-start | bytes 2359304 | tf_op jit(solution)/shard_map/ppermute | solution.py:44
  102.7 19.6 %collective-permute-start.20 = (bf16[1536,256]{1,0:T(8,128)(2,1)}, bf16[1536,256]{1,0:T(8,128)(2,1)}, u32[]{:S(2)}, u32[]{:S(2)}) collective-permute-start(bf16[1536,256]{1,0:T(8,128)(2,1)} %collective-permute-done.16.refs_1_), channel_id=1, source_target_pairs={{0,128},{1,129},{2,130},{3,131},{4,132},{5,133},{6,134},{7,135},{8... | collective-permute-start | bytes 2359304 | tf_op jit(solution)/shard_map/ppermute | solution.py:44
  108.0 21.6 %collective-permute-start.14 = (f32[8,2,3,16,256]{4,3,2,1,0:T(8,128)}, f32[8,2,3,16,256]{4,3,2,1,0:T(8,128)S(1)}, u32[]{:S(2)}, u32[]{:S(2)}) collective-permute-start(f32[8,2,3,16,256]{4,3,2,1,0:T(8,128)} %get-tuple-element.24), channel_id=1, source_target_pairs={{0,1},{1,0},{2,3},{3,2},{4,5},{5,4},{6,7},{7,6},{8,9},{9,8},{10,11... | collective-permute-start | bytes 2359304 | tf_op jit(solution)/shard_map/ppermute | solution.py:44
  111.7 31.0 %all-to-all-start.1 = ((f16[8,200,256]{2,1,0:T(8,128)(2,1)}), f16[8,200,256]{2,1,0:T(8,128)(2,1)S(1)}, u32[]{:S(2)}, u32[]{:S(2)}) async-start(f16[8,200,256]{2,1,0:T(8,128)(2,1)} %pad_maximum_fusion), calls=%async_computation.1 | async-start | bytes 1638400 | tf_op jit(solution)/shard_map/all_to_all | solution.py:261
  126.7 19.4 %collective-permute-start.21 = (f32[8,2,3,16,256]{4,3,2,1,0:T(8,128)}, f32[8,2,3,16,256]{4,3,2,1,0:T(8,128)}, u32[]{:S(2)}, u32[]{:S(2)}) collective-permute-start(f32[8,2,3,16,256]{4,3,2,1,0:T(8,128)} %get-tuple-element.30), channel_id=1, source_target_pairs={{0,1},{1,0},{2,3},{3,2},{4,5},{5,4},{6,7},{7,6},{8,9},{9,8},{10,11... | collective-permute-start | bytes 2359304 | tf_op jit(solution)/shard_map/ppermute | solution.py:44
  142.7 19.2 %all-to-all-start.2 = ((f16[8,104,256]{2,1,0:T(8,128)(2,1)}), f16[8,104,256]{2,1,0:T(8,128)(2,1)S(1)}, u32[]{:S(2)}, u32[]{:S(2)}) async-start(f16[8,104,256]{2,1,0:T(8,128)(2,1)} %pad_maximum_fusion.2), calls=%async_computation.2 | async-start | bytes 851968 | tf_op jit(solution)/shard_map/all_to_all | solution.py:261
  161.9 23.2 %all-to-all-start.3 = ((f16[16,88,256]{2,1,0:T(8,128)(2,1)}), f16[16,88,256]{2,1,0:T(8,128)(2,1)S(1)}, u32[]{:S(2)}, u32[]{:S(2)}) async-start(f16[16,88,256]{2,1,0:T(8,128)(2,1)} %pad_maximum_fusion.1), calls=%async_computation.3 | async-start | bytes 1441792 | tf_op jit(solution)/shard_map/all_to_all | solution.py:261
  167.4 6.2 %collective-permute-start.9 = (f32[6,16,256]{2,1,0:T(8,128)S(1)}, f32[6,16,256]{2,1,0:T(8,128)S(1)}, u32[]{:S(2)}, u32[]{:S(2)}) collective-permute-start(f32[6,16,256]{2,1,0:T(8,128)S(1)} %bitcast.38), channel_id=1, source_target_pairs={{0,2},{1,3},{2,0},{3,1},{4,6},{5,7},{6,4},{7,5},{8,10},{9,11},{10,... | collective-permute-start | bytes 294920 | tf_op jit(solution)/shard_map/ppermute | solution.py:44
  169.6 3.9 %collective-permute-start.15 = (f32[3,16,256]{2,1,0:T(8,128)S(1)}, f32[3,16,256]{2,1,0:T(8,128)S(1)}, u32[]{:S(2)}, u32[]{:S(2)}) collective-permute-start(f32[3,16,256]{2,1,0:T(8,128)S(1)} %bitcast.39), channel_id=1, source_target_pairs={{0,2},{1,3},{2,0},{3,1},{4,6},{5,7},{6,4},{7,5},{8,10},{9,11},{10,... | collective-permute-start | bytes 147464 | tf_op jit(solution)/shard_map/ppermute | solution.py:44
  170.5 3.1 %collective-permute-start.1 = (f32[2,16,256]{2,1,0:T(8,128)S(1)}, f32[2,16,256]{2,1,0:T(8,128)S(1)}, u32[]{:S(2)}, u32[]{:S(2)}) collective-permute-start(f32[2,16,256]{2,1,0:T(8,128)S(1)} %bitcast.40), channel_id=1, source_target_pairs={{0,2},{1,3},{2,0},{3,1},{4,6},{5,7},{6,4},{7,5},{8,10},{9,11},{10,... | collective-permute-start | bytes 98312 | tf_op jit(solution)/shard_map/ppermute | solution.py:44
  (12 other events, 85.8 us)

commit v7 on v6

--- a/solution.py
+++ b/solution.py
@@ -263,7 +263,7 @@
         for total in sums:
             ends.append((total,) if both else (total[0], move(total[1], dxl=1)))
 
-    own = (values[:, :HALF], values[:, HALF:])
+    own = (values[:, :HALF], lax.optimization_barrier(values)[:, HALF:])
     up = [move(own[t], dy=1) for t in range(2)]
     down = [move(own[t], dy=3) for t in range(2)]
     over = [move(own[t], dxh=1) for t in range(2)]
@@ -274,13 +274,12 @@
 
     exchange([partial(0, [whole(values)])])
     exchange([partial(1, [pair(*up), pair(*down), pair(*over)])])
-    exchange([partial(2, [one(over_up[0]), one(over_down[0]), one(over_far[0])])])
-    last = [partial(3, [pair(*far)], both=True)]
-    last.append(partial(4, [one(over_up[1]), one(over_down[1]), one(over_far[1])], both=True))
-    exchange(last, both=True)
-
-    before = squares(meta, ends[:3], 0)
-    squared, sums = squares(meta, ends[3:], sum(end[0].shape[0] for end in ends[:3]), before)
+    third = partial(3, [pair(*far)])
+    exchange([partial(2, [one(over_up[0]), one(over_down[0]), one(over_far[0])]), third])
+    exchange([partial(4, [one(over_up[1]), one(over_down[1]), one(over_far[1])], both=True)], both=True)
+
+    before = squares(meta, ends[:4], 0)
+    squared, sums = squares(meta, ends[4:], sum(end[0].shape[0] for end in ends[:4]), before)
     sums = jnp.sum(lax.all_to_all(sums, ("z", "xl"), 0, 0), axis=0)
     sums = lax.all_to_all(jnp.broadcast_to(sums[None], (16, 32, 128)), ("xh", "y", "core"), 0, 0)
     return scaled(squared, sums)

time: 223 us -> 239 us (1.072)
  waiting for transfers between devices: 78.9 us -> 93.9 us
    all_to_all x4, waiting for transfers between devices: 33.6 us -> 43.8 us  [exchange(): lax.all_to_all(encode(totals), ('z', 'xl') if both else 'z', 0, 0, tiled=...]
    ppermute x22 -> x23, waiting for transfers between devices: 45.3 us -> 50.1 us  [send(): return lax.ppermute(x, AXES, moves(**by))]
    ppermute x22 -> x23, starting transfers between devices: 38.7 us -> 35.7 us  [send(): return lax.ppermute(x, AXES, moves(**by))]
  transfers between devices with their start and end apart: 26 -> 27, of which waited for: 10 -> 12; matrix products, arithmetic and copies ran while one was open for 7% -> 7% of each run, Pallas kernels for 9% -> 7%
where the time goes in v7:
time: 239 us; the launch traced here: 238 us
  waiting for transfers between devices  93.9 us (39%)
  starting transfers between devices  59.1 us (25%)
  Pallas kernels  32.5 us (14%)
  blocking collectives  32.4 us (14%)
  other arithmetic  13 us (5%)
  local copies, waits for them, and re-layouts  6.89 us (3%)
    ppermute x23, waiting for transfers between devices, send(): return lax.ppermute(x, AXES, moves(**by))  50.1 us
    all_to_all x4, waiting for transfers between devices, exchange(): lax.all_to_all(encode(totals), ('z', 'xl') if both else 'z', 0, 0, tiled=...  43.8 us
    ppermute x23, starting transfers between devices, send(): return lax.ppermute(x, AXES, moves(**by))  35.7 us
    pallas_call x5, Pallas kernels, product(): pl.pallas_call(body, out_shape=(out, out), grid_spec=pltpu.PrefetchScalar...  25.9 us
    all_to_all x4, starting transfers between devices, exchange(): lax.all_to_all(encode(totals), ('z', 'xl') if both else 'z', 0, 0, tiled=...  23.4 us
    all_to_all x1, blocking collectives, pipeline(): lax.all_to_all(jnp.broadcast_to(sums[None], (16, 32, 128)), ('xh', 'y', '...  18.5 us
    all_to_all x1, blocking collectives, pipeline(): sums = jnp.sum(lax.all_to_all(sums, ('z', 'xl'), 0, 0), axis=0)  13.9 us
    pallas_call x2, Pallas kernels, squares(): pl.pallas_call(body, out_shape=(jax.ShapeDtypeStruct((16, 4096), F32), su...  4.89 us
  transfers between devices with their start and end apart: 27, of which 12 were waited for; matrix products, arithmetic and copies ran while one was open for 7% of the time, Pallas kernels for 7%

profile of v7, /device:TPU:1, one launch (start us, length us, event | category | flops | bytes accessed | tf_op | source)
XLA Modules:
  0.0 238.3 jit_solution(13305211905197005651)
XLA Ops:
  0.0 2.1 slice.72
  2.2 2.1 collective-permute-start.2
  5.5 3.6 %shard_map.91 = (f32[8,2,2,16,256]{4,3,2,1,0:T(8,128)}, f32[8,2,2,16,256]{4,3,2,1,0:T(8,128)}) custom-call(s32[13]{0:T(128)} %select_add_fusion.meta, s32[24]{0:T(128)} %reshape.100.index, s32[8]{0:T(128)} %bitcast.41, bf16[512,4096]{1,0:T(8,128)(2,1)} %w_hbm.9, bf16[1536,512]{1,0:T(8,128)(2,1)} %refs_0_.1), custom_call_target="tpu_custom_call" | custom-call | tf_op jit(solution)/shard_map/pallas_call | solution.py:133
  13.3 2.7 %collective-permute-start.5 = (bf16[1536,256]{1,0:T(8,128)(2,1)S(1)}, bf16[1536,256]{1,0:T(8,128)(2,1)S(1)}, u32[]{:S(2)}, u32[]{:S(2)}) collective-permute-start(bf16[1536,256]{1,0:T(8,128)(2,1)S(1)} %slice.92), channel_id=1, source_target_pairs={{0,96},{1,97},{2,98},{3,99},{4,100},{5,101},{6,102},{7,103},{8,104... | collective-permute-start | bytes 2359304 | tf_op jit(solution)/shard_map/ppermute | solution.py:44
  17.1 4.2 %collective-permute-done.2.refs_0_ = bf16[1536,256]{1,0:T(8,128)(2,1)S(1)} collective-permute-done((bf16[1536,256]{1,0:T(8,128)(2,1)}, bf16[1536,256]{1,0:T(8,128)(2,1)S(1)}, u32[]{:S(2)}, u32[]{:S(2)}) %collective-permute-start.2) | collective-permute-done | bytes 786464 | tf_op jit(solution)/shard_map/ppermute | solution.py:44
  21.3 4.4 %collective-permute-start.7 = (bf16[1536,256]{1,0:T(8,128)(2,1)S(1)}, bf16[1536,256]{1,0:T(8,128)(2,1)}, u32[]{:S(2)}, u32[]{:S(2)}) collective-permute-start(bf16[1536,256]{1,0:T(8,128)(2,1)S(1)} %slice.92), channel_id=1, source_target_pairs={{0,128},{1,129},{2,130},{3,131},{4,132},{5,133},{6,134},{7,135},{8... | collective-permute-start | bytes 2359304 | tf_op jit(solution)/shard_map/ppermute | solution.py:44
  25.8 12.4 %collective-permute-done.3.refs_1_ = bf16[1536,256]{1,0:T(8,128)(2,1)S(1)} collective-permute-done((bf16[1536,256]{1,0:T(8,128)(2,1)S(1)}, bf16[1536,256]{1,0:T(8,128)(2,1)S(1)}, u32[]{:S(2)}, u32[]{:S(2)}) %collective-permute-start.3) | collective-permute-done | bytes 786464 | tf_op jit(solution)/shard_map/ppermute | solution.py:44
  38.2 9.1 %collective-permute-done.5.refs_3_ = bf16[1536,256]{1,0:T(8,128)(2,1)S(1)} collective-permute-done((bf16[1536,256]{1,0:T(8,128)(2,1)S(1)}, bf16[1536,256]{1,0:T(8,128)(2,1)S(1)}, u32[]{:S(2)}, u32[]{:S(2)}) %collective-permute-start.5) | collective-permute-done | bytes 786464 | tf_op jit(solution)/shard_map/ppermute | solution.py:44
  47.3 5.5 %collective-permute-done.7.refs_5_ = bf16[1536,256]{1,0:T(8,128)(2,1)} collective-permute-done((bf16[1536,256]{1,0:T(8,128)(2,1)S(1)}, bf16[1536,256]{1,0:T(8,128)(2,1)}, u32[]{:S(2)}, u32[]{:S(2)}) %collective-permute-start.7) | collective-permute-done | bytes 786464 | tf_op jit(solution)/shard_map/ppermute | solution.py:44
  52.8 8.6 %shard_map.92 = (f32[8,2,6,16,256]{4,3,2,1,0:T(8,128)}, f32[8,2,6,16,256]{4,3,2,1,0:T(8,128)}) custom-call(s32[13]{0:T(128)} %select_add_fusion.meta, s32[24]{0:T(128)} %reshape.100.index, s32[8]{0:T(128)} %bitcast.42, bf16[512,4096]{1,0:T(8,128)(2,1)} %w_hbm.9, bf16[1536,256]{1,0:T(8,128)(2,1)} %copy-done.2, bf16[1536,256]{1,0:T(8,128)(2,1)} %copy-done.5, ...), custom_call_target="tpu_custom_call" | custom-call | tf_op jit(solution)/shard_map/pallas_call | solution.py:133
  65.3 7.9 %all-to-all-start = ((f16[8,72,256]{2,1,0:T(8,128)(2,1)}), f16[8,72,256]{2,1,0:T(8,128)(2,1)S(1)}, u32[]{:S(2)}, u32[]{:S(2)}) async-start(f16[8,72,256]{2,1,0:T(8,128)(2,1)} %pad_maximum_fusion.3), calls=%async_computation | async-start | bytes 589824 | tf_op jit(solution)/shard_map/all_to_all | solution.py:261
  73.2 8.7 %collective-permute-done.12.refs_0_ = bf16[1536,256]{1,0:T(8,128)(2,1)} collective-permute-done((bf16[1536,256]{1,0:T(8,128)(2,1)}, bf16[1536,256]{1,0:T(8,128)(2,1)}, u32[]{:S(2)}, u32[]{:S(2)}) %collective-permute-start.12) | collective-permute-done | bytes 786464 | tf_op jit(solution)/shard_map/ppermute | solution.py:44
  82.7 5.0 %shard_map.94 = (f32[8,2,2,16,256]{4,3,2,1,0:T(8,128)}, f32[8,2,2,16,256]{4,3,2,1,0:T(8,128)}) custom-call(s32[13]{0:T(128)} %select_add_fusion.meta, s32[24]{0:T(128)} %reshape.100.index, s32[8]{0:T(128)} %bitcast.43, bf16[512,4096]{1,0:T(8,128)(2,1)} %w_hbm.9, bf16[1536,256]{1,0:T(8,128)(2,1)} %collective-permute-done.12.refs_0_, ...), custom_call_target="tpu_custom_call" | custom-call | tf_op jit(solution)/shard_map/pallas_call | solution.py:133
  88.9 2.7 %collective-permute-start.11 = (bf16[1536,256]{1,0:T(8,128)(2,1)}, bf16[1536,256]{1,0:T(8,128)(2,1)}, u32[]{:S(2)}, u32[]{:S(2)}) collective-permute-start(bf16[1536,256]{1,0:T(8,128)(2,1)} %collective-permute-done.6.refs_4_), channel_id=1, source_target_pairs={{0,96},{1,97},{2,98},{3,99},{4,100},{5,101},{6,102},{7,103},{8,104... | collective-permute-start | bytes 2359304 | tf_op jit(solution)/shard_map/ppermute | solution.py:44
  95.4 2.8 %collective-permute-start.20 = (bf16[1536,256]{1,0:T(8,128)(2,1)}, bf16[1536,256]{1,0:T(8,128)(2,1)}, u32[]{:S(2)}, u32[]{:S(2)}) collective-permute-start(bf16[1536,256]{1,0:T(8,128)(2,1)} %collective-permute-done.7.refs_5_), channel_id=1, source_target_pairs={{0,96},{1,97},{2,98},{3,99},{4,100},{5,101},{6,102},{7,103},{8,104... | collective-permute-start | bytes 2359304 | tf_op jit(solution)/shard_map/ppermute | solution.py:44
  98.2 2.3 abs_reduce_fusion
  100.5 9.0 %collective-permute-done.10.refs_0_ = bf16[1536,256]{1,0:T(8,128)(2,1)} collective-permute-done((bf16[1536,256]{1,0:T(8,128)(2,1)}, bf16[1536,256]{1,0:T(8,128)(2,1)}, u32[]{:S(2)}, u32[]{:S(2)}) %collective-permute-start.10) | collective-permute-done | bytes 786464 | tf_op jit(solution)/shard_map/ppermute | solution.py:44
  109.5 3.0 %collective-permute-start.21 = (bf16[1536,256]{1,0:T(8,128)(2,1)}, bf16[1536,256]{1,0:T(8,128)(2,1)}, u32[]{:S(2)}, u32[]{:S(2)}) collective-permute-start(bf16[1536,256]{1,0:T(8,128)(2,1)} %collective-permute-done.15.refs_1_), channel_id=1, source_target_pairs={{0,128},{1,129},{2,130},{3,131},{4,132},{5,133},{6,134},{7,135},{8... | collective-permute-start | bytes 2359304 | tf_op jit(solution)/shard_map/ppermute | solution.py:44
  113.6 4.1 %shard_map.93 = (f32[8,2,3,16,256]{4,3,2,1,0:T(8,128)}, f32[8,2,3,16,256]{4,3,2,1,0:T(8,128)}) custom-call(s32[13]{0:T(128)} %select_add_fusion.meta, s32[24]{0:T(128)} %reshape.100.index, s32[8]{0:T(128)} %bitcast.44, bf16[512,4096]{1,0:T(8,128)(2,1)} %w_hbm.9, bf16[1536,256]{1,0:T(8,128)(2,1)} %collective-permute-done.10.refs_0_, ...), custom_call_target="tpu_custom_call" | custom-call | tf_op jit(solution)/shard_map/pallas_call | solution.py:133
  117.7 2.2 collective-permute-start.14
  121.4 8.4 %all-to-all-start.1 = ((f16[8,200,256]{2,1,0:T(8,128)(2,1)}), f16[8,200,256]{2,1,0:T(8,128)(2,1)S(1)}, u32[]{:S(2)}, u32[]{:S(2)}) async-start(f16[8,200,256]{2,1,0:T(8,128)(2,1)} %pad_maximum_fusion), calls=%async_computation.1 | async-start | bytes 1638400 | tf_op jit(solution)/shard_map/all_to_all | solution.py:261
  130.1 4.5 %shard_map.96 = (f32[8,2,3,16,256]{4,3,2,1,0:T(8,128)}, f32[8,2,3,16,256]{4,3,2,1,0:T(8,128)}) custom-call(s32[13]{0:T(128)} %select_add_fusion.meta, s32[24]{0:T(128)} %reshape.100.index, s32[8]{0:T(128)} %bitcast.45, bf16[512,4096]{1,0:T(8,128)(2,1)} %w_hbm.9, bf16[1536,256]{1,0:T(8,128)(2,1)} %collective-permute-done.19.refs_0_, ...), custom_call_target="tpu_custom_call" | custom-call | tf_op jit(solution)/shard_map/pallas_call | solution.py:133
  134.6 2.3 collective-permute-start.22
  139.5 14.7 %all-to-all-done.1 = f16[8,200,256]{2,1,0:T(8,128)(2,1)S(1)} async-done(((f16[8,200,256]{2,1,0:T(8,128)(2,1)}), f16[8,200,256]{2,1,0:T(8,128)(2,1)S(1)}, u32[]{:S(2)}, u32[]{:S(2)}) %all-to-all-start.1) | async-done | bytes 819232 | tf_op jit(solution)/shard_map/all_to_all | solution.py:261
  154.1 3.5 %all-to-all-start.2 = ((f16[8,168,256]{2,1,0:T(8,128)(2,1)}), f16[8,168,256]{2,1,0:T(8,128)(2,1)S(1)}, u32[]{:S(2)}, u32[]{:S(2)}) async-start(f16[8,168,256]{2,1,0:T(8,128)(2,1)} %pad_maximum_fusion.1), calls=%async_computation.2 | async-start | bytes 1376256 | tf_op jit(solution)/shard_map/all_to_all | solution.py:261
  161.3 17.7 %all-to-all-done.2 = f16[8,168,256]{2,1,0:T(8,128)(2,1)S(1)} async-done(((f16[8,168,256]{2,1,0:T(8,128)(2,1)}), f16[8,168,256]{2,1,0:T(8,128)(2,1)S(1)}, u32[]{:S(2)}, u32[]{:S(2)}) %all-to-all-start.2) | async-done | bytes 688160 | tf_op jit(solution)/shard_map/all_to_all | solution.py:261
  179.1 3.6 %all-to-all-start.3 = ((f16[16,56,256]{2,1,0:T(8,128)(2,1)}), f16[16,56,256]{2,1,0:T(8,128)(2,1)S(1)}, u32[]{:S(2)}, u32[]{:S(2)}) async-start(f16[16,56,256]{2,1,0:T(8,128)(2,1)} %pad_maximum_fusion.2), calls=%async_computation.3 | async-start | bytes 917504 | tf_op jit(solution)/shard_map/all_to_all | solution.py:261
  186.0 11.4 %all-to-all-done.3 = f16[16,56,256]{2,1,0:T(8,128)(2,1)S(1)} async-done(((f16[16,56,256]{2,1,0:T(8,128)(2,1)}), f16[16,56,256]{2,1,0:T(8,128)(2,1)S(1)}, u32[]{:S(2)}, u32[]{:S(2)}) %all-to-all-start.3) | async-done | bytes 458784 | tf_op jit(solution)/shard_map/all_to_all | solution.py:261
  199.1 2.4 %shard_map.95 = (f32[16,4096]{1,0:T(8,128)}, f32[32,128]{1,0:T(8,128)}) custom-call(s32[13]{0:T(128)} %select_add_fusion.meta, f32[2,16,256]{2,1,0:T(8,128)} %bitcast.35, f32[2,16,256]{2,1,0:T(8,128)} %copy-done.12, f32[6,16,256]{2,1,0:T(8,128)} %bitcast.31, f32[6,16,256]{2,1,0:T(8,128)} %copy-done.10, f32[3,16,256]{2,1,0:T(8,128)} %bitcast.33, ...), custom_call_target="tpu_custom_call" | custom-call | tf_op jit(solution)/shard_map/pallas_call | solution.py:183
  201.6 2.4 %shard_map.97 = (f32[16,4096]{1,0:T(8,128)}, f32[16,32,128]{2,1,0:T(8,128)}) custom-call(s32[13]{0:T(128)} %select_add_fusion.meta, f32[16,4096]{1,0:T(8,128)} %get-tuple-element.27.refs_0_, f32[32,128]{1,0:T(8,128)} %get-tuple-element.28.refs_1_, f32[3,16,256]{2,1,0:T(8,128)} %bitcast.34), custom_call_target="tpu_custom_call" | custom-call | tf_op jit(solution)/shard_map/pallas_call | solution.py:183
  204.0 13.9 %all_to_all.30 = f32[16,32,128]{2,1,0:T(8,128)S(1)} all-to-all(f32[16,32,128]{2,1,0:T(8,128)} %get-tuple-element.32), channel_id=1, replica_groups=mesh['xh'=2,'y'=4,'z'=8,'xl'=2,'core'=2] {'z','xl'}, dimensions={0} | all-to-all | bytes 524288 | tf_op jit(solution)/shard_map/all_to_all | solution.py:283
  218.0 18.5 %all_to_all.31.sum_ref = f32[16,32,128]{2,1,0:T(8,128)} all-to-all(f32[16,32,128]{2,1,0:T(8,128)S(1)} %broadcast_in_dim.14), channel_id=1, replica_groups=mesh['xh'=2,'y'=4,'z'=8,'xl'=2,'core'=2] {'xh','y','core'}, dimensions={0} | all-to-all | bytes 524288 | tf_op jit(solution)/shard_map/all_to_all | solution.py:284
  (120 shorter events, 32.0 us)
Async XLA Ops:
  2.2 19.1 %collective-permute-start.2 = (bf16[1536,256]{1,0:T(8,128)(2,1)}, bf16[1536,256]{1,0:T(8,128)(2,1)S(1)}, u32[]{:S(2)}, u32[]{:S(2)}) collective-permute-start(bf16[1536,256]{1,0:T(8,128)(2,1)} %slice.72), channel_id=1, source_target_pairs={{0,32},{1,33},{2,34},{3,35},{4,36},{5,37},{6,38},{7,39},{8,40},{9,... | collective-permute-start | bytes 2359304 | tf_op jit(solution)/shard_map/ppermute | solution.py:44
  9.1 16.6 %copy-start.9 = (f32[8,2,2,16,256]{4,3,2,1,0:T(8,128)S(1)}, f32[8,2,2,16,256]{4,3,2,1,0:T(8,128)}, u32[]{:S(2)}) copy-start(f32[8,2,2,16,256]{4,3,2,1,0:T(8,128)} %get-tuple-element.19) | copy-start | bytes 1572868
  9.1 6.9 %collective-permute-start = (f32[8,2,2,16,256]{4,3,2,1,0:T(8,128)}, f32[8,2,2,16,256]{4,3,2,1,0:T(8,128)S(1)}, u32[]{:S(2)}, u32[]{:S(2)}) collective-permute-start(f32[8,2,2,16,256]{4,3,2,1,0:T(8,128)} %get-tuple-element.20), channel_id=1, source_target_pairs={{0,1},{1,0},{2,3},{3,2},{4,5},{5,4},{6,7},{7,6},{8,9},{9,8},{10,11... | collective-permute-start | bytes 1572872 | tf_op jit(solution)/shard_map/ppermute | solution.py:44
  11.1 27.1 %collective-permute-start.4 = (bf16[1536,256]{1,0:T(8,128)(2,1)}, bf16[1536,256]{1,0:T(8,128)(2,1)S(1)}, u32[]{:S(2)}, u32[]{:S(2)}) collective-permute-start(bf16[1536,256]{1,0:T(8,128)(2,1)} %slice.72), channel_id=1, source_target_pairs={{0,96},{1,97},{2,98},{3,99},{4,100},{5,101},{6,102},{7,103},{8,104... | collective-permute-start | bytes 2359304 | tf_op jit(solution)/shard_map/ppermute | solution.py:44
  13.2 25.0 %collective-permute-start.3 = (bf16[1536,256]{1,0:T(8,128)(2,1)S(1)}, bf16[1536,256]{1,0:T(8,128)(2,1)S(1)}, u32[]{:S(2)}, u32[]{:S(2)}) collective-permute-start(bf16[1536,256]{1,0:T(8,128)(2,1)S(1)} %slice.92), channel_id=1, source_target_pairs={{0,32},{1,33},{2,34},{3,35},{4,36},{5,37},{6,38},{7,39},{8,40},{9,... | collective-permute-start | bytes 2359304 | tf_op jit(solution)/shard_map/ppermute | solution.py:44
  13.3 34.0 %collective-permute-start.5 = (bf16[1536,256]{1,0:T(8,128)(2,1)S(1)}, bf16[1536,256]{1,0:T(8,128)(2,1)S(1)}, u32[]{:S(2)}, u32[]{:S(2)}) collective-permute-start(bf16[1536,256]{1,0:T(8,128)(2,1)S(1)} %slice.92), channel_id=1, source_target_pairs={{0,96},{1,97},{2,98},{3,99},{4,100},{5,101},{6,102},{7,103},{8,104... | collective-permute-start | bytes 2359304 | tf_op jit(solution)/shard_map/ppermute | solution.py:44
  16.0 31.3 %collective-permute-start.6 = (bf16[1536,256]{1,0:T(8,128)(2,1)}, bf16[1536,256]{1,0:T(8,128)(2,1)}, u32[]{:S(2)}, u32[]{:S(2)}) collective-permute-start(bf16[1536,256]{1,0:T(8,128)(2,1)} %slice.72), channel_id=1, source_target_pairs={{0,128},{1,129},{2,130},{3,131},{4,132},{5,133},{6,134},{7,135},{8... | collective-permute-start | bytes 2359304 | tf_op jit(solution)/shard_map/ppermute | solution.py:44
  21.3 31.6 %copy-start.2 = (bf16[1536,256]{1,0:T(8,128)(2,1)}, bf16[1536,256]{1,0:T(8,128)(2,1)S(1)}, u32[]{:S(2)}) copy-start(bf16[1536,256]{1,0:T(8,128)(2,1)S(1)} %collective-permute-done.2.refs_0_) | copy-start | bytes 2359300
  21.3 31.6 %collective-permute-start.7 = (bf16[1536,256]{1,0:T(8,128)(2,1)S(1)}, bf16[1536,256]{1,0:T(8,128)(2,1)}, u32[]{:S(2)}, u32[]{:S(2)}) collective-permute-start(bf16[1536,256]{1,0:T(8,128)(2,1)S(1)} %slice.92), channel_id=1, source_target_pairs={{0,128},{1,129},{2,130},{3,131},{4,132},{5,133},{6,134},{7,135},{8... | collective-permute-start | bytes 2359304 | tf_op jit(solution)/shard_map/ppermute | solution.py:44
  38.2 9.1 %copy-start.5 = (bf16[1536,256]{1,0:T(8,128)(2,1)}, bf16[1536,256]{1,0:T(8,128)(2,1)S(1)}, u32[]{:S(2)}) copy-start(bf16[1536,256]{1,0:T(8,128)(2,1)S(1)} %collective-permute-done.3.refs_1_) | copy-start | bytes 2359300
  38.2 14.6 %copy-start.4 = (bf16[1536,256]{1,0:T(8,128)(2,1)}, bf16[1536,256]{1,0:T(8,128)(2,1)S(1)}, u32[]{:S(2)}) copy-start(bf16[1536,256]{1,0:T(8,128)(2,1)S(1)} %collective-permute-done.4.refs_2_) | copy-start | bytes 2359300
  61.5 33.9 %collective-permute-start.8 = (f32[8,2,6,16,256]{4,3,2,1,0:T(8,128)}, f32[8,2,6,16,256]{4,3,2,1,0:T(8,128)S(1)}, u32[]{:S(2)}, u32[]{:S(2)}) collective-permute-start(f32[8,2,6,16,256]{4,3,2,1,0:T(8,128)} %get-tuple-element.22), channel_id=1, source_target_pairs={{0,1},{1,0},{2,3},{3,2},{4,5},{5,4},{6,7},{7,6},{8,9},{9,8},{10,11... | collective-permute-start | bytes 4718600 | tf_op jit(solution)/shard_map/ppermute | solution.py:44
  61.6 20.3 %collective-permute-start.12 = (bf16[1536,256]{1,0:T(8,128)(2,1)}, bf16[1536,256]{1,0:T(8,128)(2,1)}, u32[]{:S(2)}, u32[]{:S(2)}) collective-permute-start(bf16[1536,256]{1,0:T(8,128)(2,1)} %copy-done.2), channel_id=1, source_target_pairs={{0,32},{1,33},{2,34},{3,35},{4,36},{5,37},{6,38},{7,39},{8,40},{9,... | collective-permute-start | bytes 2359304 | tf_op jit(solution)/shard_map/ppermute | solution.py:44
  63.6 19.0 %collective-permute-start.15 = (bf16[1536,256]{1,0:T(8,128)(2,1)}, bf16[1536,256]{1,0:T(8,128)(2,1)}, u32[]{:S(2)}, u32[]{:S(2)}) collective-permute-start(bf16[1536,256]{1,0:T(8,128)(2,1)} %copy-done.3), channel_id=1, source_target_pairs={{0,96},{1,97},{2,98},{3,99},{4,100},{5,101},{6,102},{7,103},{8,104... | collective-permute-start | bytes 2359304 | tf_op jit(solution)/shard_map/ppermute | solution.py:44
  65.3 26.4 %all-to-all-start = ((f16[8,72,256]{2,1,0:T(8,128)(2,1)}), f16[8,72,256]{2,1,0:T(8,128)(2,1)S(1)}, u32[]{:S(2)}, u32[]{:S(2)}) async-start(f16[8,72,256]{2,1,0:T(8,128)(2,1)} %pad_maximum_fusion.3), calls=%async_computation | async-start | bytes 589824 | tf_op jit(solution)/shard_map/all_to_all | solution.py:261
  87.7 4.8 %collective-permute-start.16 = (f32[8,2,2,16,256]{4,3,2,1,0:T(8,128)}, f32[8,2,2,16,256]{4,3,2,1,0:T(8,128)S(1)}, u32[]{:S(2)}, u32[]{:S(2)}) collective-permute-start(f32[8,2,2,16,256]{4,3,2,1,0:T(8,128)} %get-tuple-element.26), channel_id=1, source_target_pairs={{0,1},{1,0},{2,3},{3,2},{4,5},{5,4},{6,7},{7,6},{8,9},{9,8},{10,11... | collective-permute-start | bytes 1572872 | tf_op jit(solution)/shard_map/ppermute | solution.py:44
  88.9 20.5 %collective-permute-start.10 = (bf16[1536,256]{1,0:T(8,128)(2,1)}, bf16[1536,256]{1,0:T(8,128)(2,1)}, u32[]{:S(2)}, u32[]{:S(2)}) collective-permute-start(bf16[1536,256]{1,0:T(8,128)(2,1)} %collective-permute-done.6.refs_4_), channel_id=1, source_target_pairs={{0,32},{1,33},{2,34},{3,35},{4,36},{5,37},{6,38},{7,39},{8,40},{9,... | collective-permute-start | bytes 2359304 | tf_op jit(solution)/shard_map/ppermute | solution.py:44
  88.9 20.5 %collective-permute-start.11 = (bf16[1536,256]{1,0:T(8,128)(2,1)}, bf16[1536,256]{1,0:T(8,128)(2,1)}, u32[]{:S(2)}, u32[]{:S(2)}) collective-permute-start(bf16[1536,256]{1,0:T(8,128)(2,1)} %collective-permute-done.6.refs_4_), channel_id=1, source_target_pairs={{0,96},{1,97},{2,98},{3,99},{4,100},{5,101},{6,102},{7,103},{8,104... | collective-permute-start | bytes 2359304 | tf_op jit(solution)/shard_map/ppermute | solution.py:44
  91.6 38.3 %collective-permute-start.19 = (bf16[1536,256]{1,0:T(8,128)(2,1)}, bf16[1536,256]{1,0:T(8,128)(2,1)}, u32[]{:S(2)}, u32[]{:S(2)}) collective-permute-start(bf16[1536,256]{1,0:T(8,128)(2,1)} %collective-permute-done.7.refs_5_), channel_id=1, source_target_pairs={{0,32},{1,33},{2,34},{3,35},{4,36},{5,37},{6,38},{7,39},{8,40},{9,... | collective-permute-start | bytes 2359304 | tf_op jit(solution)/shard_map/ppermute | solution.py:44
  92.5 20.2 %collective-permute-start.13 = (bf16[1536,256]{1,0:T(8,128)(2,1)}, bf16[1536,256]{1,0:T(8,128)(2,1)S(1)}, u32[]{:S(2)}, u32[]{:S(2)}) collective-permute-start(bf16[1536,256]{1,0:T(8,128)(2,1)} %collective-permute-done.12.refs_0_), channel_id=1, source_target_pairs={{0,128},{1,129},{2,130},{3,131},{4,132},{5,133},{6,134},{7,135},{8... | collective-permute-start | bytes 2359304 | tf_op jit(solution)/shard_map/ppermute | solution.py:44
  95.4 34.5 %collective-permute-start.20 = (bf16[1536,256]{1,0:T(8,128)(2,1)}, bf16[1536,256]{1,0:T(8,128)(2,1)}, u32[]{:S(2)}, u32[]{:S(2)}) collective-permute-start(bf16[1536,256]{1,0:T(8,128)(2,1)} %collective-permute-done.7.refs_5_), channel_id=1, source_target_pairs={{0,96},{1,97},{2,98},{3,99},{4,100},{5,101},{6,102},{7,103},{8,104... | collective-permute-start | bytes 2359304 | tf_op jit(solution)/shard_map/ppermute | solution.py:44
  109.5 89.0 %collective-permute-start.1 = (f32[2,16,256]{2,1,0:T(8,128)S(1)}, f32[2,16,256]{2,1,0:T(8,128)S(1)}, u32[]{:S(2)}, u32[]{:S(2)}) collective-permute-start(f32[2,16,256]{2,1,0:T(8,128)S(1)} %bitcast.39), channel_id=1, source_target_pairs={{0,2},{1,3},{2,0},{3,1},{4,6},{5,7},{6,4},{7,5},{8,10},{9,11},{10,... | collective-permute-start | bytes 98312 | tf_op jit(solution)/shard_map/ppermute | solution.py:44
  109.5 20.6 %collective-permute-start.21 = (bf16[1536,256]{1,0:T(8,128)(2,1)}, bf16[1536,256]{1,0:T(8,128)(2,1)}, u32[]{:S(2)}, u32[]{:S(2)}) collective-permute-start(bf16[1536,256]{1,0:T(8,128)(2,1)} %collective-permute-done.15.refs_1_), channel_id=1, source_target_pairs={{0,128},{1,129},{2,130},{3,131},{4,132},{5,133},{6,134},{7,135},{8... | collective-permute-start | bytes 2359304 | tf_op jit(solution)/shard_map/ppermute | solution.py:44
  117.7 19.2 %collective-permute-start.14 = (f32[8,2,3,16,256]{4,3,2,1,0:T(8,128)}, f32[8,2,3,16,256]{4,3,2,1,0:T(8,128)}, u32[]{:S(2)}, u32[]{:S(2)}) collective-permute-start(f32[8,2,3,16,256]{4,3,2,1,0:T(8,128)} %get-tuple-element.24), channel_id=1, source_target_pairs={{0,1},{1,0},{2,3},{3,2},{4,5},{5,4},{6,7},{7,6},{8,9},{9,8},{10,11... | collective-permute-start | bytes 2359304 | tf_op jit(solution)/shard_map/ppermute | solution.py:44
  121.4 32.8 %all-to-all-start.1 = ((f16[8,200,256]{2,1,0:T(8,128)(2,1)}), f16[8,200,256]{2,1,0:T(8,128)(2,1)S(1)}, u32[]{:S(2)}, u32[]{:S(2)}) async-start(f16[8,200,256]{2,1,0:T(8,128)(2,1)} %pad_maximum_fusion), calls=%async_computation.1 | async-start | bytes 1638400 | tf_op jit(solution)/shard_map/all_to_all | solution.py:261
  134.6 23.1 %collective-permute-start.22 = (f32[8,2,3,16,256]{4,3,2,1,0:T(8,128)}, f32[8,2,3,16,256]{4,3,2,1,0:T(8,128)S(1)}, u32[]{:S(2)}, u32[]{:S(2)}) collective-permute-start(f32[8,2,3,16,256]{4,3,2,1,0:T(8,128)} %get-tuple-element.30), channel_id=1, source_target_pairs={{0,1},{1,0},{2,3},{3,2},{4,5},{5,4},{6,7},{7,6},{8,9},{9,8},{10,11... | collective-permute-start | bytes 2359304 | tf_op jit(solution)/shard_map/ppermute | solution.py:44
  138.4 19.3 %copy-start.7 = (f32[8,2,3,16,256]{4,3,2,1,0:T(8,128)S(1)}, f32[8,2,3,16,256]{4,3,2,1,0:T(8,128)}, u32[]{:S(2)}) copy-start(f32[8,2,3,16,256]{4,3,2,1,0:T(8,128)} %get-tuple-element.29) | copy-start | bytes 2359300
  154.1 24.9 %all-to-all-start.2 = ((f16[8,168,256]{2,1,0:T(8,128)(2,1)}), f16[8,168,256]{2,1,0:T(8,128)(2,1)S(1)}, u32[]{:S(2)}, u32[]{:S(2)}) async-start(f16[8,168,256]{2,1,0:T(8,128)(2,1)} %pad_maximum_fusion.1), calls=%async_computation.2 | async-start | bytes 1376256 | tf_op jit(solution)/shard_map/all_to_all | solution.py:261
  160.4 38.0 %collective-permute-start.9 = (f32[6,16,256]{2,1,0:T(8,128)S(1)}, f32[6,16,256]{2,1,0:T(8,128)S(1)}, u32[]{:S(2)}, u32[]{:S(2)}) collective-permute-start(f32[6,16,256]{2,1,0:T(8,128)S(1)} %bitcast.37), channel_id=1, source_target_pairs={{0,2},{1,3},{2,0},{3,1},{4,6},{5,7},{6,4},{7,5},{8,10},{9,11},{10,... | collective-permute-start | bytes 294920 | tf_op jit(solution)/shard_map/ppermute | solution.py:44
  179.1 18.4 %all-to-all-start.3 = ((f16[16,56,256]{2,1,0:T(8,128)(2,1)}), f16[16,56,256]{2,1,0:T(8,128)(2,1)S(1)}, u32[]{:S(2)}, u32[]{:S(2)}) async-start(f16[16,56,256]{2,1,0:T(8,128)(2,1)} %pad_maximum_fusion.2), calls=%async_computation.3 | async-start | bytes 917504 | tf_op jit(solution)/shard_map/all_to_all | solution.py:261
  183.7 14.8 %collective-permute-start.17 = (f32[3,16,256]{2,1,0:T(8,128)S(1)}, f32[3,16,256]{2,1,0:T(8,128)S(1)}, u32[]{:S(2)}, u32[]{:S(2)}) collective-permute-start(f32[3,16,256]{2,1,0:T(8,128)S(1)} %bitcast.38), channel_id=1, source_target_pairs={{0,2},{1,3},{2,0},{3,1},{4,6},{5,7},{6,4},{7,5},{8,10},{9,11},{10,... | collective-permute-start | bytes 147464 | tf_op jit(solution)/shard_map/ppermute | solution.py:44
  185.8 12.7 %collective-permute-start.18 = (f32[2,16,256]{2,1,0:T(8,128)S(1)}, f32[2,16,256]{2,1,0:T(8,128)S(1)}, u32[]{:S(2)}, u32[]{:S(2)}) collective-permute-start(f32[2,16,256]{2,1,0:T(8,128)S(1)} %bitcast.40), channel_id=1, source_target_pairs={{0,2},{1,3},{2,0},{3,1},{4,6},{5,7},{6,4},{7,5},{8,10},{9,11},{10,... | collective-permute-start | bytes 98312 | tf_op jit(solution)/shard_map/ppermute | solution.py:44
  (15 other events, 55.0 us)
